TPU v7x, 256 devices: a whole 4x4x8 slice. The times are simulated.
256 devices in a mesh: row: 32 (over y, x, core), col: 8 (over z).
Axes of the slice: x: 4, y: 4, z: 8, core: 2. Of those that a mesh axis runs over, the one named last changes fastest.
Arguments:
- retarded: bfloat16 [256, 256, 64, 128], P('row', 'col'), may hold values from -4 to 4
- mirrored: bfloat16 [256, 256, 64, 128], P('col', 'row'), may hold values from -4 to 4
- lesser_panel: bfloat16 [256, 64, 16, 128], P(('col', 'row')), may hold values from -6 to 6
- initial: float32 [64, 16, 128], P(None, 'col'), may hold values from -6 to 6
- retention: float32 [256, 64], P('row'), may hold values from 0.4 to 1, as said below
- phase_angle: float32 [64], replicated, may hold values from -3.140625 to 3.140625
Outputs:
- propagated: float32 [256, 64, 16, 128], P('row', None, 'col')
Inputs may be any that keep to these rules, and one draw needn't show every extreme that they name: `retention`: each entry is the share of an orbital's amplitude kept over one step.
All inputs are finite; a program needn't handle non-finite values.
Results may differ from a plain program's by a relative error of at most 0.0026.
Values may be sent and summed in bfloat16 or wider, within the bound.
No kernel may reach another device: no remote copies, remote signals or barrier semaphores. Data moves between devices by JAX's collectives and lax.ppermute only.
A program may use at most 128 MiB of HBM per device.

v0:
```python
import math

import jax
import jax.numpy as jnp
from jax import lax
from jax.experimental import pallas as pl
from jax.experimental.pallas import tpu as pltpu
from jax.sharding import PartitionSpec as P


Y, X, CORES, Z = 4, 4, 2, 8
OFFSETS = (0, -1, 1, 2)
BOTH = ("row", "col")


def joint(y, x, core, z):
    return (((y % Y) * X + (x % X)) * CORES + core) * Z + z % Z


def perm_of(target):
    pairs = []
    for y in range(Y):
        for x in range(X):
            for core in range(CORES):
                for z in range(Z):
                    pairs.append((joint(y, x, core, z), joint(*target(y, x, core, z))))
    return pairs


def plane_perm(by, first):
    return perm_of(
        lambda y, x, core, z: (y, x + by, core, z)
        if (core == 0) == first
        else (y + by, x, core, z)
    )


def depth_perm(by):
    return perm_of(lambda y, x, core, z: (y, x, core, z + (by if core == 0 else -by)))


CORE_SWAP = perm_of(lambda y, x, core, z: (y, x, 1 - core, z))


def send(array, perm):
    return lax.ppermute(array, BOTH, perm)


def energy_kernel(slots, times, ret_ref, mir_ref, out_ref):
    orbitals = ret_ref.shape[2]
    slot_count = ret_ref.shape[1]
    now = times[0] + pl.program_id(0)
    first_source = times[1]
    low = lax.broadcasted_iota(jnp.int32, (orbitals, 2 * orbitals), 1) < orbitals
    low_row = lax.broadcasted_iota(jnp.int32, (1, 2 * orbitals), 1) < orbitals

    def pair(n, carry):
        s0 = slots[2 * n]
        s1 = slots[2 * n + 1]
        a0 = ret_ref[0, s0].astype(jnp.float32)
        a1 = ret_ref[0, s1].astype(jnp.float32)
        b = jnp.concatenate([mir_ref[s0, 0], mir_ref[s1, 0]], axis=0).astype(jnp.float32)
        keep0 = jnp.where(first_source + s0 <= now, 1.0, 0.0)
        keep1 = jnp.where(first_source + s1 <= now, 1.0, 0.0)
        keep = jnp.where(low_row, keep0, keep1)
        bt = b.T
        b_re = bt[:orbitals] * keep
        b_im = bt[orbitals:] * keep
        re = jnp.where(low, a0, pltpu.roll(a1, orbitals, 1))
        im = jnp.where(low, pltpu.roll(a0, orbitals, 1), a1)
        sq_re = re * re - im * im
        sq_im = 2.0 * re * im
        cols = pl.ds(pl.multiple_of(n * 2 * orbitals, 2 * orbitals), 2 * orbitals)
        out_ref[pl.program_id(0), 0, :, cols] = (sq_re * b_re - sq_im * b_im).astype(jnp.bfloat16)
        out_ref[pl.program_id(0), 1, :, cols] = (sq_re * b_im + sq_im * b_re).astype(jnp.bfloat16)
        return carry

    lax.fori_loop(0, slot_count // 2, pair, 0, unroll=4)


def energy_call(retarded, mirrored, slots, times):
    steps, sources, orbitals, width = retarded.shape
    return pl.pallas_call(
        energy_kernel,
        out_shape=jax.ShapeDtypeStruct((steps, 2, orbitals, sources * orbitals), jnp.bfloat16),
        grid_spec=pltpu.PrefetchScalarGridSpec(
            num_scalar_prefetch=2,
            grid=(steps,),
            in_specs=[
                pl.BlockSpec((1, sources, orbitals, width), lambda t, *_: (t, 0, 0, 0)),
                pl.BlockSpec((sources, 1, orbitals, width), lambda t, *_: (0, t, 0, 0)),
            ],
            out_specs=pl.BlockSpec(memory_space=pltpu.VMEM),
        ),
        compiler_params=pltpu.CompilerParams(vmem_limit_bytes=14 << 20),
        cost_estimate=pl.CostEstimate(
            flops=20 * steps * sources * orbitals * width,
            bytes_accessed=6 * steps * sources * orbitals * width,
            transcendentals=0,
        ),
    )(
        slots,
        times,
        pltpu.with_memory_space_constraint(retarded, pltpu.HBM),
        pltpu.with_memory_space_constraint(mirrored, pltpu.HBM),
    )


def product_tile(energy_ref, panel_refs, norm):
    steps, _, orbitals, depth = energy_ref.shape
    width = 2 * orbitals
    left = energy_ref[...].reshape(steps * 2 * orbitals, depth)
    count = len(panel_refs) // 2
    right = jnp.concatenate(
        [
            jnp.concatenate([ref[...] for ref in panel_refs[:count]], axis=0),
            jnp.concatenate([ref[...] for ref in panel_refs[count:]], axis=0),
        ],
        axis=1,
    )
    both = jnp.dot(left, right, preferred_element_type=jnp.float32)
    both = both.reshape(steps, 2, orbitals, 2 * width)
    lane = lax.broadcasted_iota(jnp.int32, (steps, orbitals, width), 2)
    sign = jnp.where(lane < orbitals, -norm, norm)
    values = []
    for half in range(2):
        part_re = both[:, 0, :, half * width : (half + 1) * width]
        part_im = both[:, 1, :, half * width : (half + 1) * width]
        values.append(part_re * norm + sign * pltpu.roll(part_im, orbitals, 2))
    return values


def product_call(norm, cols, energy, panels, outputs):
    steps, _, orbitals, depth = energy.shape
    width = 2 * orbitals
    sizes, kinds = {}, {}
    for turn in outputs:
        for result, place, kind in turn:
            sizes[result] = max(sizes.get(result, 0), place + 1)
            kinds[result] = kind
    shape = [
        jax.ShapeDtypeStruct((sizes[n], steps, orbitals, width), kinds[n]) for n in range(len(sizes))
    ]
    count = len(panels)

    def body(cols_ref, energy_ref, *refs):
        panel_refs, out_refs = refs[: 2 * count], refs[2 * count :]
        values = product_tile(energy_ref, panel_refs, norm)
        for turn, targets in enumerate(outputs):

            @pl.when(pl.program_id(0) == turn)
            def _():
                for value, (result, place, kind) in zip(values, targets):
                    out_refs[result][place] = value.astype(kind)

    def panel_spec(panel, which):
        return pl.BlockSpec((panel.shape[0], width), lambda n, cols: (0, cols[2 * n + which]))

    return pl.pallas_call(
        body,
        out_shape=shape,
        grid_spec=pltpu.PrefetchScalarGridSpec(
            num_scalar_prefetch=1,
            grid=(len(outputs),),
            in_specs=[pl.BlockSpec(memory_space=pltpu.VMEM)]
            + [panel_spec(panel, which) for which in range(2) for panel in panels],
            out_specs=[pl.BlockSpec(s.shape, lambda n, cols: (0, 0, 0, 0)) for s in shape],
        ),
        compiler_params=pltpu.CompilerParams(vmem_limit_bytes=20 << 20),
        cost_estimate=pl.CostEstimate(
            flops=2 * len(outputs) * steps * 2 * orbitals * depth * 2 * width,
            bytes_accessed=2 * depth * (steps * 2 * orbitals + len(outputs) * 2 * width),
            transcendentals=0,
        ),
    )(cols, energy, *panels, *panels)


def turned(factor_re, factor_im, value):
    return factor_re * value + factor_im * pltpu.roll(value, value.shape[-1] // 2, value.ndim - 1)


def end_kernel(fre_ref, fim_ref, *refs):
    part_refs, (sum_ref, end_ref) = refs[:-2], refs[-2:]
    steps, orbitals, width = sum_ref.shape
    state = jnp.zeros((orbitals, width), jnp.float32)
    for t in range(steps):
        value = part_refs[0][t]
        for ref in part_refs[1:]:
            value = value + ref[t].astype(jnp.float32)
        sum_ref[t] = value
        state = turned(fre_ref[t], fim_ref[t], state + value)
    end_ref[...] = state


def message_kernel(fre_ref, fim_ref, end0_ref, end1_ref, msg_ref):
    steps, orbitals, width = fre_ref.shape
    lane = lax.broadcasted_iota(jnp.int32, (orbitals, width), 1)
    block = jnp.where(lane < width // 2, 1.0, 0.0).astype(jnp.float32)
    for t in range(steps):
        block = turned(fre_ref[t], fim_ref[t], block)
    msg_ref[0] = end0_ref[...]
    msg_ref[1] = end1_ref[...]
    msg_ref[2] = block


def apply(later, earlier):
    width = later.shape[-1]
    lane = lax.broadcasted_iota(jnp.int32, later.shape[1:], 1)
    low = lane < width // 2
    factor = later[2]
    swapped = pltpu.roll(factor, width // 2, 1)
    fre = jnp.where(low, factor, swapped)
    fim = jnp.where(low, -swapped, factor)
    planes = [
        turned(fre, fim, earlier[0]) + later[0],
        turned(fre, fim, earlier[1]) + later[1],
        turned(fre, fim, earlier[2]),
    ]
    return planes


def chosen(keep, planes, other):
    return [jnp.where(keep, a, b) for a, b in zip(planes, other)]


def unit(shape):
    lane = lax.broadcasted_iota(jnp.int32, shape, 1)
    return [
        jnp.zeros(shape, jnp.float32),
        jnp.zeros(shape, jnp.float32),
        jnp.where(lane < shape[-1] // 2, 1.0, 0.0).astype(jnp.float32),
    ]


def read(ref):
    return [ref[0], ref[1], ref[2]]


class Planes:
    def __init__(self, planes):
        self.planes = planes
        self.shape = (3,) + planes[0].shape

    def __getitem__(self, index):
        return self.planes[index]


def after(later, earlier):
    return apply(Planes(later), Planes(earlier))


def chip_kernel(where_ref, own_ref, other_ref, out_ref):
    odd = where_ref[0] == 1
    own, other = read(own_ref), read(other_ref)
    later = chosen(odd, own, other)
    earlier = chosen(odd, other, own)
    for n, plane in enumerate(after(later, earlier)):
        out_ref[n] = plane


def line_kernel(place, where_ref, own_ref, d1_ref, d2_ref, d3_ref, before_ref, total_ref):
    at = where_ref[place]
    one = unit(own_ref.shape[1:])
    behind = [read(d1_ref), read(d2_ref), read(d3_ref)]
    before = one
    for back in (3, 2, 1):
        here = chosen(at >= back, behind[back - 1], one)
        before = after(here, before)
    for n, plane in enumerate(before):
        before_ref[n] = plane
    if total_ref is not None:
        total = after(read(own_ref), before)
        for back in (3, 2, 1):
            here = chosen(at < back, behind[back - 1], one)
            total = after(here, total)
        for n, plane in enumerate(total):
            total_ref[n] = plane


def column_kernel(where_ref, own_ref, d1_ref, d2_ref, d3_ref, before_ref):
    line_kernel(2, where_ref, own_ref, d1_ref, d2_ref, d3_ref, before_ref, None)


def last_kernel(where_ref, fre_ref, fim_ref, sum0_ref, sum1_ref, init_ref, y_ref, x_ref, core_ref, out_ref):
    steps = fre_ref.shape[0]
    one = unit(init_ref.shape[1:])
    from_core = chosen(where_ref[0] == 1, read(core_ref), one)
    entering = after(from_core, after(read(x_ref), read(y_ref)))
    start = after(entering, [init_ref[0], init_ref[1], one[2]])
    for half, sum_ref in enumerate((sum0_ref, sum1_ref)):
        state = start[half]
        for t in range(steps):
            state = turned(fre_ref[t], fim_ref[t], state + sum_ref[t])
            out_ref[t, half] = state


def small_call(kernel, out_shape, scalars, *arrays):
    specs = [pl.BlockSpec(memory_space=pltpu.SMEM)] if scalars is not None else []
    specs += [pl.BlockSpec(memory_space=pltpu.VMEM)] * len(arrays)
    out_specs = jax.tree.map(lambda _: pl.BlockSpec(memory_space=pltpu.VMEM), out_shape)
    args = ([scalars] if scalars is not None else []) + list(arrays)
    return pl.pallas_call(
        kernel,
        out_shape=out_shape,
        in_specs=specs,
        out_specs=out_specs,
        compiler_params=pltpu.CompilerParams(vmem_limit_bytes=8 << 20),
        cost_estimate=pl.CostEstimate(flops=1000000, bytes_accessed=1 << 20, transcendentals=0),
    )(*args)


def near_line(local):
    moved = [local] + [send(local, plane_perm(-off, True)) for off in OFFSETS[1:]]
    return [jnp.concatenate([m[chunk] for m in moved], axis=0) for chunk in range(2)]


def far_blocks(line):
    blocks = [line]
    for off in OFFSETS[1:]:
        blocks.append(send(line, plane_perm(-off, False)))
    return blocks


def add_rounded(*parts):
    total = parts[0]
    for part in parts[1:]:
        total = total + part.astype(jnp.float32)
    return total.astype(jnp.bfloat16)


def column_sum(norm, cols_of, energy, panels):
    bf16, f32 = jnp.bfloat16, jnp.float32
    s46, s2, s7 = product_call(
        norm,
        cols_of((4, 6, 2, 7)),
        energy,
        panels,
        (((0, 0, bf16), (0, 1, bf16)), ((1, 0, bf16), (2, 0, bf16))),
    )
    r46 = send(s46, depth_perm(1))
    r2 = send(s2, depth_perm(-1))
    p3, p5, s1, p0 = product_call(
        norm,
        cols_of((3, 5, 1, 0)),
        energy,
        panels,
        (((0, 0, f32), (1, 0, f32)), ((2, 0, bf16), (3, 0, f32))),
    )
    r5 = send(add_rounded(p5[0], r46[1]), depth_perm(-3))
    r3 = send(add_rounded(p3[0], r46[0], r2[0]), depth_perm(3))
    r1 = send(s1[0], depth_perm(1))
    r7 = send(s7[0], depth_perm(-1))
    return [p0[0], r1, r7, r5, r3]


def slot_table(row_index):
    core = row_index % CORES
    x = (row_index // CORES) % X
    y = row_index // (CORES * X)
    offs = jnp.array(OFFSETS, jnp.int32)
    outer = jnp.repeat(offs, len(OFFSETS))
    inner = jnp.tile(offs, len(OFFSETS))

    def of(which):
        dy = jnp.where(which == 0, outer, inner)
        dx = jnp.where(which == 0, inner, outer)
        return (((y + dy) % Y) * X + (x + dx) % X) * CORES + which

    return jnp.concatenate([of(core), of(1 - core)]).astype(jnp.int32)


def per_device(retarded, mirrored, lesser_panel, initial, retention, phase_angle):
    row_index = lax.axis_index("row")
    col_index = lax.axis_index("col")
    steps, sources, orbitals, width = retarded.shape
    window = steps * lax.axis_size("row")
    panels = lesser_panel.shape[2]
    norm = 1.0 / (orbitals * math.sqrt(window))
    core = row_index % CORES
    x = (row_index // CORES) % X
    y = row_index // (CORES * X)
    where = jnp.stack([core, x, y]).astype(jnp.int32)
    way = jnp.where(core == 0, 1, -1)

    local = jnp.moveaxis(lesser_panel.reshape(orbitals, panels // 2, 2, width), 2, 0)
    local = local.reshape(2, orbitals, panels // 2 * width)
    times = jnp.stack([row_index * steps, col_index * sources]).astype(jnp.int32)
    energy = energy_call(retarded, mirrored, slot_table(row_index), times)

    def cols_of(rels):
        return ((col_index + way * jnp.array(rels, jnp.int32)) % Z).astype(jnp.int32)

    line0, line1 = near_line(local)
    blocks0 = far_blocks(line0)
    blocks1 = far_blocks(line1)
    panels0 = blocks0 + [send(block, CORE_SWAP) for block in blocks0]
    parts0 = column_sum(norm, cols_of, energy, panels0)
    panels1 = blocks1 + [send(block, CORE_SWAP) for block in blocks1]
    parts1 = column_sum(norm, cols_of, energy, panels1)

    rotate_re = retention * jnp.cos(phase_angle)[None, :]
    rotate_im = retention * jnp.sin(phase_angle)[None, :]
    lane = jnp.arange(width, dtype=jnp.int32)
    sign = jnp.where(lane < orbitals, -1.0, 1.0).astype(jnp.float32)
    fre = jnp.broadcast_to(rotate_re[:, :, None], (steps, orbitals, width))
    fim = rotate_im[:, :, None] * sign
    start = jnp.swapaxes(initial, 0, 1)

    message = jax.ShapeDtypeStruct((3, orbitals, width), jnp.float32)
    total = jax.ShapeDtypeStruct((steps, orbitals, width), jnp.float32)
    end = jax.ShapeDtypeStruct((orbitals, width), jnp.float32)
    sum0, end0 = small_call(end_kernel, (total, end), None, fre, fim, *parts0)
    sum1, end1 = small_call(end_kernel, (total, end), None, fre, fim, *parts1)
    ends = small_call(message_kernel, message, None, fre, fim, end0, end1)
    other = send(ends, CORE_SWAP)
    chip = small_call(chip_kernel, message, where, ends, other)
    row_perm = lambda by: perm_of(lambda y, x, core, z: (y, x + by, core, z))
    column_perm = lambda by: perm_of(lambda y, x, core, z: (y + by, x, core, z))
    behind = [send(chip, row_perm(back)) for back in (1, 2, 3)]

    def across(*refs):
        line_kernel(1, *refs)

    before_x, line = small_call(across, (message, message), where, chip, *behind)
    behind = [send(line, column_perm(back)) for back in (1, 2, 3)]
    before_y = small_call(column_kernel, message, where, line, *behind)
    out = small_call(
        last_kernel,
        jax.ShapeDtypeStruct((steps, 2, orbitals, width), jnp.float32),
        where,
        fre,
        fim,
        sum0,
        sum1,
        start,
        before_y,
        before_x,
        other,
    )
    return jnp.swapaxes(out, 1, 2)


def solution(mesh):
    return jax.shard_map(
        per_device,
        mesh=mesh,
        in_specs=(
            P("row", "col", None, None),
            P("col", "row", None, None),
            P(("col", "row"), None, None, None),
            P(None, "col", None),
            P("row", None),
            P(),
        ),
        out_specs=P("row", None, "col", None),
        check_vma=False,
    )
```

profile of v0, /device:TPU:78, one launch (start us, length us, event | category | flops | bytes accessed | tf_op | source)
XLA Modules:
  0.0 135.9 jit_solution(11311452131565013714)
XLA Ops:
  0.0 1.0 copy.21
  1.1 0.1 reshape.54
  1.2 0.6 collective-permute-start
  1.7 1.5 %collective-permute-start.1 = (bf16[2,64,1024]{2,1,0:T(8,128)(2,1)S(1)}, bf16[2,64,1024]{2,1,0:T(8,128)(2,1)S(1)}, u32[]{:S(2)}, u32[]{:S(2)}) collective-permute-start(bf16[2,64,1024]{2,1,0:T(8,128)(2,1)S(1)} %reshape.54), channel_id=1, source_target_pairs={{0,48},{1,49},{2,50},{3,51},{4,52},{5,53},{6,54},{7,55},{8,200},{9... | collective-permute-start | bytes 786440 | tf_op jit(solution)/shard_map/ppermute | solution.py:46
  3.3 1.4 %collective-permute-start.2 = (bf16[2,64,1024]{2,1,0:T(8,128)(2,1)S(1)}, bf16[2,64,1024]{2,1,0:T(8,128)(2,1)S(1)}, u32[]{:S(2)}, u32[]{:S(2)}) collective-permute-start(bf16[2,64,1024]{2,1,0:T(8,128)(2,1)S(1)} %reshape.54), channel_id=1, source_target_pairs={{0,32},{1,33},{2,34},{3,35},{4,36},{5,37},{6,38},{7,39},{8,136},{9... | collective-permute-start | bytes 786440 | tf_op jit(solution)/shard_map/ppermute | solution.py:46
  4.8 0.8 select_add_fusion.3
  5.6 2.0 %collective-permute-done = bf16[2,64,1024]{2,1,0:T(8,128)(2,1)S(1)} collective-permute-done((bf16[2,64,1024]{2,1,0:T(8,128)(2,1)S(1)}, bf16[2,64,1024]{2,1,0:T(8,128)(2,1)S(1)}, u32[]{:S(2)}, u32[]{:S(2)}) %collective-permute-start) | collective-permute-done | bytes 262176 | tf_op jit(solution)/shard_map/ppermute | solution.py:46
  7.6 4.5 %collective-permute-done.1 = bf16[2,64,1024]{2,1,0:T(8,128)(2,1)S(1)} collective-permute-done((bf16[2,64,1024]{2,1,0:T(8,128)(2,1)S(1)}, bf16[2,64,1024]{2,1,0:T(8,128)(2,1)S(1)}, u32[]{:S(2)}, u32[]{:S(2)}) %collective-permute-start.1) | collective-permute-done | bytes 262176 | tf_op jit(solution)/shard_map/ppermute | solution.py:46
  12.2 1.7 %collective-permute-start.16 = (bf16[256,1024]{1,0:T(8,128)(2,1)S(1)}, bf16[256,1024]{1,0:T(8,128)(2,1)S(1)}, u32[]{:S(2)}, u32[]{:S(2)}) collective-permute-start(bf16[256,1024]{1,0:T(8,128)(2,1)S(1)} %pad_maximum_fusion.1.refs_0_.refs_8_), channel_id=1, source_target_pairs={{0,64},{1,65},{2,66},{3,67},{4,68},{5,69},{6,70},{7,71},{8,24},{9,... | collective-permute-start | bytes 1572872 | tf_op jit(solution)/shard_map/ppermute | solution.py:46
  13.9 0.5 collective-permute-start.17
  14.3 2.3 %collective-permute-start.18 = (bf16[256,1024]{1,0:T(8,128)(2,1)S(1)}, bf16[256,1024]{1,0:T(8,128)(2,1)S(1)}, u32[]{:S(2)}, u32[]{:S(2)}) collective-permute-start(bf16[256,1024]{1,0:T(8,128)(2,1)S(1)} %pad_maximum_fusion.1.refs_0_.refs_8_), channel_id=1, source_target_pairs={{0,128},{1,129},{2,130},{3,131},{4,132},{5,133},{6,134},{7,135},{8... | collective-permute-start | bytes 1572872 | tf_op jit(solution)/shard_map/ppermute | solution.py:46
  16.7 0.9 collective-permute-start.3
  18.0 3.5 %collective-permute-done.16.refs_1_.refs_9_ = bf16[256,1024]{1,0:T(8,128)(2,1)S(1)} collective-permute-done((bf16[256,1024]{1,0:T(8,128)(2,1)S(1)}, bf16[256,1024]{1,0:T(8,128)(2,1)S(1)}, u32[]{:S(2)}, u32[]{:S(2)}) %collective-permute-start.16) | collective-permute-done | bytes 524320 | tf_op jit(solution)/shard_map/ppermute | solution.py:46
  21.5 1.7 %collective-permute-start.4 = (bf16[256,1024]{1,0:T(8,128)(2,1)S(1)}, bf16[256,1024]{1,0:T(8,128)(2,1)S(1)}, u32[]{:S(2)}, u32[]{:S(2)}) collective-permute-start(bf16[256,1024]{1,0:T(8,128)(2,1)S(1)} %pad_maximum_fusion.refs_0_.refs_8_), channel_id=1, source_target_pairs={{0,192},{1,193},{2,194},{3,195},{4,196},{5,197},{6,198},{7,199},{8... | collective-permute-start | bytes 1572872 | tf_op jit(solution)/shard_map/ppermute | solution.py:46
  23.1 7.7 %collective-permute-start.5 = (bf16[256,1024]{1,0:T(8,128)(2,1)S(1)}, bf16[256,1024]{1,0:T(8,128)(2,1)S(1)}, u32[]{:S(2)}, u32[]{:S(2)}) collective-permute-start(bf16[256,1024]{1,0:T(8,128)(2,1)S(1)} %pad_maximum_fusion.refs_0_.refs_8_), channel_id=1, source_target_pairs={{0,128},{1,129},{2,130},{3,131},{4,132},{5,133},{6,134},{7,135},{8... | collective-permute-start | bytes 1572872 | tf_op jit(solution)/shard_map/ppermute | solution.py:46
  30.8 0.5 collective-permute-start.21
  31.4 1.4 %collective-permute-done.3.refs_1_.refs_9_ = bf16[256,1024]{1,0:T(8,128)(2,1)S(1)} collective-permute-done((bf16[256,1024]{1,0:T(8,128)(2,1)S(1)}, bf16[256,1024]{1,0:T(8,128)(2,1)S(1)}, u32[]{:S(2)}, u32[]{:S(2)}) %collective-permute-start.3) | collective-permute-done | bytes 524320 | tf_op jit(solution)/shard_map/ppermute | solution.py:46
  32.9 3.0 %collective-permute-done.4.refs_2_.refs_10_ = bf16[256,1024]{1,0:T(8,128)(2,1)S(1)} collective-permute-done((bf16[256,1024]{1,0:T(8,128)(2,1)S(1)}, bf16[256,1024]{1,0:T(8,128)(2,1)S(1)}, u32[]{:S(2)}, u32[]{:S(2)}) %collective-permute-start.4) | collective-permute-done | bytes 524320 | tf_op jit(solution)/shard_map/ppermute | solution.py:46
  35.8 2.2 %collective-permute-start.6 = (bf16[256,1024]{1,0:T(8,128)(2,1)S(1)}, bf16[256,1024]{1,0:T(8,128)(2,1)S(1)}, u32[]{:S(2)}, u32[]{:S(2)}) collective-permute-start(bf16[256,1024]{1,0:T(8,128)(2,1)S(1)} %pad_maximum_fusion.refs_0_.refs_8_), channel_id=1, source_target_pairs={{0,8},{1,9},{2,10},{3,11},{4,12},{5,13},{6,14},{7,15},{8,0},{9,1},... | collective-permute-start | bytes 1572872 | tf_op jit(solution)/shard_map/ppermute | solution.py:46
  38.0 4.9 %collective-permute-done.5.refs_3_.refs_11_ = bf16[256,1024]{1,0:T(8,128)(2,1)S(1)} collective-permute-done((bf16[256,1024]{1,0:T(8,128)(2,1)S(1)}, bf16[256,1024]{1,0:T(8,128)(2,1)S(1)}, u32[]{:S(2)}, u32[]{:S(2)}) %collective-permute-start.5) | collective-permute-done | bytes 524320 | tf_op jit(solution)/shard_map/ppermute | solution.py:46
  42.9 0.5 collective-permute-start.8
  43.4 0.3 collective-permute-start.9
  43.8 9.3 %shard_map.109.energy_ref = bf16[8,2,64,2048]{3,2,1,0:T(8,128)(2,1)S(1)} custom-call(s32[32]{0:T(128)S(1)} %pad_add_fusion.1.slots, s32[2]{0:T(128)S(1)} %pad_add_fusion.2.times, bf16[8,32,64,128]{3,2,1,0:T(8,128)(2,1)} %ret_ref.1, bf16[32,8,64,128]{3,2,1,0:T(8,128)(2,1)} %mir_ref.1), custom_call_target="tpu_custom_call" | custom-call | flops 41943040 | bytes 12582912 | tf_op jit(solution)/shard_map/pallas_call | solution.py:83
  53.1 4.7 %shard_map.114 = (bf16[2,8,64,128]{3,2,1,0:T(8,128)(2,1)S(1)}, bf16[1,8,64,128]{3,2,1,0:T(8,128)(2,1)S(1)}, bf16[1,8,64,128]{3,2,1,0:T(8,128)(2,1)S(1)}) custom-call(s32[4]{0:T(128)S(1)} %get-tuple-element.65.cols_ref, bf16[8,2,64,2048]{3,2,1,0:T(8,128)(2,1)S(1)} %shard_map.109.energy_ref, bf16[256,1024]{1,0:T(8,128)(2,1)S(1)} %pad_maximum_fusion.1.refs_0_.refs_8_, ...), custom_call_target="tpu_custom_call" | custom-call | flops 2147483648 | bytes 6291456 | tf_op jit(solution)/shard_map/pallas_call | solution.py:159
  57.8 2.0 %collective-permute-start.25 = (bf16[2,8,64,128]{3,2,1,0:T(8,128)(2,1)S(1)}, bf16[2,8,64,128]{3,2,1,0:T(8,128)(2,1)S(1)}, u32[]{:S(2)}, u32[]{:S(2)}) collective-permute-start(bf16[2,8,64,128]{3,2,1,0:T(8,128)(2,1)S(1)} %get-tuple-element.37), channel_id=1, source_target_pairs={{0,1},{1,2},{2,3},{3,4},{4,5},{5,6},{6,7},{7,0},{8,15},{9,8},{10,9... | collective-permute-start | bytes 786440 | tf_op jit(solution)/shard_map/ppermute | solution.py:46
  59.8 4.7 %shard_map.113 = (f32[1,8,64,128]{3,2,1,0:T(8,128)S(1)}, f32[1,8,64,128]{3,2,1,0:T(8,128)S(1)}, bf16[1,8,64,128]{3,2,1,0:T(8,128)(2,1)S(1)}, f32[1,8,64,128]{3,2,1,0:T(8,128)S(1)}) custom-call(s32[4]{0:T(128)S(1)} %get-tuple-element.66.cols_ref, bf16[8,2,64,2048]{3,2,1,0:T(8,128)(2,1)S(1)} %shard_map.109.energy_ref, ...), custom_call_target="tpu_custom_call" | custom-call | flops 2147483648 | bytes 6291456 | tf_op jit(solution)/shard_map/pallas_call | solution.py:159
  64.5 0.2 collective-permute-start.27
  64.7 0.1 collective-permute-start.24
  64.8 3.1 %collective-permute-start.23 = (bf16[8,64,128]{2,1,0:T(8,128)(2,1)S(1)}, bf16[8,64,128]{2,1,0:T(8,128)(2,1)S(1)}, u32[]{:S(2)}, u32[]{:S(2)}) collective-permute-start(bf16[8,64,128]{2,1,0:T(8,128)(2,1)S(1)} %bitcast.55), channel_id=1, source_target_pairs={{0,1},{1,2},{2,3},{3,4},{4,5},{5,6},{6,7},{7,0},{8,15},{9,8},{10,9... | collective-permute-start | bytes 393224 | tf_op jit(solution)/shard_map/ppermute | solution.py:46
  67.9 4.4 %shard_map.111 = (bf16[2,8,64,128]{3,2,1,0:T(8,128)(2,1)S(1)}, bf16[1,8,64,128]{3,2,1,0:T(8,128)(2,1)S(1)}, bf16[1,8,64,128]{3,2,1,0:T(8,128)(2,1)S(1)}) custom-call(s32[4]{0:T(128)S(1)} %get-tuple-element.65.cols_ref, bf16[8,2,64,2048]{3,2,1,0:T(8,128)(2,1)S(1)} %shard_map.109.energy_ref, bf16[256,1024]{1,0:T(8,128)(2,1)S(1)} %pad_maximum_fusion.refs_0_.refs_8_, ...), custom_call_target="tpu_custom_call" | custom-call | flops 2147483648 | bytes 6291456 | tf_op jit(solution)/shard_map/pallas_call | solution.py:159
  72.3 3.2 %collective-permute-start.12 = (bf16[2,8,64,128]{3,2,1,0:T(8,128)(2,1)S(1)}, bf16[2,8,64,128]{3,2,1,0:T(8,128)(2,1)S(1)}, u32[]{:S(2)}, u32[]{:S(2)}) collective-permute-start(bf16[2,8,64,128]{3,2,1,0:T(8,128)(2,1)S(1)} %get-tuple-element.29), channel_id=1, source_target_pairs={{0,1},{1,2},{2,3},{3,4},{4,5},{5,6},{6,7},{7,0},{8,15},{9,8},{10,9... | collective-permute-start | bytes 786440 | tf_op jit(solution)/shard_map/ppermute | solution.py:46
  75.5 4.4 %shard_map.110 = (f32[1,8,64,128]{3,2,1,0:T(8,128)S(1)}, f32[1,8,64,128]{3,2,1,0:T(8,128)S(1)}, bf16[1,8,64,128]{3,2,1,0:T(8,128)(2,1)S(1)}, f32[1,8,64,128]{3,2,1,0:T(8,128)S(1)}) custom-call(s32[4]{0:T(128)S(1)} %get-tuple-element.66.cols_ref, bf16[8,2,64,2048]{3,2,1,0:T(8,128)(2,1)S(1)} %shard_map.109.energy_ref, ...), custom_call_target="tpu_custom_call" | custom-call | flops 2147483648 | bytes 6291456 | tf_op jit(solution)/shard_map/pallas_call | solution.py:159
  79.9 0.1 collective-permute-start.14
  80.1 0.1 fusion.3
  80.2 4.9 %collective-permute-done.14 = bf16[1,8,64,128]{3,2,1,0:T(8,128)(2,1)S(1)} collective-permute-done((bf16[1,8,64,128]{3,2,1,0:T(8,128)(2,1)S(1)}, bf16[1,8,64,128]{3,2,1,0:T(8,128)(2,1)S(1)}, u32[]{:S(2)}, u32[]{:S(2)}) %collective-permute-start.14) | collective-permute-done | bytes 131104 | tf_op jit(solution)/shard_map/ppermute | solution.py:46
  85.1 4.0 %collective-permute-start.10 = (bf16[8,64,128]{2,1,0:T(8,128)(2,1)S(1)}, bf16[8,64,128]{2,1,0:T(8,128)(2,1)S(1)}, u32[]{:S(2)}, u32[]{:S(2)}) collective-permute-start(bf16[8,64,128]{2,1,0:T(8,128)(2,1)S(1)} %bitcast.58), channel_id=1, source_target_pairs={{0,1},{1,2},{2,3},{3,4},{4,5},{5,6},{6,7},{7,0},{8,15},{9,8},{10,9... | collective-permute-start | bytes 393224 | tf_op jit(solution)/shard_map/ppermute | solution.py:46
  89.1 0.1 fusion.1
  89.2 5.1 %collective-permute-start.28 = (bf16[8,64,128]{2,1,0:T(8,128)(2,1)S(1)}, bf16[8,64,128]{2,1,0:T(8,128)(2,1)S(1)}, u32[]{:S(2)}, u32[]{:S(2)}) collective-permute-start(bf16[8,64,128]{2,1,0:T(8,128)(2,1)S(1)} %get-tuple-element.45), channel_id=1, source_target_pairs={{0,3},{1,4},{2,5},{3,6},{4,7},{5,0},{6,1},{7,2},{8,13},{9,14},{10,... | collective-permute-start | bytes 393224 | tf_op jit(solution)/shard_map/ppermute | solution.py:46
  94.3 8.8 %collective-permute-done.26.refs_3_ = bf16[8,64,128]{2,1,0:T(8,128)(2,1)S(1)} collective-permute-done((bf16[8,64,128]{2,1,0:T(8,128)(2,1)S(1)}, bf16[8,64,128]{2,1,0:T(8,128)(2,1)S(1)}, u32[]{:S(2)}, u32[]{:S(2)}) %collective-permute-start.26) | collective-permute-done | bytes 131104 | tf_op jit(solution)/shard_map/ppermute | solution.py:46
  103.1 0.6 collective-permute-start.15
  103.7 0.1 broadcast_multiply_fusion.fim_ref
  103.9 0.1 broadcast_in_dim.12.fre_ref
  104.0 0.6 shard_map.115
  104.6 3.2 %collective-permute-done.13.refs_3_ = bf16[8,64,128]{2,1,0:T(8,128)(2,1)S(1)} collective-permute-done((bf16[8,64,128]{2,1,0:T(8,128)(2,1)S(1)}, bf16[8,64,128]{2,1,0:T(8,128)(2,1)S(1)}, u32[]{:S(2)}, u32[]{:S(2)}) %collective-permute-start.13) | collective-permute-done | bytes 131104 | tf_op jit(solution)/shard_map/ppermute | solution.py:46
  107.8 3.3 %collective-permute-done.15.refs_4_ = bf16[8,64,128]{2,1,0:T(8,128)(2,1)S(1)} collective-permute-done((bf16[8,64,128]{2,1,0:T(8,128)(2,1)S(1)}, bf16[8,64,128]{2,1,0:T(8,128)(2,1)S(1)}, u32[]{:S(2)}, u32[]{:S(2)}) %collective-permute-start.15) | collective-permute-done | bytes 131104 | tf_op jit(solution)/shard_map/ppermute | solution.py:46
  111.1 0.6 shard_map.112
  111.7 0.6 shard_map.116.own_ref
  112.4 1.2 collective-permute-done.29.other_ref.core_ref
  113.6 0.6 shard_map.117.refs_1_
  114.2 1.0 collective-permute-start.30
  115.3 1.0 collective-permute-start.31
  116.2 1.3 collective-permute-start.32
  117.5 2.4 %collective-permute-done.30.refs_2_ = f32[3,64,128]{2,1,0:T(8,128)S(1)} collective-permute-done((f32[3,64,128]{2,1,0:T(8,128)S(1)}, f32[3,64,128]{2,1,0:T(8,128)S(1)}, u32[]{:S(2)}, u32[]{:S(2)}) %collective-permute-start.30) | collective-permute-done | bytes 98336 | tf_op jit(solution)/shard_map/ppermute | solution.py:46
  120.0 2.1 %collective-permute-done.31.refs_3_ = f32[3,64,128]{2,1,0:T(8,128)S(1)} collective-permute-done((f32[3,64,128]{2,1,0:T(8,128)S(1)}, f32[3,64,128]{2,1,0:T(8,128)S(1)}, u32[]{:S(2)}, u32[]{:S(2)}) %collective-permute-start.31) | collective-permute-done | bytes 98336 | tf_op jit(solution)/shard_map/ppermute | solution.py:46
  122.1 1.3 collective-permute-done.32.refs_4_
  123.4 1.1 shard_map.118
  124.6 0.4 collective-permute-start.34
  125.1 1.7 %collective-permute-start.35 = (f32[3,64,128]{2,1,0:T(8,128)S(1)}, f32[3,64,128]{2,1,0:T(8,128)S(1)}, u32[]{:S(2)}, u32[]{:S(2)}) collective-permute-start(f32[3,64,128]{2,1,0:T(8,128)S(1)} %get-tuple-element.43.own_ref), channel_id=1, source_target_pairs={{0,192},{1,193},{2,194},{3,195},{4,196},{5,197},{6,198},{7,199},{8... | collective-permute-start | bytes 294920 | tf_op jit(solution)/shard_map/ppermute | solution.py:46
  126.8 3.5 %collective-permute-done.33.d1_ref = f32[3,64,128]{2,1,0:T(8,128)S(1)} collective-permute-done((f32[3,64,128]{2,1,0:T(8,128)S(1)}, f32[3,64,128]{2,1,0:T(8,128)S(1)}, u32[]{:S(2)}, u32[]{:S(2)}) %collective-permute-start.33) | collective-permute-done | bytes 98336 | tf_op jit(solution)/shard_map/ppermute | solution.py:46
  130.3 1.6 %collective-permute-done.34.d2_ref = f32[3,64,128]{2,1,0:T(8,128)S(1)} collective-permute-done((f32[3,64,128]{2,1,0:T(8,128)S(1)}, f32[3,64,128]{2,1,0:T(8,128)S(1)}, u32[]{:S(2)}, u32[]{:S(2)}) %collective-permute-start.34) | collective-permute-done | bytes 98336 | tf_op jit(solution)/shard_map/ppermute | solution.py:46
  131.9 0.6 collective-permute-done.35.d3_ref
  132.5 0.8 shard_map.119.y_ref
  133.3 1.3 shard_map.120
  134.7 1.2 copy.14
  (59 shorter events, 1.1 us)
Async XLA Ops:
  0.0 17.6 %copy-start.2 = (s32[4]{0:T(128)S(1)}, s32[4]{0:T(128)}, u32[]{:S(2)}) copy-start(s32[4]{0:T(128)} %constant.131.clone) | copy-start | bytes 52
  0.0 17.6 %copy-start.3 = (s32[4]{0:T(128)S(1)}, s32[4]{0:T(128)}, u32[]{:S(2)}) copy-start(s32[4]{0:T(128)} %constant.132.clone) | copy-start | bytes 52
  0.0 31.3 %copy-start.4 = (f32[64]{0:T(128)S(1)}, f32[64]{0:T(128)}, u32[]{:S(2)}) copy-start(f32[64]{0:T(128)} %param.16) | copy-start | bytes 772
  0.0 32.8 %copy-start.1 = (f32[8,64]{1,0:T(8,128)S(1)}, f32[8,64]{1,0:T(8,128)}, u32[]{:S(2)}) copy-start(f32[8,64]{1,0:T(8,128)} %param.15) | copy-start | bytes 6148
  1.2 6.4 %collective-permute-start = (bf16[2,64,1024]{2,1,0:T(8,128)(2,1)S(1)}, bf16[2,64,1024]{2,1,0:T(8,128)(2,1)S(1)}, u32[]{:S(2)}, u32[]{:S(2)}) collective-permute-start(bf16[2,64,1024]{2,1,0:T(8,128)(2,1)S(1)} %reshape.54), channel_id=1, source_target_pairs={{0,16},{1,17},{2,18},{3,19},{4,20},{5,21},{6,22},{7,23},{8,72},{9,... | collective-permute-start | bytes 786440 | tf_op jit(solution)/shard_map/ppermute | solution.py:46
  1.7 10.4 %collective-permute-start.1 = (bf16[2,64,1024]{2,1,0:T(8,128)(2,1)S(1)}, bf16[2,64,1024]{2,1,0:T(8,128)(2,1)S(1)}, u32[]{:S(2)}, u32[]{:S(2)}) collective-permute-start(bf16[2,64,1024]{2,1,0:T(8,128)(2,1)S(1)} %reshape.54), channel_id=1, source_target_pairs={{0,48},{1,49},{2,50},{3,51},{4,52},{5,53},{6,54},{7,55},{8,200},{9... | collective-permute-start | bytes 786440 | tf_op jit(solution)/shard_map/ppermute | solution.py:46
  3.3 8.9 %collective-permute-start.2 = (bf16[2,64,1024]{2,1,0:T(8,128)(2,1)S(1)}, bf16[2,64,1024]{2,1,0:T(8,128)(2,1)S(1)}, u32[]{:S(2)}, u32[]{:S(2)}) collective-permute-start(bf16[2,64,1024]{2,1,0:T(8,128)(2,1)S(1)} %reshape.54), channel_id=1, source_target_pairs={{0,32},{1,33},{2,34},{3,35},{4,36},{5,37},{6,38},{7,39},{8,136},{9... | collective-permute-start | bytes 786440 | tf_op jit(solution)/shard_map/ppermute | solution.py:46
  12.2 9.3 %collective-permute-start.16 = (bf16[256,1024]{1,0:T(8,128)(2,1)S(1)}, bf16[256,1024]{1,0:T(8,128)(2,1)S(1)}, u32[]{:S(2)}, u32[]{:S(2)}) collective-permute-start(bf16[256,1024]{1,0:T(8,128)(2,1)S(1)} %pad_maximum_fusion.1.refs_0_.refs_8_), channel_id=1, source_target_pairs={{0,64},{1,65},{2,66},{3,67},{4,68},{5,69},{6,70},{7,71},{8,24},{9,... | collective-permute-start | bytes 1572872 | tf_op jit(solution)/shard_map/ppermute | solution.py:46
  13.9 9.3 %collective-permute-start.17 = (bf16[256,1024]{1,0:T(8,128)(2,1)S(1)}, bf16[256,1024]{1,0:T(8,128)(2,1)S(1)}, u32[]{:S(2)}, u32[]{:S(2)}) collective-permute-start(bf16[256,1024]{1,0:T(8,128)(2,1)S(1)} %pad_maximum_fusion.1.refs_0_.refs_8_), channel_id=1, source_target_pairs={{0,192},{1,193},{2,194},{3,195},{4,196},{5,197},{6,198},{7,199},{8... | collective-permute-start | bytes 1572872 | tf_op jit(solution)/shard_map/ppermute | solution.py:46
  14.3 16.5 %collective-permute-start.18 = (bf16[256,1024]{1,0:T(8,128)(2,1)S(1)}, bf16[256,1024]{1,0:T(8,128)(2,1)S(1)}, u32[]{:S(2)}, u32[]{:S(2)}) collective-permute-start(bf16[256,1024]{1,0:T(8,128)(2,1)S(1)} %pad_maximum_fusion.1.refs_0_.refs_8_), channel_id=1, source_target_pairs={{0,128},{1,129},{2,130},{3,131},{4,132},{5,133},{6,134},{7,135},{8... | collective-permute-start | bytes 1572872 | tf_op jit(solution)/shard_map/ppermute | solution.py:46
  16.6 14.2 %collective-permute-start.19 = (bf16[256,1024]{1,0:T(8,128)(2,1)S(1)}, bf16[256,1024]{1,0:T(8,128)(2,1)}, u32[]{:S(2)}, u32[]{:S(2)}) collective-permute-start(bf16[256,1024]{1,0:T(8,128)(2,1)S(1)} %pad_maximum_fusion.1.refs_0_.refs_8_), channel_id=1, source_target_pairs={{0,8},{1,9},{2,10},{3,11},{4,12},{5,13},{6,14},{7,15},{8,0},{9,1},... | collective-permute-start | bytes 1572872 | tf_op jit(solution)/shard_map/ppermute | solution.py:46
  16.7 16.1 %collective-permute-start.3 = (bf16[256,1024]{1,0:T(8,128)(2,1)S(1)}, bf16[256,1024]{1,0:T(8,128)(2,1)S(1)}, u32[]{:S(2)}, u32[]{:S(2)}) collective-permute-start(bf16[256,1024]{1,0:T(8,128)(2,1)S(1)} %pad_maximum_fusion.refs_0_.refs_8_), channel_id=1, source_target_pairs={{0,64},{1,65},{2,66},{3,67},{4,68},{5,69},{6,70},{7,71},{8,24},{9,... | collective-permute-start | bytes 1572872 | tf_op jit(solution)/shard_map/ppermute | solution.py:46
  21.5 14.4 %collective-permute-start.4 = (bf16[256,1024]{1,0:T(8,128)(2,1)S(1)}, bf16[256,1024]{1,0:T(8,128)(2,1)S(1)}, u32[]{:S(2)}, u32[]{:S(2)}) collective-permute-start(bf16[256,1024]{1,0:T(8,128)(2,1)S(1)} %pad_maximum_fusion.refs_0_.refs_8_), channel_id=1, source_target_pairs={{0,192},{1,193},{2,194},{3,195},{4,196},{5,197},{6,198},{7,199},{8... | collective-permute-start | bytes 1572872 | tf_op jit(solution)/shard_map/ppermute | solution.py:46
  23.1 19.8 %collective-permute-start.5 = (bf16[256,1024]{1,0:T(8,128)(2,1)S(1)}, bf16[256,1024]{1,0:T(8,128)(2,1)S(1)}, u32[]{:S(2)}, u32[]{:S(2)}) collective-permute-start(bf16[256,1024]{1,0:T(8,128)(2,1)S(1)} %pad_maximum_fusion.refs_0_.refs_8_), channel_id=1, source_target_pairs={{0,128},{1,129},{2,130},{3,131},{4,132},{5,133},{6,134},{7,135},{8... | collective-permute-start | bytes 1572872 | tf_op jit(solution)/shard_map/ppermute | solution.py:46
  30.8 12.1 %collective-permute-start.20 = (bf16[256,1024]{1,0:T(8,128)(2,1)S(1)}, bf16[256,1024]{1,0:T(8,128)(2,1)S(1)}, u32[]{:S(2)}, u32[]{:S(2)}) collective-permute-start(bf16[256,1024]{1,0:T(8,128)(2,1)S(1)} %collective-permute-done.16.refs_1_.refs_9_), channel_id=1, source_target_pairs={{0,8},{1,9},{2,10},{3,11},{4,12},{5,13},{6,14},{7,15},{8,0},{9,1},... | collective-permute-start | bytes 1572872 | tf_op jit(solution)/shard_map/ppermute | solution.py:46
  30.8 12.6 %collective-permute-start.21 = (bf16[256,1024]{1,0:T(8,128)(2,1)S(1)}, bf16[256,1024]{1,0:T(8,128)(2,1)S(1)}, u32[]{:S(2)}, u32[]{:S(2)}) collective-permute-start(bf16[256,1024]{1,0:T(8,128)(2,1)S(1)} %collective-permute-done.17.refs_2_.refs_10_), channel_id=1, source_target_pairs={{0,8},{1,9},{2,10},{3,11},{4,12},{5,13},{6,14},{7,15},{8,0},{9,1},... | collective-permute-start | bytes 1572872 | tf_op jit(solution)/shard_map/ppermute | solution.py:46
  32.8 20.3 %collective-permute-start.22 = (bf16[256,1024]{1,0:T(8,128)(2,1)S(1)}, bf16[256,1024]{1,0:T(8,128)(2,1)S(1)}, u32[]{:S(2)}, u32[]{:S(2)}) collective-permute-start(bf16[256,1024]{1,0:T(8,128)(2,1)S(1)} %collective-permute-done.18.refs_3_.refs_11_), channel_id=1, source_target_pairs={{0,8},{1,9},{2,10},{3,11},{4,12},{5,13},{6,14},{7,15},{8,0},{9,1},... | collective-permute-start | bytes 1572872 | tf_op jit(solution)/shard_map/ppermute | solution.py:46
  35.8 28.6 %collective-permute-start.6 = (bf16[256,1024]{1,0:T(8,128)(2,1)S(1)}, bf16[256,1024]{1,0:T(8,128)(2,1)S(1)}, u32[]{:S(2)}, u32[]{:S(2)}) collective-permute-start(bf16[256,1024]{1,0:T(8,128)(2,1)S(1)} %pad_maximum_fusion.refs_0_.refs_8_), channel_id=1, source_target_pairs={{0,8},{1,9},{2,10},{3,11},{4,12},{5,13},{6,14},{7,15},{8,0},{9,1},... | collective-permute-start | bytes 1572872 | tf_op jit(solution)/shard_map/ppermute | solution.py:46
  42.9 21.7 %collective-permute-start.7 = (bf16[256,1024]{1,0:T(8,128)(2,1)S(1)}, bf16[256,1024]{1,0:T(8,128)(2,1)S(1)}, u32[]{:S(2)}, u32[]{:S(2)}) collective-permute-start(bf16[256,1024]{1,0:T(8,128)(2,1)S(1)} %collective-permute-done.3.refs_1_.refs_9_), channel_id=1, source_target_pairs={{0,8},{1,9},{2,10},{3,11},{4,12},{5,13},{6,14},{7,15},{8,0},{9,1},... | collective-permute-start | bytes 1572872 | tf_op jit(solution)/shard_map/ppermute | solution.py:46
  42.9 21.8 %collective-permute-start.8 = (bf16[256,1024]{1,0:T(8,128)(2,1)S(1)}, bf16[256,1024]{1,0:T(8,128)(2,1)S(1)}, u32[]{:S(2)}, u32[]{:S(2)}) collective-permute-start(bf16[256,1024]{1,0:T(8,128)(2,1)S(1)} %collective-permute-done.4.refs_2_.refs_10_), channel_id=1, source_target_pairs={{0,8},{1,9},{2,10},{3,11},{4,12},{5,13},{6,14},{7,15},{8,0},{9,1},... | collective-permute-start | bytes 1572872 | tf_op jit(solution)/shard_map/ppermute | solution.py:46
  43.4 24.4 %collective-permute-start.9 = (bf16[256,1024]{1,0:T(8,128)(2,1)S(1)}, bf16[256,1024]{1,0:T(8,128)(2,1)S(1)}, u32[]{:S(2)}, u32[]{:S(2)}) collective-permute-start(bf16[256,1024]{1,0:T(8,128)(2,1)S(1)} %collective-permute-done.5.refs_3_.refs_11_), channel_id=1, source_target_pairs={{0,8},{1,9},{2,10},{3,11},{4,12},{5,13},{6,14},{7,15},{8,0},{9,1},... | collective-permute-start | bytes 1572872 | tf_op jit(solution)/shard_map/ppermute | solution.py:46
  57.8 22.2 %collective-permute-start.25 = (bf16[2,8,64,128]{3,2,1,0:T(8,128)(2,1)S(1)}, bf16[2,8,64,128]{3,2,1,0:T(8,128)(2,1)S(1)}, u32[]{:S(2)}, u32[]{:S(2)}) collective-permute-start(bf16[2,8,64,128]{3,2,1,0:T(8,128)(2,1)S(1)} %get-tuple-element.37), channel_id=1, source_target_pairs={{0,1},{1,2},{2,3},{3,4},{4,5},{5,6},{6,7},{7,0},{8,15},{9,8},{10,9... | collective-permute-start | bytes 786440 | tf_op jit(solution)/shard_map/ppermute | solution.py:46
  64.5 15.4 %collective-permute-start.27 = (bf16[1,8,64,128]{3,2,1,0:T(8,128)(2,1)S(1)}, bf16[1,8,64,128]{3,2,1,0:T(8,128)(2,1)S(1)}, u32[]{:S(2)}, u32[]{:S(2)}) collective-permute-start(bf16[1,8,64,128]{3,2,1,0:T(8,128)(2,1)S(1)} %get-tuple-element.39), channel_id=1, source_target_pairs={{0,7},{1,0},{2,1},{3,2},{4,3},{5,4},{6,5},{7,6},{8,9},{9,10},{10,1... | collective-permute-start | bytes 393224 | tf_op jit(solution)/shard_map/ppermute | solution.py:46
  64.7 24.5 %collective-permute-start.24 = (bf16[8,64,128]{2,1,0:T(8,128)(2,1)S(1)}, bf16[8,64,128]{2,1,0:T(8,128)(2,1)S(1)}, u32[]{:S(2)}, u32[]{:S(2)}) collective-permute-start(bf16[8,64,128]{2,1,0:T(8,128)(2,1)S(1)} %bitcast.56), channel_id=1, source_target_pairs={{0,7},{1,0},{2,1},{3,2},{4,3},{5,4},{6,5},{7,6},{8,9},{9,10},{10,1... | collective-permute-start | bytes 393224 | tf_op jit(solution)/shard_map/ppermute | solution.py:46
  64.8 29.5 %collective-permute-start.23 = (bf16[8,64,128]{2,1,0:T(8,128)(2,1)S(1)}, bf16[8,64,128]{2,1,0:T(8,128)(2,1)S(1)}, u32[]{:S(2)}, u32[]{:S(2)}) collective-permute-start(bf16[8,64,128]{2,1,0:T(8,128)(2,1)S(1)} %bitcast.55), channel_id=1, source_target_pairs={{0,1},{1,2},{2,3},{3,4},{4,5},{5,6},{6,7},{7,0},{8,15},{9,8},{10,9... | collective-permute-start | bytes 393224 | tf_op jit(solution)/shard_map/ppermute | solution.py:46
  72.3 16.8 %collective-permute-start.12 = (bf16[2,8,64,128]{3,2,1,0:T(8,128)(2,1)S(1)}, bf16[2,8,64,128]{3,2,1,0:T(8,128)(2,1)S(1)}, u32[]{:S(2)}, u32[]{:S(2)}) collective-permute-start(bf16[2,8,64,128]{3,2,1,0:T(8,128)(2,1)S(1)} %get-tuple-element.29), channel_id=1, source_target_pairs={{0,1},{1,2},{2,3},{3,4},{4,5},{5,6},{6,7},{7,0},{8,15},{9,8},{10,9... | collective-permute-start | bytes 786440 | tf_op jit(solution)/shard_map/ppermute | solution.py:46
  79.9 46.9 %copy-start = (f32[64,2,128]{2,1,0:T(2,128)S(1)}, f32[64,2,128]{2,1,0:T(2,128)}, u32[]{:S(2)}) copy-start(f32[64,2,128]{2,1,0:T(2,128)} %param.14) | copy-start | bytes 196612
  79.9 5.2 %collective-permute-start.14 = (bf16[1,8,64,128]{3,2,1,0:T(8,128)(2,1)S(1)}, bf16[1,8,64,128]{3,2,1,0:T(8,128)(2,1)S(1)}, u32[]{:S(2)}, u32[]{:S(2)}) collective-permute-start(bf16[1,8,64,128]{3,2,1,0:T(8,128)(2,1)S(1)} %get-tuple-element.31), channel_id=1, source_target_pairs={{0,7},{1,0},{2,1},{3,2},{4,3},{5,4},{6,5},{7,6},{8,9},{9,10},{10,1... | collective-permute-start | bytes 393224 | tf_op jit(solution)/shard_map/ppermute | solution.py:46
  80.0 24.6 %collective-permute-start.11 = (bf16[8,64,128]{2,1,0:T(8,128)(2,1)S(1)}, bf16[8,64,128]{2,1,0:T(8,128)(2,1)S(1)}, u32[]{:S(2)}, u32[]{:S(2)}) collective-permute-start(bf16[8,64,128]{2,1,0:T(8,128)(2,1)S(1)} %bitcast.57), channel_id=1, source_target_pairs={{0,7},{1,0},{2,1},{3,2},{4,3},{5,4},{6,5},{7,6},{8,9},{9,10},{10,1... | collective-permute-start | bytes 393224 | tf_op jit(solution)/shard_map/ppermute | solution.py:46
  85.1 19.5 %collective-permute-start.10 = (bf16[8,64,128]{2,1,0:T(8,128)(2,1)S(1)}, bf16[8,64,128]{2,1,0:T(8,128)(2,1)S(1)}, u32[]{:S(2)}, u32[]{:S(2)}) collective-permute-start(bf16[8,64,128]{2,1,0:T(8,128)(2,1)S(1)} %bitcast.58), channel_id=1, source_target_pairs={{0,1},{1,2},{2,3},{3,4},{4,5},{5,6},{6,7},{7,0},{8,15},{9,8},{10,9... | collective-permute-start | bytes 393224 | tf_op jit(solution)/shard_map/ppermute | solution.py:46
  89.1 14.1 %collective-permute-start.26 = (bf16[8,64,128]{2,1,0:T(8,128)(2,1)S(1)}, bf16[8,64,128]{2,1,0:T(8,128)(2,1)S(1)}, u32[]{:S(2)}, u32[]{:S(2)}) collective-permute-start(bf16[8,64,128]{2,1,0:T(8,128)(2,1)S(1)} %get-tuple-element.46), channel_id=1, source_target_pairs={{0,5},{1,6},{2,7},{3,0},{4,1},{5,2},{6,3},{7,4},{8,11},{9,12},{10,... | collective-permute-start | bytes 393224 | tf_op jit(solution)/shard_map/ppermute | solution.py:46
  89.2 14.7 %collective-permute-start.28 = (bf16[8,64,128]{2,1,0:T(8,128)(2,1)S(1)}, bf16[8,64,128]{2,1,0:T(8,128)(2,1)S(1)}, u32[]{:S(2)}, u32[]{:S(2)}) collective-permute-start(bf16[8,64,128]{2,1,0:T(8,128)(2,1)S(1)} %get-tuple-element.45), channel_id=1, source_target_pairs={{0,3},{1,4},{2,5},{3,6},{4,7},{5,0},{6,1},{7,2},{8,13},{9,14},{10,... | collective-permute-start | bytes 393224 | tf_op jit(solution)/shard_map/ppermute | solution.py:46
  94.3 13.5 %collective-permute-start.13 = (bf16[8,64,128]{2,1,0:T(8,128)(2,1)S(1)}, bf16[8,64,128]{2,1,0:T(8,128)(2,1)S(1)}, u32[]{:S(2)}, u32[]{:S(2)}) collective-permute-start(bf16[8,64,128]{2,1,0:T(8,128)(2,1)S(1)} %get-tuple-element.56), channel_id=1, source_target_pairs={{0,5},{1,6},{2,7},{3,0},{4,1},{5,2},{6,3},{7,4},{8,11},{9,12},{10,... | collective-permute-start | bytes 393224 | tf_op jit(solution)/shard_map/ppermute | solution.py:46
  103.1 8.0 %collective-permute-start.15 = (bf16[8,64,128]{2,1,0:T(8,128)(2,1)S(1)}, bf16[8,64,128]{2,1,0:T(8,128)(2,1)S(1)}, u32[]{:S(2)}, u32[]{:S(2)}) collective-permute-start(bf16[8,64,128]{2,1,0:T(8,128)(2,1)S(1)} %get-tuple-element.55), channel_id=1, source_target_pairs={{0,3},{1,4},{2,5},{3,6},{4,7},{5,0},{6,1},{7,2},{8,13},{9,14},{10,... | collective-permute-start | bytes 393224 | tf_op jit(solution)/shard_map/ppermute | solution.py:46
  112.3 1.3 collective-permute-start.29
  114.2 5.7 %collective-permute-start.30 = (f32[3,64,128]{2,1,0:T(8,128)S(1)}, f32[3,64,128]{2,1,0:T(8,128)S(1)}, u32[]{:S(2)}, u32[]{:S(2)}) collective-permute-start(f32[3,64,128]{2,1,0:T(8,128)S(1)} %shard_map.117.refs_1_), channel_id=1, source_target_pairs={{0,16},{1,17},{2,18},{3,19},{4,20},{5,21},{6,22},{7,23},{8,24},{9,... | collective-permute-start | bytes 294920 | tf_op jit(solution)/shard_map/ppermute | solution.py:46
  115.3 6.9 %collective-permute-start.31 = (f32[3,64,128]{2,1,0:T(8,128)S(1)}, f32[3,64,128]{2,1,0:T(8,128)S(1)}, u32[]{:S(2)}, u32[]{:S(2)}) collective-permute-start(f32[3,64,128]{2,1,0:T(8,128)S(1)} %shard_map.117.refs_1_), channel_id=1, source_target_pairs={{0,32},{1,33},{2,34},{3,35},{4,36},{5,37},{6,38},{7,39},{8,40},{9,... | collective-permute-start | bytes 294920 | tf_op jit(solution)/shard_map/ppermute | solution.py:46
  116.2 7.2 %collective-permute-start.32 = (f32[3,64,128]{2,1,0:T(8,128)S(1)}, f32[3,64,128]{2,1,0:T(8,128)S(1)}, u32[]{:S(2)}, u32[]{:S(2)}) collective-permute-start(f32[3,64,128]{2,1,0:T(8,128)S(1)} %shard_map.117.refs_1_), channel_id=1, source_target_pairs={{0,48},{1,49},{2,50},{3,51},{4,52},{5,53},{6,54},{7,55},{8,56},{9,... | collective-permute-start | bytes 294920 | tf_op jit(solution)/shard_map/ppermute | solution.py:46
  124.5 5.7 %collective-permute-start.33 = (f32[3,64,128]{2,1,0:T(8,128)S(1)}, f32[3,64,128]{2,1,0:T(8,128)S(1)}, u32[]{:S(2)}, u32[]{:S(2)}) collective-permute-start(f32[3,64,128]{2,1,0:T(8,128)S(1)} %get-tuple-element.43.own_ref), channel_id=1, source_target_pairs={{0,64},{1,65},{2,66},{3,67},{4,68},{5,69},{6,70},{7,71},{8,72},{9,... | collective-permute-start | bytes 294920 | tf_op jit(solution)/shard_map/ppermute | solution.py:46
  124.6 7.3 %collective-permute-start.34 = (f32[3,64,128]{2,1,0:T(8,128)S(1)}, f32[3,64,128]{2,1,0:T(8,128)S(1)}, u32[]{:S(2)}, u32[]{:S(2)}) collective-permute-start(f32[3,64,128]{2,1,0:T(8,128)S(1)} %get-tuple-element.43.own_ref), channel_id=1, source_target_pairs={{0,128},{1,129},{2,130},{3,131},{4,132},{5,133},{6,134},{7,135},{8... | collective-permute-start | bytes 294920 | tf_op jit(solution)/shard_map/ppermute | solution.py:46
  125.1 7.5 %collective-permute-start.35 = (f32[3,64,128]{2,1,0:T(8,128)S(1)}, f32[3,64,128]{2,1,0:T(8,128)S(1)}, u32[]{:S(2)}, u32[]{:S(2)}) collective-permute-start(f32[3,64,128]{2,1,0:T(8,128)S(1)} %get-tuple-element.43.own_ref), channel_id=1, source_target_pairs={{0,192},{1,193},{2,194},{3,195},{4,196},{5,197},{6,198},{7,199},{8... | collective-permute-start | bytes 294920 | tf_op jit(solution)/shard_map/ppermute | solution.py:46
where the time goes:
time: 136 us
  waiting for transfers between devices  52.4 us (39%)
  starting transfers between devices  45.7 us (34%)
  Pallas kernels  33 us (24%)
  local copies, waits for them, and re-layouts  2.97 us (2%)
  other arithmetic  1.44 us (1%)
    ppermute x36, waiting for transfers between devices, send(): return lax.ppermute(array, BOTH, perm)  52.4 us
    ppermute x36, starting transfers between devices, send(): return lax.ppermute(array, BOTH, perm)  45.7 us
    pallas_call x4, Pallas kernels, product_call(): pl.pallas_call(body, out_shape=shape, grid_spec=pltpu.PrefetchScalarGridS...  18.1 us
    pallas_call x1, Pallas kernels, energy_call(): pl.pallas_call(energy_kernel, out_shape=jax.ShapeDtypeStruct((steps, 2, o...  9.27 us
    pallas_call x7, Pallas kernels, small_call(): pl.pallas_call(kernel, out_shape=out_shape, in_specs=specs, out_specs=out...  5.6 us
  transfers between devices with their start and end apart: 36, of which 17 were waited for; matrix products, arithmetic and copies ran while one was open for 1% of the time, Pallas kernels for 21%

commit v1 on v0

--- a/solution.py
+++ b/solution.py
@@ -71,8 +71,8 @@
         sq_re = re * re - im * im
         sq_im = 2.0 * re * im
         cols = pl.ds(pl.multiple_of(n * 2 * orbitals, 2 * orbitals), 2 * orbitals)
-        out_ref[pl.program_id(0), 0, :, cols] = (sq_re * b_re - sq_im * b_im).astype(jnp.bfloat16)
-        out_ref[pl.program_id(0), 1, :, cols] = (sq_re * b_im + sq_im * b_re).astype(jnp.bfloat16)
+        out_ref[0, 0, :, cols] = (sq_re * b_re - sq_im * b_im).astype(jnp.bfloat16)
+        out_ref[0, 1, :, cols] = (sq_re * b_im + sq_im * b_re).astype(jnp.bfloat16)
         return carry
 
     lax.fori_loop(0, slot_count // 2, pair, 0, unroll=4)
@@ -90,7 +90,9 @@
                 pl.BlockSpec((1, sources, orbitals, width), lambda t, *_: (t, 0, 0, 0)),
                 pl.BlockSpec((sources, 1, orbitals, width), lambda t, *_: (0, t, 0, 0)),
             ],
-            out_specs=pl.BlockSpec(memory_space=pltpu.VMEM),
+            out_specs=pl.BlockSpec(
+                (1, 2, orbitals, sources * orbitals), lambda t, *_: (t, 0, 0, 0)
+            ),
         ),
         compiler_params=pltpu.CompilerParams(vmem_limit_bytes=14 << 20),
         cost_estimate=pl.CostEstimate(
@@ -106,100 +108,88 @@
     )
 
 
-def product_tile(energy_ref, panel_refs, norm):
-    steps, _, orbitals, depth = energy_ref.shape
-    width = 2 * orbitals
-    left = energy_ref[...].reshape(steps * 2 * orbitals, depth)
-    count = len(panel_refs) // 2
-    right = jnp.concatenate(
-        [
-            jnp.concatenate([ref[...] for ref in panel_refs[:count]], axis=0),
-            jnp.concatenate([ref[...] for ref in panel_refs[count:]], axis=0),
-        ],
-        axis=1,
-    )
-    both = jnp.dot(left, right, preferred_element_type=jnp.float32)
-    both = both.reshape(steps, 2, orbitals, 2 * width)
-    lane = lax.broadcasted_iota(jnp.int32, (steps, orbitals, width), 2)
-    sign = jnp.where(lane < orbitals, -norm, norm)
-    values = []
-    for half in range(2):
-        part_re = both[:, 0, :, half * width : (half + 1) * width]
-        part_im = both[:, 1, :, half * width : (half + 1) * width]
-        values.append(part_re * norm + sign * pltpu.roll(part_im, orbitals, 2))
-    return values
-
-
-def product_call(norm, cols, energy, panels, outputs):
+def product_call(norm, cols, energy, panels, kinds):
     steps, _, orbitals, depth = energy.shape
     width = 2 * orbitals
-    sizes, kinds = {}, {}
-    for turn in outputs:
-        for result, place, kind in turn:
-            sizes[result] = max(sizes.get(result, 0), place + 1)
-            kinds[result] = kind
-    shape = [
-        jax.ShapeDtypeStruct((sizes[n], steps, orbitals, width), kinds[n]) for n in range(len(sizes))
-    ]
-    count = len(panels)
+    shape = [jax.ShapeDtypeStruct((count, steps, orbitals, width), kind) for count, kind in kinds]
+    places = [(n, at) for n, (count, _) in enumerate(kinds) for at in range(count)]
+    pieces, tiles = len(panels), len(places)
 
     def body(cols_ref, energy_ref, *refs):
-        panel_refs, out_refs = refs[: 2 * count], refs[2 * count :]
-        values = product_tile(energy_ref, panel_refs, norm)
-        for turn, targets in enumerate(outputs):
-
-            @pl.when(pl.program_id(0) == turn)
-            def _():
-                for value, (result, place, kind) in zip(values, targets):
-                    out_refs[result][place] = value.astype(kind)
-
-    def panel_spec(panel, which):
-        return pl.BlockSpec((panel.shape[0], width), lambda n, cols: (0, cols[2 * n + which]))
+        panel_refs, out_refs = refs[: tiles * pieces], refs[tiles * pieces :]
+        left = energy_ref[...].reshape(steps * 2 * orbitals, depth)
+        right = jnp.concatenate(
+            [
+                jnp.concatenate(
+                    [ref[...] for ref in panel_refs[tile * pieces : (tile + 1) * pieces]], axis=0
+                )
+                for tile in range(tiles)
+            ],
+            axis=1,
+        )
+        both = jnp.dot(left, right, preferred_element_type=jnp.float32)
+        both = both.reshape(steps, 2, orbitals, tiles * width)
+        lane = lax.broadcasted_iota(jnp.int32, (steps, orbitals, width), 2)
+        sign = jnp.where(lane < orbitals, -norm, norm)
+        for tile, (result, at) in enumerate(places):
+            part_re = both[:, 0, :, tile * width : (tile + 1) * width]
+            part_im = both[:, 1, :, tile * width : (tile + 1) * width]
+            value = part_re * norm + sign * pltpu.roll(part_im, orbitals, 2)
+            out_refs[result][at] = value.astype(kinds[result][1])
+
+    def panel_spec(panel, tile):
+        return pl.BlockSpec((panel.shape[0], width), lambda n, cols: (0, cols[tile]))
 
     return pl.pallas_call(
         body,
         out_shape=shape,
         grid_spec=pltpu.PrefetchScalarGridSpec(
             num_scalar_prefetch=1,
-            grid=(len(outputs),),
+            grid=(1,),
             in_specs=[pl.BlockSpec(memory_space=pltpu.VMEM)]
-            + [panel_spec(panel, which) for which in range(2) for panel in panels],
+            + [panel_spec(panel, tile) for tile in range(tiles) for panel in panels],
             out_specs=[pl.BlockSpec(s.shape, lambda n, cols: (0, 0, 0, 0)) for s in shape],
         ),
-        compiler_params=pltpu.CompilerParams(vmem_limit_bytes=20 << 20),
+        compiler_params=pltpu.CompilerParams(vmem_limit_bytes=32 << 20),
         cost_estimate=pl.CostEstimate(
-            flops=2 * len(outputs) * steps * 2 * orbitals * depth * 2 * width,
-            bytes_accessed=2 * depth * (steps * 2 * orbitals + len(outputs) * 2 * width),
+            flops=2 * tiles * steps * 2 * orbitals * depth * width,
+            bytes_accessed=2 * depth * (steps * 2 * orbitals + tiles * width),
             transcendentals=0,
         ),
-    )(cols, energy, *panels, *panels)
+    )(cols, energy, *(panels * tiles))
 
 
 def turned(factor_re, factor_im, value):
     return factor_re * value + factor_im * pltpu.roll(value, value.shape[-1] // 2, value.ndim - 1)
 
 
-def end_kernel(fre_ref, fim_ref, *refs):
-    part_refs, (sum_ref, end_ref) = refs[:-2], refs[-2:]
+def end_of(fre_ref, fim_ref, parts, sum_ref):
+    own_ref, ahead_ref, back_ref, from5_ref, from3_ref = parts
     steps, orbitals, width = sum_ref.shape
     state = jnp.zeros((orbitals, width), jnp.float32)
     for t in range(steps):
-        value = part_refs[0][t]
-        for ref in part_refs[1:]:
-            value = value + ref[t].astype(jnp.float32)
+        value = own_ref[0, t]
+        for arrived in (ahead_ref[2, t], back_ref[1, t], from5_ref[t], from3_ref[t]):
+            value = value + arrived.astype(jnp.float32)
         sum_ref[t] = value
         state = turned(fre_ref[t], fim_ref[t], state + value)
-    end_ref[...] = state
-
-
-def message_kernel(fre_ref, fim_ref, end0_ref, end1_ref, msg_ref):
+    return state
+
+
+def even_kernel(fre_ref, fim_ref, *refs):
+    parts, (sum_ref, end_ref) = refs[:-2], refs[-2:]
+    end_ref[...] = end_of(fre_ref, fim_ref, parts, sum_ref)
+
+
+def odd_kernel(fre_ref, fim_ref, even_ref, *refs):
+    parts, (sum_ref, msg_ref) = refs[:-2], refs[-2:]
     steps, orbitals, width = fre_ref.shape
     lane = lax.broadcasted_iota(jnp.int32, (orbitals, width), 1)
     block = jnp.where(lane < width // 2, 1.0, 0.0).astype(jnp.float32)
     for t in range(steps):
         block = turned(fre_ref[t], fim_ref[t], block)
-    msg_ref[0] = end0_ref[...]
-    msg_ref[1] = end1_ref[...]
+    msg_ref[0] = even_ref[...]
+    msg_ref[1] = end_of(fre_ref, fim_ref, parts, sum_ref)
     msg_ref[2] = block
 
 
@@ -258,40 +248,54 @@
         out_ref[n] = plane
 
 
-def line_kernel(place, where_ref, own_ref, d1_ref, d2_ref, d3_ref, before_ref, total_ref):
-    at = where_ref[place]
-    one = unit(own_ref.shape[1:])
-    behind = [read(d1_ref), read(d2_ref), read(d3_ref)]
+def before_of(at, behind, one):
     before = one
     for back in (3, 2, 1):
         here = chosen(at >= back, behind[back - 1], one)
         before = after(here, before)
+    return before
+
+
+def line_kernel(where_ref, own_ref, d1_ref, d2_ref, d3_ref, before_ref, total_ref):
+    at = where_ref[1]
+    one = unit(own_ref.shape[1:])
+    behind = [read(d1_ref), read(d2_ref), read(d3_ref)]
+    before = before_of(at, behind, one)
     for n, plane in enumerate(before):
         before_ref[n] = plane
-    if total_ref is not None:
-        total = after(read(own_ref), before)
-        for back in (3, 2, 1):
-            here = chosen(at < back, behind[back - 1], one)
-            total = after(here, total)
-        for n, plane in enumerate(total):
-            total_ref[n] = plane
-
-
-def column_kernel(where_ref, own_ref, d1_ref, d2_ref, d3_ref, before_ref):
-    line_kernel(2, where_ref, own_ref, d1_ref, d2_ref, d3_ref, before_ref, None)
-
-
-def last_kernel(where_ref, fre_ref, fim_ref, sum0_ref, sum1_ref, init_ref, y_ref, x_ref, core_ref, out_ref):
+    total = after(read(own_ref), before)
+    for back in (3, 2, 1):
+        here = chosen(at < back, behind[back - 1], one)
+        total = after(here, total)
+    for n, plane in enumerate(total):
+        total_ref[n] = plane
+
+
+def last_kernel(
+    where_ref,
+    fre_ref,
+    fim_ref,
+    sum0_ref,
+    sum1_ref,
+    init_ref,
+    d1_ref,
+    d2_ref,
+    d3_ref,
+    x_ref,
+    core_ref,
+    out_ref,
+):
     steps = fre_ref.shape[0]
     one = unit(init_ref.shape[1:])
-    from_core = chosen(where_ref[0] == 1, read(core_ref), one)
-    entering = after(from_core, after(read(x_ref), read(y_ref)))
-    start = after(entering, [init_ref[0], init_ref[1], one[2]])
+    column = before_of(where_ref[2], [read(d1_ref), read(d2_ref), read(d3_ref)], one)
+    start = after(column, [init_ref[0], init_ref[1], one[2]])
+    start = after(read(x_ref), start)
+    start = after(chosen(where_ref[0] == 1, read(core_ref), one), start)
     for half, sum_ref in enumerate((sum0_ref, sum1_ref)):
         state = start[half]
         for t in range(steps):
             state = turned(fre_ref[t], fim_ref[t], state + sum_ref[t])
-            out_ref[t, half] = state
+            out_ref[t, :, half, :] = state
 
 
 def small_call(kernel, out_shape, scalars, *arrays):
@@ -328,29 +332,21 @@
     return total.astype(jnp.bfloat16)
 
 
-def column_sum(norm, cols_of, energy, panels):
-    bf16, f32 = jnp.bfloat16, jnp.float32
-    s46, s2, s7 = product_call(
-        norm,
-        cols_of((4, 6, 2, 7)),
-        energy,
-        panels,
-        (((0, 0, bf16), (0, 1, bf16)), ((1, 0, bf16), (2, 0, bf16))),
-    )
-    r46 = send(s46, depth_perm(1))
-    r2 = send(s2, depth_perm(-1))
-    p3, p5, s1, p0 = product_call(
-        norm,
-        cols_of((3, 5, 1, 0)),
-        energy,
-        panels,
-        (((0, 0, f32), (1, 0, f32)), ((2, 0, bf16), (3, 0, f32))),
-    )
-    r5 = send(add_rounded(p5[0], r46[1]), depth_perm(-3))
-    r3 = send(add_rounded(p3[0], r46[0], r2[0]), depth_perm(3))
-    r1 = send(s1[0], depth_perm(1))
-    r7 = send(s7[0], depth_perm(-1))
-    return [p0[0], r1, r7, r5, r3]
+def column_sum(norm, cols_of, energy, panels, split):
+    near = ((3, jnp.bfloat16), (2, jnp.bfloat16), (1, jnp.float32))
+    far = ((2, jnp.float32),)
+    order = (4, 6, 1, 2, 7, 0, 3, 5)
+    if split:
+        ahead, back, own = product_call(norm, cols_of(order[:6]), energy, panels, near)
+    else:
+        ahead, back, own, rest = product_call(norm, cols_of(order), energy, panels, near + far)
+    ahead = send(ahead, depth_perm(1))
+    back = send(back, depth_perm(-1))
+    if split:
+        (rest,) = product_call(norm, cols_of(order[6:]), energy, panels, far)
+    from5 = send(add_rounded(rest[1], ahead[1]), depth_perm(-3))
+    from3 = send(add_rounded(rest[0], ahead[0], back[0]), depth_perm(3))
+    return [own, ahead, back, from5, from3]
 
 
 def slot_table(row_index):
@@ -394,9 +390,11 @@
     blocks0 = far_blocks(line0)
     blocks1 = far_blocks(line1)
     panels0 = blocks0 + [send(block, CORE_SWAP) for block in blocks0]
-    parts0 = column_sum(norm, cols_of, energy, panels0)
-    panels1 = blocks1 + [send(block, CORE_SWAP) for block in blocks1]
-    parts1 = column_sum(norm, cols_of, energy, panels1)
+    parts0 = column_sum(norm, cols_of, energy, panels0, False)
+    panels1 = list(blocks1)
+    for block in blocks1:
+        panels1.append(send(block, CORE_SWAP))
+    parts1 = column_sum(norm, cols_of, energy, panels1, True)
 
     rotate_re = retention * jnp.cos(phase_angle)[None, :]
     rotate_im = retention * jnp.sin(phase_angle)[None, :]
@@ -409,35 +407,29 @@
     message = jax.ShapeDtypeStruct((3, orbitals, width), jnp.float32)
     total = jax.ShapeDtypeStruct((steps, orbitals, width), jnp.float32)
     end = jax.ShapeDtypeStruct((orbitals, width), jnp.float32)
-    sum0, end0 = small_call(end_kernel, (total, end), None, fre, fim, *parts0)
-    sum1, end1 = small_call(end_kernel, (total, end), None, fre, fim, *parts1)
-    ends = small_call(message_kernel, message, None, fre, fim, end0, end1)
+    sum0, end0 = small_call(even_kernel, (total, end), None, fre, fim, *parts0)
+    sum1, ends = small_call(odd_kernel, (total, message), None, fre, fim, end0, *parts1)
     other = send(ends, CORE_SWAP)
     chip = small_call(chip_kernel, message, where, ends, other)
     row_perm = lambda by: perm_of(lambda y, x, core, z: (y, x + by, core, z))
     column_perm = lambda by: perm_of(lambda y, x, core, z: (y + by, x, core, z))
     behind = [send(chip, row_perm(back)) for back in (1, 2, 3)]
 
-    def across(*refs):
-        line_kernel(1, *refs)
-
-    before_x, line = small_call(across, (message, message), where, chip, *behind)
+    before_x, line = small_call(line_kernel, (message, message), where, chip, *behind)
     behind = [send(line, column_perm(back)) for back in (1, 2, 3)]
-    before_y = small_call(column_kernel, message, where, line, *behind)
-    out = small_call(
+    return small_call(
         last_kernel,
-        jax.ShapeDtypeStruct((steps, 2, orbitals, width), jnp.float32),
+        jax.ShapeDtypeStruct((steps, orbitals, 2, width), jnp.float32),
         where,
         fre,
         fim,
         sum0,
         sum1,
         start,
-        before_y,
+        *behind,
         before_x,
         other,
     )
-    return jnp.swapaxes(out, 1, 2)
 
 
 def solution(mesh):

time: 136 us -> 115 us (0.85)
  the two profiles are of different devices: /device:TPU:78 before, /device:TPU:8 now
where the time goes in v1:
time: 115 us; the launch traced here: 114 us
  starting transfers between devices  54.3 us (47%)
  waiting for transfers between devices  29 us (25%)
  Pallas kernels  27.2 us (24%)
  local copies, waits for them, and re-layouts  1.76 us (2%)
  other arithmetic  1.46 us (1%)
    ppermute x32, starting transfers between devices, send(): return lax.ppermute(array, BOTH, perm)  54.3 us
    ppermute x32, waiting for transfers between devices, send(): return lax.ppermute(array, BOTH, perm)  29 us
    pallas_call x3, Pallas kernels, product_call(): pl.pallas_call(body, out_shape=shape, grid_spec=pltpu.PrefetchScalarGridS...  12.6 us
    pallas_call x1, Pallas kernels, energy_call(): pl.pallas_call(energy_kernel, out_shape=jax.ShapeDtypeStruct((steps, 2, o...  9.29 us
    pallas_call x5, Pallas kernels, small_call(): pl.pallas_call(kernel, out_shape=out_shape, in_specs=specs, out_specs=out...  5.34 us
  transfers between devices with their start and end apart: 32, of which 16 were waited for; matrix products, arithmetic and copies ran while one was open for 2% of the time, Pallas kernels for 20%

profile of v1, /device:TPU:8, one launch (start us, length us, event | category | flops | bytes accessed | tf_op | source)
XLA Modules:
  0.0 114.1 jit_solution(12990793557927363705)
XLA Ops:
  0.0 1.0 copy.19
  1.0 0.1 reshape.54
  1.1 3.1 %collective-permute-start.2 = (bf16[2,64,1024]{2,1,0:T(8,128)(2,1)S(1)}, bf16[2,64,1024]{2,1,0:T(8,128)(2,1)S(1)}, u32[]{:S(2)}, u32[]{:S(2)}) collective-permute-start(bf16[2,64,1024]{2,1,0:T(8,128)(2,1)S(1)} %reshape.54), channel_id=1, source_target_pairs={{0,32},{1,33},{2,34},{3,35},{4,36},{5,37},{6,38},{7,39},{8,136},{9... | collective-permute-start | bytes 786440 | tf_op jit(solution)/shard_map/ppermute | solution.py:46
  4.3 1.1 collective-permute-start.1
  5.4 0.9 collective-permute-start
  6.3 0.8 select_add_fusion.3
  7.1 0.1 add.159
  7.2 0.1 add.156
  7.3 0.1 add.150
  7.4 0.1 add.146
  7.5 1.6 %collective-permute-done.2 = bf16[2,64,1024]{2,1,0:T(8,128)(2,1)S(1)} collective-permute-done((bf16[2,64,1024]{2,1,0:T(8,128)(2,1)S(1)}, bf16[2,64,1024]{2,1,0:T(8,128)(2,1)S(1)}, u32[]{:S(2)}, u32[]{:S(2)}) %collective-permute-start.2) | collective-permute-done | bytes 262176 | tf_op jit(solution)/shard_map/ppermute | solution.py:46
  9.1 2.9 %collective-permute-done.1 = bf16[2,64,1024]{2,1,0:T(8,128)(2,1)S(1)} collective-permute-done((bf16[2,64,1024]{2,1,0:T(8,128)(2,1)S(1)}, bf16[2,64,1024]{2,1,0:T(8,128)(2,1)S(1)}, u32[]{:S(2)}, u32[]{:S(2)}) %collective-permute-start.1) | collective-permute-done | bytes 262176 | tf_op jit(solution)/shard_map/ppermute | solution.py:46
  12.0 0.9 collective-permute-done
  13.0 1.7 %collective-permute-start.3 = (bf16[256,1024]{1,0:T(8,128)(2,1)S(1)}, bf16[256,1024]{1,0:T(8,128)(2,1)S(1)}, u32[]{:S(2)}, u32[]{:S(2)}) collective-permute-start(bf16[256,1024]{1,0:T(8,128)(2,1)S(1)} %pad_maximum_fusion.refs_0_.refs_8_.refs_16_.refs_24_.refs_32_.refs_40_.refs_48_.refs_56_), channel_id=1, source_target_pairs={{0,64},{1,65},{2,66},{3,67},{4,68},{5,69},{6,70},{7,71},{8,24},{9,... | collective-permute-start | bytes 1572872 | tf_op jit(solution)/shard_map/ppermute | solution.py:46
  14.7 0.4 collective-permute-start.4
  15.1 2.3 %collective-permute-start.5 = (bf16[256,1024]{1,0:T(8,128)(2,1)S(1)}, bf16[256,1024]{1,0:T(8,128)(2,1)S(1)}, u32[]{:S(2)}, u32[]{:S(2)}) collective-permute-start(bf16[256,1024]{1,0:T(8,128)(2,1)S(1)} %pad_maximum_fusion.refs_0_.refs_8_.refs_16_.refs_24_.refs_32_.refs_40_.refs_48_.refs_56_), channel_id=1, source_target_pairs={{0,128},{1,129},{2,130},{3,131},{4,132},{5,133},{6,134},{7,135},{8... | collective-permute-start | bytes 1572872 | tf_op jit(solution)/shard_map/ppermute | solution.py:46
  17.5 1.6 %collective-permute-start.14 = (bf16[256,1024]{1,0:T(8,128)(2,1)S(1)}, bf16[256,1024]{1,0:T(8,128)(2,1)S(1)}, u32[]{:S(2)}, u32[]{:S(2)}) collective-permute-start(bf16[256,1024]{1,0:T(8,128)(2,1)S(1)} %pad_maximum_fusion.1.refs_0_.refs_8_.refs_16_.refs_24_.refs_32_.refs_40_), channel_id=1, source_target_pairs={{0,64},{1,65},{2,66},{3,67},{4,68},{5,69},{6,70},{7,71},{8,24},{9,... | collective-permute-start | bytes 1572872 | tf_op jit(solution)/shard_map/ppermute | solution.py:46
  19.2 3.1 %collective-permute-done.3.refs_1_.refs_9_.refs_17_.refs_25_.refs_33_.refs_41_.refs_49_.refs_57_ = bf16[256,1024]{1,0:T(8,128)(2,1)S(1)} collective-permute-done((bf16[256,1024]{1,0:T(8,128)(2,1)S(1)}, bf16[256,1024]{1,0:T(8,128)(2,1)S(1)}, u32[]{:S(2)}, u32[]{:S(2)}) %collective-permute-start.3) | collective-permute-done | bytes 524320 | tf_op jit(solution)/shard_map/ppermute | solution.py:46
  22.3 2.3 %collective-permute-start.15 = (bf16[256,1024]{1,0:T(8,128)(2,1)S(1)}, bf16[256,1024]{1,0:T(8,128)(2,1)S(1)}, u32[]{:S(2)}, u32[]{:S(2)}) collective-permute-start(bf16[256,1024]{1,0:T(8,128)(2,1)S(1)} %pad_maximum_fusion.1.refs_0_.refs_8_.refs_16_.refs_24_.refs_32_.refs_40_), channel_id=1, source_target_pairs={{0,192},{1,193},{2,194},{3,195},{4,196},{5,197},{6,198},{7,199},{8... | collective-permute-start | bytes 1572872 | tf_op jit(solution)/shard_map/ppermute | solution.py:46
  24.6 7.7 %collective-permute-start.16 = (bf16[256,1024]{1,0:T(8,128)(2,1)S(1)}, bf16[256,1024]{1,0:T(8,128)(2,1)S(1)}, u32[]{:S(2)}, u32[]{:S(2)}) collective-permute-start(bf16[256,1024]{1,0:T(8,128)(2,1)S(1)} %pad_maximum_fusion.1.refs_0_.refs_8_.refs_16_.refs_24_.refs_32_.refs_40_), channel_id=1, source_target_pairs={{0,128},{1,129},{2,130},{3,131},{4,132},{5,133},{6,134},{7,135},{8... | collective-permute-start | bytes 1572872 | tf_op jit(solution)/shard_map/ppermute | solution.py:46
  32.3 0.5 collective-permute-start.8
  32.8 0.8 collective-permute-done.14.refs_1_.refs_9_.refs_17_.refs_25_.refs_33_.refs_41_
  33.7 9.3 %shard_map.100.energy_ref = bf16[8,2,64,2048]{3,2,1,0:T(8,128)(2,1)S(1)} custom-call(s32[32]{0:T(128)S(1)} %pad_add_fusion.1.slots, s32[2]{0:T(128)S(1)} %pad_add_fusion.2.times, bf16[8,32,64,128]{3,2,1,0:T(8,128)(2,1)} %ret_ref.1, bf16[32,8,64,128]{3,2,1,0:T(8,128)(2,1)} %mir_ref.1), custom_call_target="tpu_custom_call" | custom-call | flops 41943040 | bytes 12582912 | tf_op jit(solution)/shard_map/pallas_call | solution.py:83
  43.0 0.6 collective-permute-start.17
  43.6 0.2 collective-permute-done.16.refs_3_.refs_11_.refs_19_.refs_27_.refs_35_.refs_43_
  43.7 0.5 collective-permute-start.19
  44.3 0.3 collective-permute-start.20
  44.5 5.9 %shard_map.101 = (bf16[3,8,64,128]{3,2,1,0:T(8,128)(2,1)S(1)}, bf16[2,8,64,128]{3,2,1,0:T(8,128)(2,1)S(1)}, f32[1,8,64,128]{3,2,1,0:T(8,128)S(1)}, f32[2,8,64,128]{3,2,1,0:T(8,128)S(1)}) custom-call(s32[8]{0:T(128)S(1)} %and_select_fusion.6.cols_ref, bf16[8,2,64,2048]{3,2,1,0:T(8,128)(2,1)S(1)} %shard_map.100.energy_ref, ...), custom_call_target="tpu_custom_call" | custom-call | flops 4294967296 | bytes 8388608 | tf_op jit(solution)/shard_map/pallas_call | solution.py:143
  50.5 2.0 %collective-permute-start.10 = (bf16[3,8,64,128]{3,2,1,0:T(8,128)(2,1)S(1)}, bf16[3,8,64,128]{3,2,1,0:T(8,128)(2,1)S(1)}, u32[]{:S(2)}, u32[]{:S(2)}) collective-permute-start(bf16[3,8,64,128]{3,2,1,0:T(8,128)(2,1)S(1)} %get-tuple-element.19), channel_id=1, source_target_pairs={{0,1},{1,2},{2,3},{3,4},{4,5},{5,6},{6,7},{7,0},{8,15},{9,8},{10,9... | collective-permute-start | bytes 1179656 | tf_op jit(solution)/shard_map/ppermute | solution.py:46
  52.5 4.0 %collective-permute-start.11 = (bf16[2,8,64,128]{3,2,1,0:T(8,128)(2,1)S(1)}, bf16[2,8,64,128]{3,2,1,0:T(8,128)(2,1)S(1)}, u32[]{:S(2)}, u32[]{:S(2)}) collective-permute-start(bf16[2,8,64,128]{3,2,1,0:T(8,128)(2,1)S(1)} %get-tuple-element.20), channel_id=1, source_target_pairs={{0,7},{1,0},{2,1},{3,2},{4,3},{5,4},{6,5},{7,6},{8,9},{9,10},{10,1... | collective-permute-start | bytes 786440 | tf_op jit(solution)/shard_map/ppermute | solution.py:46
  56.5 4.6 %shard_map.103 = (bf16[3,8,64,128]{3,2,1,0:T(8,128)(2,1)S(1)}, bf16[2,8,64,128]{3,2,1,0:T(8,128)(2,1)S(1)}, f32[1,8,64,128]{3,2,1,0:T(8,128)S(1)}) custom-call(s32[6]{0:T(128)S(1)} %and_select_fusion.1.cols_ref, bf16[8,2,64,2048]{3,2,1,0:T(8,128)(2,1)S(1)} %shard_map.100.energy_ref, ...), custom_call_target="tpu_custom_call" | custom-call | flops 3221225472 | bytes 7340032 | tf_op jit(solution)/shard_map/pallas_call | solution.py:143
  61.1 0.1 collective-permute-start.21
  61.3 3.2 %collective-permute-start.22 = (bf16[2,8,64,128]{3,2,1,0:T(8,128)(2,1)S(1)}, bf16[2,8,64,128]{3,2,1,0:T(8,128)(2,1)S(1)}, u32[]{:S(2)}, u32[]{:S(2)}) collective-permute-start(bf16[2,8,64,128]{3,2,1,0:T(8,128)(2,1)S(1)} %get-tuple-element.26), channel_id=1, source_target_pairs={{0,7},{1,0},{2,1},{3,2},{4,3},{5,4},{6,5},{7,6},{8,9},{9,10},{10,1... | collective-permute-start | bytes 786440 | tf_op jit(solution)/shard_map/ppermute | solution.py:46
  64.5 2.0 %shard_map.104 = f32[2,8,64,128]{3,2,1,0:T(8,128)S(1)} custom-call(s32[2]{0:T(128)S(1)} %and_select_fusion.cols_ref, bf16[8,2,64,2048]{3,2,1,0:T(8,128)(2,1)S(1)} %shard_map.100.energy_ref, bf16[256,1024]{1,0:T(8,128)(2,1)S(1)} %pad_maximum_fusion.1.refs_0_.refs_8_.refs_16_.refs_24_.refs_32_.refs_40_, ...), custom_call_target="tpu_custom_call" | custom-call | flops 1073741824 | bytes 5242880 | tf_op jit(solution)/shard_map/pallas_call | solution.py:143
  66.6 0.1 fusion.4
  66.7 2.2 %collective-permute-start.12 = (bf16[8,64,128]{2,1,0:T(8,128)(2,1)S(1)}, bf16[8,64,128]{2,1,0:T(8,128)(2,1)S(1)}, u32[]{:S(2)}, u32[]{:S(2)}) collective-permute-start(bf16[8,64,128]{2,1,0:T(8,128)(2,1)S(1)} %get-tuple-element.34), channel_id=1, source_target_pairs={{0,5},{1,6},{2,7},{3,0},{4,1},{5,2},{6,3},{7,4},{8,11},{9,12},{10,... | collective-permute-start | bytes 393224 | tf_op jit(solution)/shard_map/ppermute | solution.py:46
  68.8 1.7 %collective-permute-start.13 = (bf16[8,64,128]{2,1,0:T(8,128)(2,1)S(1)}, bf16[8,64,128]{2,1,0:T(8,128)(2,1)S(1)}, u32[]{:S(2)}, u32[]{:S(2)}) collective-permute-start(bf16[8,64,128]{2,1,0:T(8,128)(2,1)S(1)} %get-tuple-element.33), channel_id=1, source_target_pairs={{0,3},{1,4},{2,5},{3,6},{4,7},{5,0},{6,1},{7,2},{8,13},{9,14},{10,... | collective-permute-start | bytes 393224 | tf_op jit(solution)/shard_map/ppermute | solution.py:46
  70.6 2.2 %collective-permute-done.22.refs_2_ = bf16[2,8,64,128]{3,2,1,0:T(8,128)(2,1)S(1)} collective-permute-done((bf16[2,8,64,128]{3,2,1,0:T(8,128)(2,1)S(1)}, bf16[2,8,64,128]{3,2,1,0:T(8,128)(2,1)S(1)}, u32[]{:S(2)}, u32[]{:S(2)}) %collective-permute-start.22) | collective-permute-done | bytes 262176 | tf_op jit(solution)/shard_map/ppermute | solution.py:46
  72.8 1.7 %collective-permute-done.21.refs_1_ = bf16[3,8,64,128]{3,2,1,0:T(8,128)(2,1)S(1)} collective-permute-done((bf16[3,8,64,128]{3,2,1,0:T(8,128)(2,1)S(1)}, bf16[3,8,64,128]{3,2,1,0:T(8,128)(2,1)S(1)}, u32[]{:S(2)}, u32[]{:S(2)}) %collective-permute-start.21) | collective-permute-done | bytes 393248 | tf_op jit(solution)/shard_map/ppermute | solution.py:46
  74.5 0.1 fusion.6
  74.6 4.1 %collective-permute-start.23 = (bf16[8,64,128]{2,1,0:T(8,128)(2,1)S(1)}, bf16[8,64,128]{2,1,0:T(8,128)(2,1)S(1)}, u32[]{:S(2)}, u32[]{:S(2)}) collective-permute-start(bf16[8,64,128]{2,1,0:T(8,128)(2,1)S(1)} %get-tuple-element.32), channel_id=1, source_target_pairs={{0,5},{1,6},{2,7},{3,0},{4,1},{5,2},{6,3},{7,4},{8,11},{9,12},{10,... | collective-permute-start | bytes 393224 | tf_op jit(solution)/shard_map/ppermute | solution.py:46
  78.7 4.4 %collective-permute-start.24 = (bf16[8,64,128]{2,1,0:T(8,128)(2,1)S(1)}, bf16[8,64,128]{2,1,0:T(8,128)(2,1)S(1)}, u32[]{:S(2)}, u32[]{:S(2)}) collective-permute-start(bf16[8,64,128]{2,1,0:T(8,128)(2,1)S(1)} %get-tuple-element.31), channel_id=1, source_target_pairs={{0,3},{1,4},{2,5},{3,6},{4,7},{5,0},{6,1},{7,2},{8,13},{9,14},{10,... | collective-permute-start | bytes 393224 | tf_op jit(solution)/shard_map/ppermute | solution.py:46
  83.1 0.1 broadcast_multiply_fusion.fim_ref
  83.2 0.1 broadcast_in_dim.12.fre_ref
  83.3 0.6 shard_map.102
  83.9 6.5 %collective-permute-done.23.refs_3_ = bf16[8,64,128]{2,1,0:T(8,128)(2,1)S(1)} collective-permute-done((bf16[8,64,128]{2,1,0:T(8,128)(2,1)S(1)}, bf16[8,64,128]{2,1,0:T(8,128)(2,1)S(1)}, u32[]{:S(2)}, u32[]{:S(2)}) %collective-permute-start.23) | collective-permute-done | bytes 131104 | tf_op jit(solution)/shard_map/ppermute | solution.py:46
  90.5 0.6 shard_map.105
  91.1 0.1 collective-permute-start.25
  91.3 1.2 %collective-permute-done.25.other_ref.core_ref = f32[3,64,128]{2,1,0:T(8,128)S(1)} collective-permute-done((f32[3,64,128]{2,1,0:T(8,128)S(1)}, f32[3,64,128]{2,1,0:T(8,128)S(1)}, u32[]{:S(2)}, u32[]{:S(2)}) %collective-permute-start.25) | collective-permute-done | bytes 98336 | tf_op jit(solution)/shard_map/ppermute | solution.py:46
  92.5 0.6 shard_map.106.own_ref
  93.1 0.6 collective-permute-start.26
  93.7 2.7 %collective-permute-start.27 = (f32[3,64,128]{2,1,0:T(8,128)S(1)}, f32[3,64,128]{2,1,0:T(8,128)S(1)}, u32[]{:S(2)}, u32[]{:S(2)}) collective-permute-start(f32[3,64,128]{2,1,0:T(8,128)S(1)} %shard_map.106.own_ref), channel_id=1, source_target_pairs={{0,32},{1,33},{2,34},{3,35},{4,36},{5,37},{6,38},{7,39},{8,40},{9,... | collective-permute-start | bytes 294920 | tf_op jit(solution)/shard_map/ppermute | solution.py:46
  96.4 1.4 %collective-permute-start.28 = (f32[3,64,128]{2,1,0:T(8,128)S(1)}, f32[3,64,128]{2,1,0:T(8,128)S(1)}, u32[]{:S(2)}, u32[]{:S(2)}) collective-permute-start(f32[3,64,128]{2,1,0:T(8,128)S(1)} %shard_map.106.own_ref), channel_id=1, source_target_pairs={{0,48},{1,49},{2,50},{3,51},{4,52},{5,53},{6,54},{7,55},{8,56},{9,... | collective-permute-start | bytes 294920 | tf_op jit(solution)/shard_map/ppermute | solution.py:46
  97.8 2.3 %collective-permute-done.26.d1_ref = f32[3,64,128]{2,1,0:T(8,128)S(1)} collective-permute-done((f32[3,64,128]{2,1,0:T(8,128)S(1)}, f32[3,64,128]{2,1,0:T(8,128)S(1)}, u32[]{:S(2)}, u32[]{:S(2)}) %collective-permute-start.26) | collective-permute-done | bytes 98336 | tf_op jit(solution)/shard_map/ppermute | solution.py:46
  100.1 1.3 %collective-permute-done.27.d2_ref = f32[3,64,128]{2,1,0:T(8,128)S(1)} collective-permute-done((f32[3,64,128]{2,1,0:T(8,128)S(1)}, f32[3,64,128]{2,1,0:T(8,128)S(1)}, u32[]{:S(2)}, u32[]{:S(2)}) %collective-permute-start.27) | collective-permute-done | bytes 98336 | tf_op jit(solution)/shard_map/ppermute | solution.py:46
  101.4 0.6 collective-permute-done.28.d3_ref
  102.0 1.1 shard_map.107
  103.1 1.5 %collective-permute-start.29 = (f32[3,64,128]{2,1,0:T(8,128)S(1)}, f32[3,64,128]{2,1,0:T(8,128)S(1)}, u32[]{:S(2)}, u32[]{:S(2)}) collective-permute-start(f32[3,64,128]{2,1,0:T(8,128)S(1)} %get-tuple-element.29), channel_id=1, source_target_pairs={{0,64},{1,65},{2,66},{3,67},{4,68},{5,69},{6,70},{7,71},{8,72},{9,... | collective-permute-start | bytes 294920 | tf_op jit(solution)/shard_map/ppermute | solution.py:46
  104.6 2.1 %collective-permute-start.30 = (f32[3,64,128]{2,1,0:T(8,128)S(1)}, f32[3,64,128]{2,1,0:T(8,128)S(1)}, u32[]{:S(2)}, u32[]{:S(2)}) collective-permute-start(f32[3,64,128]{2,1,0:T(8,128)S(1)} %get-tuple-element.29), channel_id=1, source_target_pairs={{0,128},{1,129},{2,130},{3,131},{4,132},{5,133},{6,134},{7,135},{8... | collective-permute-start | bytes 294920 | tf_op jit(solution)/shard_map/ppermute | solution.py:46
  106.7 1.3 %collective-permute-start.31 = (f32[3,64,128]{2,1,0:T(8,128)S(1)}, f32[3,64,128]{2,1,0:T(8,128)S(1)}, u32[]{:S(2)}, u32[]{:S(2)}) collective-permute-start(f32[3,64,128]{2,1,0:T(8,128)S(1)} %get-tuple-element.29), channel_id=1, source_target_pairs={{0,192},{1,193},{2,194},{3,195},{4,196},{5,197},{6,198},{7,199},{8... | collective-permute-start | bytes 294920 | tf_op jit(solution)/shard_map/ppermute | solution.py:46
  108.0 0.3 collective-permute-done.29.d1_ref
  108.3 2.5 %collective-permute-done.30.d2_ref = f32[3,64,128]{2,1,0:T(8,128)S(1)} collective-permute-done((f32[3,64,128]{2,1,0:T(8,128)S(1)}, f32[3,64,128]{2,1,0:T(8,128)S(1)}, u32[]{:S(2)}, u32[]{:S(2)}) %collective-permute-start.30) | collective-permute-done | bytes 98336 | tf_op jit(solution)/shard_map/ppermute | solution.py:46
  110.7 1.0 collective-permute-done.31.d3_ref
  111.7 2.4 %shard_map.108 = f32[8,64,2,128]{3,2,1,0:T(2,128)} custom-call(s32[3]{0:T(128)S(1)} %pad_add_fusion.where_ref, f32[8,64,128]{2,1,0:T(8,128)S(1)} %broadcast_in_dim.12.fre_ref, f32[8,64,128]{2,1,0:T(8,128)S(1)} %broadcast_multiply_fusion.fim_ref, f32[8,64,128]{2,1,0:T(8,128)S(1)} %get-tuple-element.22.sum0_ref, f32[8,64,128]{2,1,0:T(8,128)S(1)} %get-tuple-element.27.sum1_ref, ...), custom_call_target="tpu_custom_call" | custom-call | flops 1000000 | bytes 1048576 | tf_op jit(solution)/shard_map/pallas_call | solution.py:306
  (51 shorter events, 0.6 us)
Async XLA Ops:
  0.0 17.4 %copy-start.4 = (s32[8]{0:T(128)S(1)}, s32[8]{0:T(128)}, u32[]{:S(2)}) copy-start(s32[8]{0:T(128)} %constant.134.clone) | copy-start | bytes 100
  0.0 32.8 %copy-start.3 = (s32[6]{0:T(128)S(1)}, s32[6]{0:T(128)}, u32[]{:S(2)}) copy-start(s32[6]{0:T(128)} %constant.135.clone) | copy-start | bytes 76
  0.0 19.2 %copy-start.5 = (f32[64]{0:T(128)S(1)}, f32[64]{0:T(128)}, u32[]{:S(2)}) copy-start(f32[64]{0:T(128)} %param.15) | copy-start | bytes 772
  1.1 8.0 %collective-permute-start.2 = (bf16[2,64,1024]{2,1,0:T(8,128)(2,1)S(1)}, bf16[2,64,1024]{2,1,0:T(8,128)(2,1)S(1)}, u32[]{:S(2)}, u32[]{:S(2)}) collective-permute-start(bf16[2,64,1024]{2,1,0:T(8,128)(2,1)S(1)} %reshape.54), channel_id=1, source_target_pairs={{0,32},{1,33},{2,34},{3,35},{4,36},{5,37},{6,38},{7,39},{8,136},{9... | collective-permute-start | bytes 786440 | tf_op jit(solution)/shard_map/ppermute | solution.py:46
  4.3 7.8 %collective-permute-start.1 = (bf16[2,64,1024]{2,1,0:T(8,128)(2,1)S(1)}, bf16[2,64,1024]{2,1,0:T(8,128)(2,1)S(1)}, u32[]{:S(2)}, u32[]{:S(2)}) collective-permute-start(bf16[2,64,1024]{2,1,0:T(8,128)(2,1)S(1)} %reshape.54), channel_id=1, source_target_pairs={{0,48},{1,49},{2,50},{3,51},{4,52},{5,53},{6,54},{7,55},{8,200},{9... | collective-permute-start | bytes 786440 | tf_op jit(solution)/shard_map/ppermute | solution.py:46
  5.4 7.6 %collective-permute-start = (bf16[2,64,1024]{2,1,0:T(8,128)(2,1)S(1)}, bf16[2,64,1024]{2,1,0:T(8,128)(2,1)S(1)}, u32[]{:S(2)}, u32[]{:S(2)}) collective-permute-start(bf16[2,64,1024]{2,1,0:T(8,128)(2,1)S(1)} %reshape.54), channel_id=1, source_target_pairs={{0,16},{1,17},{2,18},{3,19},{4,20},{5,21},{6,22},{7,23},{8,72},{9,... | collective-permute-start | bytes 786440 | tf_op jit(solution)/shard_map/ppermute | solution.py:46
  13.0 9.3 %collective-permute-start.3 = (bf16[256,1024]{1,0:T(8,128)(2,1)S(1)}, bf16[256,1024]{1,0:T(8,128)(2,1)S(1)}, u32[]{:S(2)}, u32[]{:S(2)}) collective-permute-start(bf16[256,1024]{1,0:T(8,128)(2,1)S(1)} %pad_maximum_fusion.refs_0_.refs_8_.refs_16_.refs_24_.refs_32_.refs_40_.refs_48_.refs_56_), channel_id=1, source_target_pairs={{0,64},{1,65},{2,66},{3,67},{4,68},{5,69},{6,70},{7,71},{8,24},{9,... | collective-permute-start | bytes 1572872 | tf_op jit(solution)/shard_map/ppermute | solution.py:46
  14.7 9.9 %collective-permute-start.4 = (bf16[256,1024]{1,0:T(8,128)(2,1)S(1)}, bf16[256,1024]{1,0:T(8,128)(2,1)S(1)}, u32[]{:S(2)}, u32[]{:S(2)}) collective-permute-start(bf16[256,1024]{1,0:T(8,128)(2,1)S(1)} %pad_maximum_fusion.refs_0_.refs_8_.refs_16_.refs_24_.refs_32_.refs_40_.refs_48_.refs_56_), channel_id=1, source_target_pairs={{0,192},{1,193},{2,194},{3,195},{4,196},{5,197},{6,198},{7,199},{8... | collective-permute-start | bytes 1572872 | tf_op jit(solution)/shard_map/ppermute | solution.py:46
  15.1 17.1 %collective-permute-start.5 = (bf16[256,1024]{1,0:T(8,128)(2,1)S(1)}, bf16[256,1024]{1,0:T(8,128)(2,1)S(1)}, u32[]{:S(2)}, u32[]{:S(2)}) collective-permute-start(bf16[256,1024]{1,0:T(8,128)(2,1)S(1)} %pad_maximum_fusion.refs_0_.refs_8_.refs_16_.refs_24_.refs_32_.refs_40_.refs_48_.refs_56_), channel_id=1, source_target_pairs={{0,128},{1,129},{2,130},{3,131},{4,132},{5,133},{6,134},{7,135},{8... | collective-permute-start | bytes 1572872 | tf_op jit(solution)/shard_map/ppermute | solution.py:46
  17.4 14.9 %collective-permute-start.6 = (bf16[256,1024]{1,0:T(8,128)(2,1)S(1)}, bf16[256,1024]{1,0:T(8,128)(2,1)S(1)}, u32[]{:S(2)}, u32[]{:S(2)}) collective-permute-start(bf16[256,1024]{1,0:T(8,128)(2,1)S(1)} %pad_maximum_fusion.refs_0_.refs_8_.refs_16_.refs_24_.refs_32_.refs_40_.refs_48_.refs_56_), channel_id=1, source_target_pairs={{0,8},{1,9},{2,10},{3,11},{4,12},{5,13},{6,14},{7,15},{8,0},{9,1},... | collective-permute-start | bytes 1572872 | tf_op jit(solution)/shard_map/ppermute | solution.py:46
  17.5 16.1 %collective-permute-start.14 = (bf16[256,1024]{1,0:T(8,128)(2,1)S(1)}, bf16[256,1024]{1,0:T(8,128)(2,1)S(1)}, u32[]{:S(2)}, u32[]{:S(2)}) collective-permute-start(bf16[256,1024]{1,0:T(8,128)(2,1)S(1)} %pad_maximum_fusion.1.refs_0_.refs_8_.refs_16_.refs_24_.refs_32_.refs_40_), channel_id=1, source_target_pairs={{0,64},{1,65},{2,66},{3,67},{4,68},{5,69},{6,70},{7,71},{8,24},{9,... | collective-permute-start | bytes 1572872 | tf_op jit(solution)/shard_map/ppermute | solution.py:46
  22.3 20.7 %collective-permute-start.15 = (bf16[256,1024]{1,0:T(8,128)(2,1)S(1)}, bf16[256,1024]{1,0:T(8,128)(2,1)S(1)}, u32[]{:S(2)}, u32[]{:S(2)}) collective-permute-start(bf16[256,1024]{1,0:T(8,128)(2,1)S(1)} %pad_maximum_fusion.1.refs_0_.refs_8_.refs_16_.refs_24_.refs_32_.refs_40_), channel_id=1, source_target_pairs={{0,192},{1,193},{2,194},{3,195},{4,196},{5,197},{6,198},{7,199},{8... | collective-permute-start | bytes 1572872 | tf_op jit(solution)/shard_map/ppermute | solution.py:46
  24.6 19.1 %collective-permute-start.16 = (bf16[256,1024]{1,0:T(8,128)(2,1)S(1)}, bf16[256,1024]{1,0:T(8,128)(2,1)S(1)}, u32[]{:S(2)}, u32[]{:S(2)}) collective-permute-start(bf16[256,1024]{1,0:T(8,128)(2,1)S(1)} %pad_maximum_fusion.1.refs_0_.refs_8_.refs_16_.refs_24_.refs_32_.refs_40_), channel_id=1, source_target_pairs={{0,128},{1,129},{2,130},{3,131},{4,132},{5,133},{6,134},{7,135},{8... | collective-permute-start | bytes 1572872 | tf_op jit(solution)/shard_map/ppermute | solution.py:46
  32.3 11.4 %collective-permute-start.7 = (bf16[256,1024]{1,0:T(8,128)(2,1)S(1)}, bf16[256,1024]{1,0:T(8,128)(2,1)S(1)}, u32[]{:S(2)}, u32[]{:S(2)}) collective-permute-start(bf16[256,1024]{1,0:T(8,128)(2,1)S(1)} %collective-permute-done.3.refs_1_.refs_9_.refs_17_.refs_25_.refs_33_.refs_41_.refs_49_.refs_57_), channel_id=1, source_target_pairs={{0,8},{1,9},{2,10},{3,11},{4,12},{5,13},{6,14},{7,15},{8,0},{9,1},... | collective-permute-start | bytes 1572872 | tf_op jit(solution)/shard_map/ppermute | solution.py:46
  32.3 11.9 %collective-permute-start.8 = (bf16[256,1024]{1,0:T(8,128)(2,1)S(1)}, bf16[256,1024]{1,0:T(8,128)(2,1)S(1)}, u32[]{:S(2)}, u32[]{:S(2)}) collective-permute-start(bf16[256,1024]{1,0:T(8,128)(2,1)S(1)} %collective-permute-done.4.refs_2_.refs_10_.refs_18_.refs_26_.refs_34_.refs_42_.refs_50_.refs_58_), channel_id=1, source_target_pairs={{0,8},{1,9},{2,10},{3,11},{4,12},{5,13},{6,14},{7,15},{8,0},{9,1},... | collective-permute-start | bytes 1572872 | tf_op jit(solution)/shard_map/ppermute | solution.py:46
  33.6 11.0 %collective-permute-start.9 = (bf16[256,1024]{1,0:T(8,128)(2,1)S(1)}, bf16[256,1024]{1,0:T(8,128)(2,1)S(1)}, u32[]{:S(2)}, u32[]{:S(2)}) collective-permute-start(bf16[256,1024]{1,0:T(8,128)(2,1)S(1)} %collective-permute-done.5.refs_3_.refs_11_.refs_19_.refs_27_.refs_35_.refs_43_.refs_51_.refs_59_), channel_id=1, source_target_pairs={{0,8},{1,9},{2,10},{3,11},{4,12},{5,13},{6,14},{7,15},{8,0},{9,1},... | collective-permute-start | bytes 1572872 | tf_op jit(solution)/shard_map/ppermute | solution.py:46
  33.7 9.3 %copy-start.1 = (f32[8,64]{1,0:T(8,128)S(1)}, f32[8,64]{1,0:T(8,128)}, u32[]{:S(2)}) copy-start(f32[8,64]{1,0:T(8,128)} %param.14) | copy-start | bytes 6148
  33.7 10.9 %copy-start.2 = (s32[2]{0:T(128)S(1)}, s32[2]{0:T(128)}, u32[]{:S(2)}) copy-start(s32[2]{0:T(128)} %constant.136.clone) | copy-start | bytes 28
  43.0 9.5 %collective-permute-start.17 = (bf16[256,1024]{1,0:T(8,128)(2,1)S(1)}, bf16[256,1024]{1,0:T(8,128)(2,1)S(1)}, u32[]{:S(2)}, u32[]{:S(2)}) collective-permute-start(bf16[256,1024]{1,0:T(8,128)(2,1)S(1)} %pad_maximum_fusion.1.refs_0_.refs_8_.refs_16_.refs_24_.refs_32_.refs_40_), channel_id=1, source_target_pairs={{0,8},{1,9},{2,10},{3,11},{4,12},{5,13},{6,14},{7,15},{8,0},{9,1},... | collective-permute-start | bytes 1572872 | tf_op jit(solution)/shard_map/ppermute | solution.py:46
  43.7 12.8 %collective-permute-start.18 = (bf16[256,1024]{1,0:T(8,128)(2,1)S(1)}, bf16[256,1024]{1,0:T(8,128)(2,1)S(1)}, u32[]{:S(2)}, u32[]{:S(2)}) collective-permute-start(bf16[256,1024]{1,0:T(8,128)(2,1)S(1)} %collective-permute-done.14.refs_1_.refs_9_.refs_17_.refs_25_.refs_33_.refs_41_), channel_id=1, source_target_pairs={{0,8},{1,9},{2,10},{3,11},{4,12},{5,13},{6,14},{7,15},{8,0},{9,1},... | collective-permute-start | bytes 1572872 | tf_op jit(solution)/shard_map/ppermute | solution.py:46
  43.7 12.8 %collective-permute-start.19 = (bf16[256,1024]{1,0:T(8,128)(2,1)S(1)}, bf16[256,1024]{1,0:T(8,128)(2,1)S(1)}, u32[]{:S(2)}, u32[]{:S(2)}) collective-permute-start(bf16[256,1024]{1,0:T(8,128)(2,1)S(1)} %collective-permute-done.15.refs_2_.refs_10_.refs_18_.refs_26_.refs_34_.refs_42_), channel_id=1, source_target_pairs={{0,8},{1,9},{2,10},{3,11},{4,12},{5,13},{6,14},{7,15},{8,0},{9,1},... | collective-permute-start | bytes 1572872 | tf_op jit(solution)/shard_map/ppermute | solution.py:46
  44.3 12.2 %collective-permute-start.20 = (bf16[256,1024]{1,0:T(8,128)(2,1)S(1)}, bf16[256,1024]{1,0:T(8,128)(2,1)S(1)}, u32[]{:S(2)}, u32[]{:S(2)}) collective-permute-start(bf16[256,1024]{1,0:T(8,128)(2,1)S(1)} %collective-permute-done.16.refs_3_.refs_11_.refs_19_.refs_27_.refs_35_.refs_43_), channel_id=1, source_target_pairs={{0,8},{1,9},{2,10},{3,11},{4,12},{5,13},{6,14},{7,15},{8,0},{9,1},... | collective-permute-start | bytes 1572872 | tf_op jit(solution)/shard_map/ppermute | solution.py:46
  50.5 16.1 %collective-permute-start.10 = (bf16[3,8,64,128]{3,2,1,0:T(8,128)(2,1)S(1)}, bf16[3,8,64,128]{3,2,1,0:T(8,128)(2,1)S(1)}, u32[]{:S(2)}, u32[]{:S(2)}) collective-permute-start(bf16[3,8,64,128]{3,2,1,0:T(8,128)(2,1)S(1)} %get-tuple-element.19), channel_id=1, source_target_pairs={{0,1},{1,2},{2,3},{3,4},{4,5},{5,6},{6,7},{7,0},{8,15},{9,8},{10,9... | collective-permute-start | bytes 1179656 | tf_op jit(solution)/shard_map/ppermute | solution.py:46
  52.5 14.1 %collective-permute-start.11 = (bf16[2,8,64,128]{3,2,1,0:T(8,128)(2,1)S(1)}, bf16[2,8,64,128]{3,2,1,0:T(8,128)(2,1)S(1)}, u32[]{:S(2)}, u32[]{:S(2)}) collective-permute-start(bf16[2,8,64,128]{3,2,1,0:T(8,128)(2,1)S(1)} %get-tuple-element.20), channel_id=1, source_target_pairs={{0,7},{1,0},{2,1},{3,2},{4,3},{5,4},{6,5},{7,6},{8,9},{9,10},{10,1... | collective-permute-start | bytes 786440 | tf_op jit(solution)/shard_map/ppermute | solution.py:46
  61.1 13.3 %collective-permute-start.21 = (bf16[3,8,64,128]{3,2,1,0:T(8,128)(2,1)S(1)}, bf16[3,8,64,128]{3,2,1,0:T(8,128)(2,1)S(1)}, u32[]{:S(2)}, u32[]{:S(2)}) collective-permute-start(bf16[3,8,64,128]{3,2,1,0:T(8,128)(2,1)S(1)} %get-tuple-element.25), channel_id=1, source_target_pairs={{0,1},{1,2},{2,3},{3,4},{4,5},{5,6},{6,7},{7,0},{8,15},{9,8},{10,9... | collective-permute-start | bytes 1179656 | tf_op jit(solution)/shard_map/ppermute | solution.py:46
  61.3 11.5 %collective-permute-start.22 = (bf16[2,8,64,128]{3,2,1,0:T(8,128)(2,1)S(1)}, bf16[2,8,64,128]{3,2,1,0:T(8,128)(2,1)S(1)}, u32[]{:S(2)}, u32[]{:S(2)}) collective-permute-start(bf16[2,8,64,128]{3,2,1,0:T(8,128)(2,1)S(1)} %get-tuple-element.26), channel_id=1, source_target_pairs={{0,7},{1,0},{2,1},{3,2},{4,3},{5,4},{6,5},{7,6},{8,9},{9,10},{10,1... | collective-permute-start | bytes 786440 | tf_op jit(solution)/shard_map/ppermute | solution.py:46
  66.5 41.4 %copy-start = (f32[64,2,128]{2,1,0:T(2,128)S(1)}, f32[64,2,128]{2,1,0:T(2,128)}, u32[]{:S(2)}) copy-start(f32[64,2,128]{2,1,0:T(2,128)} %param.13) | copy-start | bytes 196612
  66.7 16.5 %collective-permute-start.12 = (bf16[8,64,128]{2,1,0:T(8,128)(2,1)S(1)}, bf16[8,64,128]{2,1,0:T(8,128)(2,1)S(1)}, u32[]{:S(2)}, u32[]{:S(2)}) collective-permute-start(bf16[8,64,128]{2,1,0:T(8,128)(2,1)S(1)} %get-tuple-element.34), channel_id=1, source_target_pairs={{0,5},{1,6},{2,7},{3,0},{4,1},{5,2},{6,3},{7,4},{8,11},{9,12},{10,... | collective-permute-start | bytes 393224 | tf_op jit(solution)/shard_map/ppermute | solution.py:46
  68.8 14.4 %collective-permute-start.13 = (bf16[8,64,128]{2,1,0:T(8,128)(2,1)S(1)}, bf16[8,64,128]{2,1,0:T(8,128)(2,1)S(1)}, u32[]{:S(2)}, u32[]{:S(2)}) collective-permute-start(bf16[8,64,128]{2,1,0:T(8,128)(2,1)S(1)} %get-tuple-element.33), channel_id=1, source_target_pairs={{0,3},{1,4},{2,5},{3,6},{4,7},{5,0},{6,1},{7,2},{8,13},{9,14},{10,... | collective-permute-start | bytes 393224 | tf_op jit(solution)/shard_map/ppermute | solution.py:46
  74.6 15.9 %collective-permute-start.23 = (bf16[8,64,128]{2,1,0:T(8,128)(2,1)S(1)}, bf16[8,64,128]{2,1,0:T(8,128)(2,1)S(1)}, u32[]{:S(2)}, u32[]{:S(2)}) collective-permute-start(bf16[8,64,128]{2,1,0:T(8,128)(2,1)S(1)} %get-tuple-element.32), channel_id=1, source_target_pairs={{0,5},{1,6},{2,7},{3,0},{4,1},{5,2},{6,3},{7,4},{8,11},{9,12},{10,... | collective-permute-start | bytes 393224 | tf_op jit(solution)/shard_map/ppermute | solution.py:46
  78.7 11.8 %collective-permute-start.24 = (bf16[8,64,128]{2,1,0:T(8,128)(2,1)S(1)}, bf16[8,64,128]{2,1,0:T(8,128)(2,1)S(1)}, u32[]{:S(2)}, u32[]{:S(2)}) collective-permute-start(bf16[8,64,128]{2,1,0:T(8,128)(2,1)S(1)} %get-tuple-element.31), channel_id=1, source_target_pairs={{0,3},{1,4},{2,5},{3,6},{4,7},{5,0},{6,1},{7,2},{8,13},{9,14},{10,... | collective-permute-start | bytes 393224 | tf_op jit(solution)/shard_map/ppermute | solution.py:46
  91.1 1.4 %collective-permute-start.25 = (f32[3,64,128]{2,1,0:T(8,128)S(1)}, f32[3,64,128]{2,1,0:T(8,128)S(1)}, u32[]{:S(2)}, u32[]{:S(2)}) collective-permute-start(f32[3,64,128]{2,1,0:T(8,128)S(1)} %get-tuple-element.28.own_ref), channel_id=1, source_target_pairs={{0,8},{1,9},{2,10},{3,11},{4,12},{5,13},{6,14},{7,15},{8,0},{9,1},... | collective-permute-start | bytes 294920 | tf_op jit(solution)/shard_map/ppermute | solution.py:46
  93.1 7.0 %collective-permute-start.26 = (f32[3,64,128]{2,1,0:T(8,128)S(1)}, f32[3,64,128]{2,1,0:T(8,128)S(1)}, u32[]{:S(2)}, u32[]{:S(2)}) collective-permute-start(f32[3,64,128]{2,1,0:T(8,128)S(1)} %shard_map.106.own_ref), channel_id=1, source_target_pairs={{0,16},{1,17},{2,18},{3,19},{4,20},{5,21},{6,22},{7,23},{8,24},{9,... | collective-permute-start | bytes 294920 | tf_op jit(solution)/shard_map/ppermute | solution.py:46
  93.7 7.7 %collective-permute-start.27 = (f32[3,64,128]{2,1,0:T(8,128)S(1)}, f32[3,64,128]{2,1,0:T(8,128)S(1)}, u32[]{:S(2)}, u32[]{:S(2)}) collective-permute-start(f32[3,64,128]{2,1,0:T(8,128)S(1)} %shard_map.106.own_ref), channel_id=1, source_target_pairs={{0,32},{1,33},{2,34},{3,35},{4,36},{5,37},{6,38},{7,39},{8,40},{9,... | collective-permute-start | bytes 294920 | tf_op jit(solution)/shard_map/ppermute | solution.py:46
  96.4 5.5 %collective-permute-start.28 = (f32[3,64,128]{2,1,0:T(8,128)S(1)}, f32[3,64,128]{2,1,0:T(8,128)S(1)}, u32[]{:S(2)}, u32[]{:S(2)}) collective-permute-start(f32[3,64,128]{2,1,0:T(8,128)S(1)} %shard_map.106.own_ref), channel_id=1, source_target_pairs={{0,48},{1,49},{2,50},{3,51},{4,52},{5,53},{6,54},{7,55},{8,56},{9,... | collective-permute-start | bytes 294920 | tf_op jit(solution)/shard_map/ppermute | solution.py:46
  103.1 5.2 %collective-permute-start.29 = (f32[3,64,128]{2,1,0:T(8,128)S(1)}, f32[3,64,128]{2,1,0:T(8,128)S(1)}, u32[]{:S(2)}, u32[]{:S(2)}) collective-permute-start(f32[3,64,128]{2,1,0:T(8,128)S(1)} %get-tuple-element.29), channel_id=1, source_target_pairs={{0,64},{1,65},{2,66},{3,67},{4,68},{5,69},{6,70},{7,71},{8,72},{9,... | collective-permute-start | bytes 294920 | tf_op jit(solution)/shard_map/ppermute | solution.py:46
  104.6 6.2 %collective-permute-start.30 = (f32[3,64,128]{2,1,0:T(8,128)S(1)}, f32[3,64,128]{2,1,0:T(8,128)S(1)}, u32[]{:S(2)}, u32[]{:S(2)}) collective-permute-start(f32[3,64,128]{2,1,0:T(8,128)S(1)} %get-tuple-element.29), channel_id=1, source_target_pairs={{0,128},{1,129},{2,130},{3,131},{4,132},{5,133},{6,134},{7,135},{8... | collective-permute-start | bytes 294920 | tf_op jit(solution)/shard_map/ppermute | solution.py:46
  106.7 5.1 %collective-permute-start.31 = (f32[3,64,128]{2,1,0:T(8,128)S(1)}, f32[3,64,128]{2,1,0:T(8,128)S(1)}, u32[]{:S(2)}, u32[]{:S(2)}) collective-permute-start(f32[3,64,128]{2,1,0:T(8,128)S(1)} %get-tuple-element.29), channel_id=1, source_target_pairs={{0,192},{1,193},{2,194},{3,195},{4,196},{5,197},{6,198},{7,199},{8... | collective-permute-start | bytes 294920 | tf_op jit(solution)/shard_map/ppermute | solution.py:46

commit v2 on v1

--- a/solution.py
+++ b/solution.py
@@ -108,14 +108,30 @@
     )
 
 
-def product_call(norm, cols, energy, panels, kinds):
+def turned(factor_re, factor_im, value):
+    return factor_re * value + factor_im * pltpu.roll(value, value.shape[-1] // 2, value.ndim - 1)
+
+
+def product_call(norm, cols, energy, factors, panels, kinds, even_ends=None):
     steps, _, orbitals, depth = energy.shape
     width = 2 * orbitals
     shape = [jax.ShapeDtypeStruct((count, steps, orbitals, width), kind) for count, kind in kinds]
     places = [(n, at) for n, (count, _) in enumerate(kinds) for at in range(count)]
     pieces, tiles = len(panels), len(places)
-
-    def body(cols_ref, energy_ref, *refs):
+    first = len(shape)
+    if even_ends is None:
+        shape.append(jax.ShapeDtypeStruct((tiles, orbitals, width), jnp.float32))
+        extra = []
+    else:
+        shape += [
+            jax.ShapeDtypeStruct((count, 2, orbitals, width), kind)
+            for count, kind in ((3, jnp.bfloat16), (2, jnp.bfloat16), (3, jnp.float32))
+        ]
+        extra = [even_ends]
+    packed = [(0, 0), (0, 1), (0, 2), (1, 0), (1, 1), (2, 0), (2, 1), (2, 2)]
+
+    def body(cols_ref, energy_ref, fre_ref, fim_ref, *refs):
+        even_refs, refs = refs[: len(extra)], refs[len(extra) :]
         panel_refs, out_refs = refs[: tiles * pieces], refs[tiles * pieces :]
         left = energy_ref[...].reshape(steps * 2 * orbitals, depth)
         right = jnp.concatenate(
@@ -136,6 +152,16 @@
             part_im = both[:, 1, :, tile * width : (tile + 1) * width]
             value = part_re * norm + sign * pltpu.roll(part_im, orbitals, 2)
             out_refs[result][at] = value.astype(kinds[result][1])
+            end = jnp.zeros((orbitals, width), jnp.float32)
+            for t in range(steps):
+                end = turned(fre_ref[t], fim_ref[t], end + value[t])
+            if not extra:
+                out_refs[first][tile] = end
+            else:
+                group, place = packed[tile]
+                target = out_refs[first + group]
+                target[place, 0] = even_refs[0][tile].astype(target.dtype)
+                target[place, 1] = end.astype(target.dtype)
 
     def panel_spec(panel, tile):
         return pl.BlockSpec((panel.shape[0], width), lambda n, cols: (0, cols[tile]))
@@ -146,50 +172,37 @@
         grid_spec=pltpu.PrefetchScalarGridSpec(
             num_scalar_prefetch=1,
             grid=(1,),
-            in_specs=[pl.BlockSpec(memory_space=pltpu.VMEM)]
+            in_specs=[pl.BlockSpec(memory_space=pltpu.VMEM)] * (3 + len(extra))
             + [panel_spec(panel, tile) for tile in range(tiles) for panel in panels],
-            out_specs=[pl.BlockSpec(s.shape, lambda n, cols: (0, 0, 0, 0)) for s in shape],
+            out_specs=[pl.BlockSpec(memory_space=pltpu.VMEM)] * len(shape),
         ),
-        compiler_params=pltpu.CompilerParams(vmem_limit_bytes=32 << 20),
+        compiler_params=pltpu.CompilerParams(vmem_limit_bytes=34 << 20),
         cost_estimate=pl.CostEstimate(
             flops=2 * tiles * steps * 2 * orbitals * depth * width,
             bytes_accessed=2 * depth * (steps * 2 * orbitals + tiles * width),
             transcendentals=0,
         ),
-    )(cols, energy, *(panels * tiles))
-
-
-def turned(factor_re, factor_im, value):
-    return factor_re * value + factor_im * pltpu.roll(value, value.shape[-1] // 2, value.ndim - 1)
-
-
-def end_of(fre_ref, fim_ref, parts, sum_ref):
-    own_ref, ahead_ref, back_ref, from5_ref, from3_ref = parts
-    steps, orbitals, width = sum_ref.shape
-    state = jnp.zeros((orbitals, width), jnp.float32)
-    for t in range(steps):
-        value = own_ref[0, t]
-        for arrived in (ahead_ref[2, t], back_ref[1, t], from5_ref[t], from3_ref[t]):
-            value = value + arrived.astype(jnp.float32)
-        sum_ref[t] = value
-        state = turned(fre_ref[t], fim_ref[t], state + value)
-    return state
-
-
-def even_kernel(fre_ref, fim_ref, *refs):
-    parts, (sum_ref, end_ref) = refs[:-2], refs[-2:]
-    end_ref[...] = end_of(fre_ref, fim_ref, parts, sum_ref)
-
-
-def odd_kernel(fre_ref, fim_ref, even_ref, *refs):
-    parts, (sum_ref, msg_ref) = refs[:-2], refs[-2:]
+    )(cols, energy, *factors, *extra, *(panels * tiles))
+
+
+def sum_kernel(own_ref, ahead_ref, back_ref, from5_ref, from3_ref, sum_ref):
+    value = own_ref[0]
+    for arrived in (ahead_ref[2], back_ref[1], from5_ref[...], from3_ref[...]):
+        value = value + arrived.astype(jnp.float32)
+    sum_ref[...] = value
+
+
+def message_kernel(fre_ref, fim_ref, own_ref, ahead_ref, back_ref, from5_ref, from3_ref, msg_ref):
     steps, orbitals, width = fre_ref.shape
     lane = lax.broadcasted_iota(jnp.int32, (orbitals, width), 1)
     block = jnp.where(lane < width // 2, 1.0, 0.0).astype(jnp.float32)
     for t in range(steps):
         block = turned(fre_ref[t], fim_ref[t], block)
-    msg_ref[0] = even_ref[...]
-    msg_ref[1] = end_of(fre_ref, fim_ref, parts, sum_ref)
+    for half in range(2):
+        value = own_ref[0, half]
+        for arrived in (ahead_ref[2, half], back_ref[1, half], from5_ref[half], from3_ref[half]):
+            value = value + arrived.astype(jnp.float32)
+        msg_ref[half] = value
     msg_ref[2] = block
 
 
@@ -271,31 +284,29 @@
         total_ref[n] = plane
 
 
-def last_kernel(
-    where_ref,
-    fre_ref,
-    fim_ref,
-    sum0_ref,
-    sum1_ref,
-    init_ref,
-    d1_ref,
-    d2_ref,
-    d3_ref,
-    x_ref,
-    core_ref,
-    out_ref,
-):
-    steps = fre_ref.shape[0]
+def enter_kernel(where_ref, init_ref, d1_ref, d2_ref, d3_ref, x_ref, core_ref, out_ref):
     one = unit(init_ref.shape[1:])
     column = before_of(where_ref[2], [read(d1_ref), read(d2_ref), read(d3_ref)], one)
     start = after(column, [init_ref[0], init_ref[1], one[2]])
     start = after(read(x_ref), start)
     start = after(chosen(where_ref[0] == 1, read(core_ref), one), start)
-    for half, sum_ref in enumerate((sum0_ref, sum1_ref)):
-        state = start[half]
-        for t in range(steps):
-            state = turned(fre_ref[t], fim_ref[t], state + sum_ref[t])
-            out_ref[t, :, half, :] = state
+    for half in range(2):
+        out_ref[half] = start[half]
+
+
+def last_kernel(
+    fre_ref, fim_ref, enter_ref, even_ref, own_ref, ahead_ref, back_ref, from5_ref, from3_ref, out_ref
+):
+    steps = fre_ref.shape[0]
+    even, odd = enter_ref[0], enter_ref[1]
+    for t in range(steps):
+        value = own_ref[0, t]
+        for arrived in (ahead_ref[2, t], back_ref[1, t], from5_ref[t], from3_ref[t]):
+            value = value + arrived.astype(jnp.float32)
+        even = turned(fre_ref[t], fim_ref[t], even + even_ref[t])
+        odd = turned(fre_ref[t], fim_ref[t], odd + value)
+        out_ref[t, :, 0, :] = even
+        out_ref[t, :, 1, :] = odd
 
 
 def small_call(kernel, out_shape, scalars, *arrays):
@@ -332,21 +343,20 @@
     return total.astype(jnp.bfloat16)
 
 
-def column_sum(norm, cols_of, energy, panels, split):
-    near = ((3, jnp.bfloat16), (2, jnp.bfloat16), (1, jnp.float32))
-    far = ((2, jnp.float32),)
-    order = (4, 6, 1, 2, 7, 0, 3, 5)
-    if split:
-        ahead, back, own = product_call(norm, cols_of(order[:6]), energy, panels, near)
-    else:
-        ahead, back, own, rest = product_call(norm, cols_of(order), energy, panels, near + far)
+SHARES = (4, 6, 1, 2, 7, 0, 3, 5)
+
+
+def column_product(norm, cols_of, energy, factors, panels, even_ends=None):
+    kinds = ((3, jnp.bfloat16), (2, jnp.bfloat16), (1, jnp.float32), (2, jnp.float32))
+    return product_call(norm, cols_of(SHARES), energy, factors, panels, kinds, even_ends)
+
+
+def column_sum(ahead, back, rest):
     ahead = send(ahead, depth_perm(1))
     back = send(back, depth_perm(-1))
-    if split:
-        (rest,) = product_call(norm, cols_of(order[6:]), energy, panels, far)
     from5 = send(add_rounded(rest[1], ahead[1]), depth_perm(-3))
     from3 = send(add_rounded(rest[0], ahead[0], back[0]), depth_perm(3))
-    return [own, ahead, back, from5, from3]
+    return [ahead, back, from5, from3]
 
 
 def slot_table(row_index):
@@ -386,16 +396,6 @@
     def cols_of(rels):
         return ((col_index + way * jnp.array(rels, jnp.int32)) % Z).astype(jnp.int32)
 
-    line0, line1 = near_line(local)
-    blocks0 = far_blocks(line0)
-    blocks1 = far_blocks(line1)
-    panels0 = blocks0 + [send(block, CORE_SWAP) for block in blocks0]
-    parts0 = column_sum(norm, cols_of, energy, panels0, False)
-    panels1 = list(blocks1)
-    for block in blocks1:
-        panels1.append(send(block, CORE_SWAP))
-    parts1 = column_sum(norm, cols_of, energy, panels1, True)
-
     rotate_re = retention * jnp.cos(phase_angle)[None, :]
     rotate_im = retention * jnp.sin(phase_angle)[None, :]
     lane = jnp.arange(width, dtype=jnp.int32)
@@ -404,11 +404,27 @@
     fim = rotate_im[:, :, None] * sign
     start = jnp.swapaxes(initial, 0, 1)
 
+
+    line0, line1 = near_line(local)
+    blocks0 = far_blocks(line0)
+    blocks1 = far_blocks(line1)
+    panels0 = blocks0 + [send(block, CORE_SWAP) for block in blocks0]
+    factors = (fre, fim)
+    *terms0, own0, rest0, ends0 = column_product(norm, cols_of, energy, factors, panels0)
+    parts0 = column_sum(*terms0, rest0)
+    panels1 = list(blocks1)
+    for block in blocks1:
+        panels1.append(send(block, CORE_SWAP))
+    *terms1, own1, rest1, ends_ahead, ends_back, ends_rest = column_product(
+        norm, cols_of, energy, factors, panels1, ends0
+    )
+    end_parts = column_sum(ends_ahead, ends_back, ends_rest[1:])
+    parts1 = column_sum(*terms1, rest1)
+
     message = jax.ShapeDtypeStruct((3, orbitals, width), jnp.float32)
     total = jax.ShapeDtypeStruct((steps, orbitals, width), jnp.float32)
-    end = jax.ShapeDtypeStruct((orbitals, width), jnp.float32)
-    sum0, end0 = small_call(even_kernel, (total, end), None, fre, fim, *parts0)
-    sum1, ends = small_call(odd_kernel, (total, message), None, fre, fim, end0, *parts1)
+    sum0 = small_call(sum_kernel, total, None, own0, *parts0)
+    ends = small_call(message_kernel, message, None, fre, fim, ends_rest, *end_parts)
     other = send(ends, CORE_SWAP)
     chip = small_call(chip_kernel, message, where, ends, other)
     row_perm = lambda by: perm_of(lambda y, x, core, z: (y, x + by, core, z))
@@ -417,18 +433,25 @@
 
     before_x, line = small_call(line_kernel, (message, message), where, chip, *behind)
     behind = [send(line, column_perm(back)) for back in (1, 2, 3)]
-    return small_call(
-        last_kernel,
-        jax.ShapeDtypeStruct((steps, orbitals, 2, width), jnp.float32),
+    entering = small_call(
+        enter_kernel,
+        jax.ShapeDtypeStruct((2, orbitals, width), jnp.float32),
         where,
-        fre,
-        fim,
-        sum0,
-        sum1,
         start,
         *behind,
         before_x,
         other,
+    )
+    return small_call(
+        last_kernel,
+        jax.ShapeDtypeStruct((steps, orbitals, 2, width), jnp.float32),
+        None,
+        fre,
+        fim,
+        entering,
+        sum0,
+        own1,
+        *parts1,
     )
 
 

time: 115 us -> 120 us (1.043)
  the two profiles are of different devices: /device:TPU:8 before, /device:TPU:65 now
where the time goes in v2:
time: 120 us
  starting transfers between devices  49.9 us (42%)
  waiting for transfers between devices  39.6 us (33%)
  Pallas kernels  26.9 us (22%)
  local copies, waits for them, and re-layouts  1.73 us (1%)
  other arithmetic  1.45 us (1%)
    ppermute x36, starting transfers between devices, send(): return lax.ppermute(array, BOTH, perm)  49.9 us
    ppermute x36, waiting for transfers between devices, send(): return lax.ppermute(array, BOTH, perm)  39.6 us
    pallas_call x2, Pallas kernels, product_call(): pl.pallas_call(body, out_shape=shape, grid_spec=pltpu.PrefetchScalarGridS...  12.8 us
    pallas_call x1, Pallas kernels, energy_call(): pl.pallas_call(energy_kernel, out_shape=jax.ShapeDtypeStruct((steps, 2, o...  9.28 us
    pallas_call x6, Pallas kernels, small_call(): pl.pallas_call(kernel, out_shape=out_shape, in_specs=specs, out_specs=out...  4.8 us
  transfers between devices with their start and end apart: 36, of which 16 were waited for; matrix products, arithmetic and copies ran while one was open for 2% of the time, Pallas kernels for 16%

profile of v2, /device:TPU:65, one launch (start us, length us, event | category | flops | bytes accessed | tf_op | source)
XLA Modules:
  0.0 119.9 jit_solution(6035110577316880498)
XLA Ops:
  0.0 1.0 copy.18
  1.0 0.1 reshape.62
  1.1 1.4 %collective-permute-start = (bf16[2,64,1024]{2,1,0:T(8,128)(2,1)S(1)}, bf16[2,64,1024]{2,1,0:T(8,128)(2,1)S(1)}, u32[]{:S(2)}, u32[]{:S(2)}) collective-permute-start(bf16[2,64,1024]{2,1,0:T(8,128)(2,1)S(1)} %reshape.62), channel_id=1, source_target_pairs={{0,16},{1,17},{2,18},{3,19},{4,20},{5,21},{6,22},{7,23},{8,72},{9,... | collective-permute-start | bytes 786440 | tf_op jit(solution)/shard_map/ppermute | solution.py:46
  2.5 1.5 %collective-permute-start.1 = (bf16[2,64,1024]{2,1,0:T(8,128)(2,1)S(1)}, bf16[2,64,1024]{2,1,0:T(8,128)(2,1)S(1)}, u32[]{:S(2)}, u32[]{:S(2)}) collective-permute-start(bf16[2,64,1024]{2,1,0:T(8,128)(2,1)S(1)} %reshape.62), channel_id=1, source_target_pairs={{0,48},{1,49},{2,50},{3,51},{4,52},{5,53},{6,54},{7,55},{8,200},{9... | collective-permute-start | bytes 786440 | tf_op jit(solution)/shard_map/ppermute | solution.py:46
  4.0 1.6 %collective-permute-start.2 = (bf16[2,64,1024]{2,1,0:T(8,128)(2,1)S(1)}, bf16[2,64,1024]{2,1,0:T(8,128)(2,1)S(1)}, u32[]{:S(2)}, u32[]{:S(2)}) collective-permute-start(bf16[2,64,1024]{2,1,0:T(8,128)(2,1)S(1)} %reshape.62), channel_id=1, source_target_pairs={{0,32},{1,33},{2,34},{3,35},{4,36},{5,37},{6,38},{7,39},{8,136},{9... | collective-permute-start | bytes 786440 | tf_op jit(solution)/shard_map/ppermute | solution.py:46
  5.6 0.8 select_add_fusion.3
  6.4 0.1 add.142
  6.6 0.1 add.152
  6.9 1.1 collective-permute-done
  8.0 2.1 %collective-permute-done.1 = bf16[2,64,1024]{2,1,0:T(8,128)(2,1)S(1)} collective-permute-done((bf16[2,64,1024]{2,1,0:T(8,128)(2,1)S(1)}, bf16[2,64,1024]{2,1,0:T(8,128)(2,1)S(1)}, u32[]{:S(2)}, u32[]{:S(2)}) %collective-permute-start.1) | collective-permute-done | bytes 262176 | tf_op jit(solution)/shard_map/ppermute | solution.py:46
  10.2 1.8 %collective-permute-done.2 = bf16[2,64,1024]{2,1,0:T(8,128)(2,1)S(1)} collective-permute-done((bf16[2,64,1024]{2,1,0:T(8,128)(2,1)S(1)}, bf16[2,64,1024]{2,1,0:T(8,128)(2,1)S(1)}, u32[]{:S(2)}, u32[]{:S(2)}) %collective-permute-start.2) | collective-permute-done | bytes 262176 | tf_op jit(solution)/shard_map/ppermute | solution.py:46
  12.0 1.0 collective-permute-start.3
  13.0 1.8 %collective-permute-start.4 = (bf16[256,1024]{1,0:T(8,128)(2,1)S(1)}, bf16[256,1024]{1,0:T(8,128)(2,1)S(1)}, u32[]{:S(2)}, u32[]{:S(2)}) collective-permute-start(bf16[256,1024]{1,0:T(8,128)(2,1)S(1)} %pad_maximum_fusion.refs_0_.refs_8_.refs_16_.refs_24_.refs_32_.refs_40_.refs_48_.refs_56_), channel_id=1, source_target_pairs={{0,192},{1,193},{2,194},{3,195},{4,196},{5,197},{6,198},{7,199},{8... | collective-permute-start | bytes 1572872 | tf_op jit(solution)/shard_map/ppermute | solution.py:46
  14.8 1.2 %collective-permute-start.5 = (bf16[256,1024]{1,0:T(8,128)(2,1)S(1)}, bf16[256,1024]{1,0:T(8,128)(2,1)S(1)}, u32[]{:S(2)}, u32[]{:S(2)}) collective-permute-start(bf16[256,1024]{1,0:T(8,128)(2,1)S(1)} %pad_maximum_fusion.refs_0_.refs_8_.refs_16_.refs_24_.refs_32_.refs_40_.refs_48_.refs_56_), channel_id=1, source_target_pairs={{0,128},{1,129},{2,130},{3,131},{4,132},{5,133},{6,134},{7,135},{8... | collective-permute-start | bytes 1572872 | tf_op jit(solution)/shard_map/ppermute | solution.py:46
  16.0 2.6 %collective-permute-start.6 = (bf16[256,1024]{1,0:T(8,128)(2,1)S(1)}, bf16[256,1024]{1,0:T(8,128)(2,1)S(1)}, u32[]{:S(2)}, u32[]{:S(2)}) collective-permute-start(bf16[256,1024]{1,0:T(8,128)(2,1)S(1)} %pad_maximum_fusion.refs_0_.refs_8_.refs_16_.refs_24_.refs_32_.refs_40_.refs_48_.refs_56_), channel_id=1, source_target_pairs={{0,8},{1,9},{2,10},{3,11},{4,12},{5,13},{6,14},{7,15},{8,0},{9,1},... | collective-permute-start | bytes 1572872 | tf_op jit(solution)/shard_map/ppermute | solution.py:46
  18.7 1.2 %collective-permute-start.10 = (bf16[256,1024]{1,0:T(8,128)(2,1)S(1)}, bf16[256,1024]{1,0:T(8,128)(2,1)S(1)}, u32[]{:S(2)}, u32[]{:S(2)}) collective-permute-start(bf16[256,1024]{1,0:T(8,128)(2,1)S(1)} %pad_maximum_fusion.1.refs_1_.refs_9_.refs_17_.refs_25_.refs_33_.refs_41_.refs_49_.refs_57_), channel_id=1, source_target_pairs={{0,64},{1,65},{2,66},{3,67},{4,68},{5,69},{6,70},{7,71},{8,24},{9,... | collective-permute-start | bytes 1572872 | tf_op jit(solution)/shard_map/ppermute | solution.py:46
  20.0 9.3 %shard_map.91.energy_ref = bf16[8,2,64,2048]{3,2,1,0:T(8,128)(2,1)S(1)} custom-call(s32[32]{0:T(128)S(1)} %pad_add_fusion.1.slots, s32[2]{0:T(128)S(1)} %pad_add_fusion.2.times, bf16[8,32,64,128]{3,2,1,0:T(8,128)(2,1)} %ret_ref.1, bf16[32,8,64,128]{3,2,1,0:T(8,128)(2,1)} %mir_ref.1), custom_call_target="tpu_custom_call" | custom-call | flops 41943040 | bytes 12582912 | tf_op jit(solution)/shard_map/pallas_call | solution.py:83
  29.4 1.6 %collective-permute-start.11 = (bf16[256,1024]{1,0:T(8,128)(2,1)S(1)}, bf16[256,1024]{1,0:T(8,128)(2,1)S(1)}, u32[]{:S(2)}, u32[]{:S(2)}) collective-permute-start(bf16[256,1024]{1,0:T(8,128)(2,1)S(1)} %pad_maximum_fusion.1.refs_1_.refs_9_.refs_17_.refs_25_.refs_33_.refs_41_.refs_49_.refs_57_), channel_id=1, source_target_pairs={{0,192},{1,193},{2,194},{3,195},{4,196},{5,197},{6,198},{7,199},{8... | collective-permute-start | bytes 1572872 | tf_op jit(solution)/shard_map/ppermute | solution.py:46
  31.0 0.6 collective-permute-start.12
  31.6 0.3 collective-permute-start.7
  31.9 0.2 collective-permute-start.8
  32.1 1.7 %collective-permute-done.10.refs_2_.refs_10_.refs_18_.refs_26_.refs_34_.refs_42_.refs_50_.refs_58_ = bf16[256,1024]{1,0:T(8,128)(2,1)S(1)} collective-permute-done((bf16[256,1024]{1,0:T(8,128)(2,1)S(1)}, bf16[256,1024]{1,0:T(8,128)(2,1)S(1)}, u32[]{:S(2)}, u32[]{:S(2)}) %collective-permute-start.10) | collective-permute-done | bytes 524320 | tf_op jit(solution)/shard_map/ppermute | solution.py:46
  33.9 1.1 collective-permute-start.9
  35.0 0.1 broadcast_multiply_fusion.fim_ref
  35.2 7.6 %collective-permute-done.11.refs_3_.refs_11_.refs_19_.refs_27_.refs_35_.refs_43_.refs_51_.refs_59_ = bf16[256,1024]{1,0:T(8,128)(2,1)S(1)} collective-permute-done((bf16[256,1024]{1,0:T(8,128)(2,1)S(1)}, bf16[256,1024]{1,0:T(8,128)(2,1)S(1)}, u32[]{:S(2)}, u32[]{:S(2)}) %collective-permute-start.11) | collective-permute-done | bytes 524320 | tf_op jit(solution)/shard_map/ppermute | solution.py:46
  42.7 1.2 collective-permute-start.13
  43.9 0.5 collective-permute-start.15
  44.4 0.3 collective-permute-start.16
  44.7 0.1 broadcast_in_dim.12.fre_ref
  44.8 6.4 %shard_map.92 = (bf16[3,8,64,128]{3,2,1,0:T(8,128)(2,1)S(1)}, bf16[2,8,64,128]{3,2,1,0:T(8,128)(2,1)S(1)}, f32[1,8,64,128]{3,2,1,0:T(8,128)S(1)}, f32[2,8,64,128]{3,2,1,0:T(8,128)S(1)}, f32[8,64,128]{2,1,0:T(8,128)S(1)}) custom-call(s32[8]{0:T(128)S(1)} %and_select_fusion.4.cols_ref, bf16[8,2,64,2048]{3,2,1,0:T(8,128)(2,1)S(1)} %shard_map.91.energy_ref, ...), custom_call_target="tpu_custom_call" | custom-call | flops 4294967296 | bytes 8388608 | tf_op jit(solution)/shard_map/pallas_call | solution.py:169
  51.3 6.4 %shard_map.93 = (bf16[3,8,64,128]{3,2,1,0:T(8,128)(2,1)S(1)}, bf16[2,8,64,128]{3,2,1,0:T(8,128)(2,1)S(1)}, f32[1,8,64,128]{3,2,1,0:T(8,128)S(1)}, f32[2,8,64,128...) custom-call(s32[8]{0:T(128)S(1)} %and_select_fusion.4.cols_ref, ...), custom_call_target="tpu_custom_call" | custom-call | flops 4294967296 | bytes 8388608 | tf_op jit(solution)/shard_map/pallas_call | solution.py:169
  57.8 0.1 collective-permute-start.17
  57.8 1.7 %collective-permute-start.18 = (bf16[2,2,64,128]{3,2,1,0:T(8,128)(2,1)S(1)}, bf16[2,2,64,128]{3,2,1,0:T(8,128)(2,1)S(1)}, u32[]{:S(2)}, u32[]{:S(2)}) collective-permute-start(bf16[2,2,64,128]{3,2,1,0:T(8,128)(2,1)S(1)} %get-tuple-element.22), channel_id=1, source_target_pairs={{0,7},{1,0},{2,1},{3,2},{4,3},{5,4},{6,5},{7,6},{8,9},{9,10},{10,1... | collective-permute-start | bytes 196616 | tf_op jit(solution)/shard_map/ppermute | solution.py:46
  59.5 1.9 %collective-permute-done.18.back_ref = bf16[2,2,64,128]{3,2,1,0:T(8,128)(2,1)S(1)} collective-permute-done((bf16[2,2,64,128]{3,2,1,0:T(8,128)(2,1)S(1)}, bf16[2,2,64,128]{3,2,1,0:T(8,128)(2,1)S(1)}, u32[]{:S(2)}, u32[]{:S(2)}) %collective-permute-start.18) | collective-permute-done | bytes 65568 | tf_op jit(solution)/shard_map/ppermute | solution.py:46
  61.4 0.3 collective-permute-done.17.ahead_ref
  61.8 5.6 %collective-permute-start.19 = (bf16[2,64,128]{2,1,0:T(8,128)(2,1)S(1)}, bf16[2,64,128]{2,1,0:T(8,128)(2,1)S(1)}, u32[]{:S(2)}, u32[]{:S(2)}) collective-permute-start(bf16[2,64,128]{2,1,0:T(8,128)(2,1)S(1)} %get-tuple-element.38), channel_id=1, source_target_pairs={{0,5},{1,6},{2,7},{3,0},{4,1},{5,2},{6,3},{7,4},{8,11},{9,12},{10,... | collective-permute-start | bytes 98312 | tf_op jit(solution)/shard_map/ppermute | solution.py:46
  67.4 0.5 collective-permute-start.20
  67.9 0.6 collective-permute-start.29
  68.5 1.0 collective-permute-done.19.from5_ref
  69.4 4.7 %collective-permute-done.20.from3_ref = bf16[2,64,128]{2,1,0:T(8,128)(2,1)S(1)} collective-permute-done((bf16[2,64,128]{2,1,0:T(8,128)(2,1)S(1)}, bf16[2,64,128]{2,1,0:T(8,128)(2,1)S(1)}, u32[]{:S(2)}, u32[]{:S(2)}) %collective-permute-start.20) | collective-permute-done | bytes 32800 | tf_op jit(solution)/shard_map/ppermute | solution.py:46
  74.2 0.6 shard_map.94.own_ref
  74.7 1.9 %collective-permute-start.21 = (f32[3,64,128]{2,1,0:T(8,128)S(1)}, f32[3,64,128]{2,1,0:T(8,128)S(1)}, u32[]{:S(2)}, u32[]{:S(2)}) collective-permute-start(f32[3,64,128]{2,1,0:T(8,128)S(1)} %shard_map.94.own_ref), channel_id=1, source_target_pairs={{0,8},{1,9},{2,10},{3,11},{4,12},{5,13},{6,14},{7,15},{8,0},{9,1},... | collective-permute-start | bytes 294920 | tf_op jit(solution)/shard_map/ppermute | solution.py:46
  76.7 0.9 collective-permute-done.21.other_ref.core_ref
  77.6 0.6 shard_map.95.own_ref
  78.2 1.2 %collective-permute-start.22 = (f32[3,64,128]{2,1,0:T(8,128)S(1)}, f32[3,64,128]{2,1,0:T(8,128)S(1)}, u32[]{:S(2)}, u32[]{:S(2)}) collective-permute-start(f32[3,64,128]{2,1,0:T(8,128)S(1)} %shard_map.95.own_ref), channel_id=1, source_target_pairs={{0,16},{1,17},{2,18},{3,19},{4,20},{5,21},{6,22},{7,23},{8,24},{9,... | collective-permute-start | bytes 294920 | tf_op jit(solution)/shard_map/ppermute | solution.py:46
  79.4 1.5 %collective-permute-start.32 = (bf16[3,8,64,128]{3,2,1,0:T(8,128)(2,1)S(1)}, bf16[3,8,64,128]{3,2,1,0:T(8,128)(2,1)S(1)}, u32[]{:S(2)}, u32[]{:S(2)}) collective-permute-start(bf16[3,8,64,128]{3,2,1,0:T(8,128)(2,1)S(1)} %get-tuple-element.30), channel_id=1, source_target_pairs={{0,1},{1,2},{2,3},{3,4},{4,5},{5,6},{6,7},{7,0},{8,15},{9,8},{10,9... | collective-permute-start | bytes 1179656 | tf_op jit(solution)/shard_map/ppermute | solution.py:46
  80.9 2.3 %collective-permute-start.23 = (f32[3,64,128]{2,1,0:T(8,128)S(1)}, f32[3,64,128]{2,1,0:T(8,128)S(1)}, u32[]{:S(2)}, u32[]{:S(2)}) collective-permute-start(f32[3,64,128]{2,1,0:T(8,128)S(1)} %shard_map.95.own_ref), channel_id=1, source_target_pairs={{0,32},{1,33},{2,34},{3,35},{4,36},{5,37},{6,38},{7,39},{8,40},{9,... | collective-permute-start | bytes 294920 | tf_op jit(solution)/shard_map/ppermute | solution.py:46
  83.2 0.3 collective-permute-done.22.d1_ref
  83.5 1.0 collective-permute-start.24
  84.5 2.6 %collective-permute-done.23.d2_ref = f32[3,64,128]{2,1,0:T(8,128)S(1)} collective-permute-done((f32[3,64,128]{2,1,0:T(8,128)S(1)}, f32[3,64,128]{2,1,0:T(8,128)S(1)}, u32[]{:S(2)}, u32[]{:S(2)}) %collective-permute-start.23) | collective-permute-done | bytes 98336 | tf_op jit(solution)/shard_map/ppermute | solution.py:46
  87.1 0.3 collective-permute-done.24.d3_ref
  87.4 1.1 shard_map.96
  88.6 1.2 %collective-permute-start.25 = (f32[3,64,128]{2,1,0:T(8,128)S(1)}, f32[3,64,128]{2,1,0:T(8,128)S(1)}, u32[]{:S(2)}, u32[]{:S(2)}) collective-permute-start(f32[3,64,128]{2,1,0:T(8,128)S(1)} %get-tuple-element.23), channel_id=1, source_target_pairs={{0,64},{1,65},{2,66},{3,67},{4,68},{5,69},{6,70},{7,71},{8,72},{9,... | collective-permute-start | bytes 294920 | tf_op jit(solution)/shard_map/ppermute | solution.py:46
  89.8 3.4 %collective-permute-start.26 = (f32[3,64,128]{2,1,0:T(8,128)S(1)}, f32[3,64,128]{2,1,0:T(8,128)S(1)}, u32[]{:S(2)}, u32[]{:S(2)}) collective-permute-start(f32[3,64,128]{2,1,0:T(8,128)S(1)} %get-tuple-element.23), channel_id=1, source_target_pairs={{0,128},{1,129},{2,130},{3,131},{4,132},{5,133},{6,134},{7,135},{8... | collective-permute-start | bytes 294920 | tf_op jit(solution)/shard_map/ppermute | solution.py:46
  93.3 3.9 %collective-permute-start.30 = (bf16[8,64,128]{2,1,0:T(8,128)(2,1)S(1)}, bf16[8,64,128]{2,1,0:T(8,128)(2,1)S(1)}, u32[]{:S(2)}, u32[]{:S(2)}) collective-permute-start(bf16[8,64,128]{2,1,0:T(8,128)(2,1)S(1)} %get-tuple-element.36), channel_id=1, source_target_pairs={{0,5},{1,6},{2,7},{3,0},{4,1},{5,2},{6,3},{7,4},{8,11},{9,12},{10,... | collective-permute-start | bytes 393224 | tf_op jit(solution)/shard_map/ppermute | solution.py:46
  97.2 0.8 collective-permute-start.31
  98.0 3.8 %collective-permute-start.34 = (bf16[8,64,128]{2,1,0:T(8,128)(2,1)S(1)}, bf16[8,64,128]{2,1,0:T(8,128)(2,1)S(1)}, u32[]{:S(2)}, u32[]{:S(2)}) collective-permute-start(bf16[8,64,128]{2,1,0:T(8,128)(2,1)S(1)} %get-tuple-element.34), channel_id=1, source_target_pairs={{0,5},{1,6},{2,7},{3,0},{4,1},{5,2},{6,3},{7,4},{8,11},{9,12},{10,... | collective-permute-start | bytes 393224 | tf_op jit(solution)/shard_map/ppermute | solution.py:46
  101.8 0.8 collective-permute-start.35
  102.6 1.6 %collective-permute-start.27 = (f32[3,64,128]{2,1,0:T(8,128)S(1)}, f32[3,64,128]{2,1,0:T(8,128)S(1)}, u32[]{:S(2)}, u32[]{:S(2)}) collective-permute-start(f32[3,64,128]{2,1,0:T(8,128)S(1)} %get-tuple-element.23), channel_id=1, source_target_pairs={{0,192},{1,193},{2,194},{3,195},{4,196},{5,197},{6,198},{7,199},{8... | collective-permute-start | bytes 294920 | tf_op jit(solution)/shard_map/ppermute | solution.py:46
  104.2 2.1 %collective-permute-done.27.d3_ref = f32[3,64,128]{2,1,0:T(8,128)S(1)} collective-permute-done((f32[3,64,128]{2,1,0:T(8,128)S(1)}, f32[3,64,128]{2,1,0:T(8,128)S(1)}, u32[]{:S(2)}, u32[]{:S(2)}) %collective-permute-start.27) | collective-permute-done | bytes 98336 | tf_op jit(solution)/shard_map/ppermute | solution.py:46
  106.3 1.0 shard_map.97.enter_ref
  107.3 3.8 %collective-permute-done.31.from3_ref = bf16[8,64,128]{2,1,0:T(8,128)(2,1)S(1)} collective-permute-done((bf16[8,64,128]{2,1,0:T(8,128)(2,1)S(1)}, bf16[8,64,128]{2,1,0:T(8,128)(2,1)S(1)}, u32[]{:S(2)}, u32[]{:S(2)}) %collective-permute-start.31) | collective-permute-done | bytes 131104 | tf_op jit(solution)/shard_map/ppermute | solution.py:46
  111.2 7.2 %collective-permute-done.35.from3_ref = bf16[8,64,128]{2,1,0:T(8,128)(2,1)S(1)} collective-permute-done((bf16[8,64,128]{2,1,0:T(8,128)(2,1)S(1)}, bf16[8,64,128]{2,1,0:T(8,128)(2,1)S(1)}, u32[]{:S(2)}, u32[]{:S(2)}) %collective-permute-start.35) | collective-permute-done | bytes 131104 | tf_op jit(solution)/shard_map/ppermute | solution.py:46
  118.4 1.4 %shard_map.99 = f32[8,64,2,128]{3,2,1,0:T(2,128)} custom-call(f32[8,64,128]{2,1,0:T(8,128)S(1)} %broadcast_in_dim.12.fre_ref, f32[8,64,128]{2,1,0:T(8,128)S(1)} %broadcast_multiply_fusion.fim_ref, f32[2,64,128]{2,1,0:T(8,128)S(1)} %shard_map.97.enter_ref, f32[8,64,128]{2,1,0:T(8,128)S(1)} %shard_map.98.even_ref, ...), custom_call_target="tpu_custom_call" | custom-call | flops 1000000 | bytes 1048576 | tf_op jit(solution)/shard_map/pallas_call | solution.py:317
  (54 shorter events, 1.0 us)
Async XLA Ops:
  1.1 6.9 %collective-permute-start = (bf16[2,64,1024]{2,1,0:T(8,128)(2,1)S(1)}, bf16[2,64,1024]{2,1,0:T(8,128)(2,1)S(1)}, u32[]{:S(2)}, u32[]{:S(2)}) collective-permute-start(bf16[2,64,1024]{2,1,0:T(8,128)(2,1)S(1)} %reshape.62), channel_id=1, source_target_pairs={{0,16},{1,17},{2,18},{3,19},{4,20},{5,21},{6,22},{7,23},{8,72},{9,... | collective-permute-start | bytes 786440 | tf_op jit(solution)/shard_map/ppermute | solution.py:46
  2.5 7.7 %collective-permute-start.1 = (bf16[2,64,1024]{2,1,0:T(8,128)(2,1)S(1)}, bf16[2,64,1024]{2,1,0:T(8,128)(2,1)S(1)}, u32[]{:S(2)}, u32[]{:S(2)}) collective-permute-start(bf16[2,64,1024]{2,1,0:T(8,128)(2,1)S(1)} %reshape.62), channel_id=1, source_target_pairs={{0,48},{1,49},{2,50},{3,51},{4,52},{5,53},{6,54},{7,55},{8,200},{9... | collective-permute-start | bytes 786440 | tf_op jit(solution)/shard_map/ppermute | solution.py:46
  4.0 8.0 %collective-permute-start.2 = (bf16[2,64,1024]{2,1,0:T(8,128)(2,1)S(1)}, bf16[2,64,1024]{2,1,0:T(8,128)(2,1)S(1)}, u32[]{:S(2)}, u32[]{:S(2)}) collective-permute-start(bf16[2,64,1024]{2,1,0:T(8,128)(2,1)S(1)} %reshape.62), channel_id=1, source_target_pairs={{0,32},{1,33},{2,34},{3,35},{4,36},{5,37},{6,38},{7,39},{8,136},{9... | collective-permute-start | bytes 786440 | tf_op jit(solution)/shard_map/ppermute | solution.py:46
  12.0 17.3 %collective-permute-start.3 = (bf16[256,1024]{1,0:T(8,128)(2,1)S(1)}, bf16[256,1024]{1,0:T(8,128)(2,1)S(1)}, u32[]{:S(2)}, u32[]{:S(2)}) collective-permute-start(bf16[256,1024]{1,0:T(8,128)(2,1)S(1)} %pad_maximum_fusion.refs_0_.refs_8_.refs_16_.refs_24_.refs_32_.refs_40_.refs_48_.refs_56_), channel_id=1, source_target_pairs={{0,64},{1,65},{2,66},{3,67},{4,68},{5,69},{6,70},{7,71},{8,24},{9,... | collective-permute-start | bytes 1572872 | tf_op jit(solution)/shard_map/ppermute | solution.py:46
  13.0 18.0 %collective-permute-start.4 = (bf16[256,1024]{1,0:T(8,128)(2,1)S(1)}, bf16[256,1024]{1,0:T(8,128)(2,1)S(1)}, u32[]{:S(2)}, u32[]{:S(2)}) collective-permute-start(bf16[256,1024]{1,0:T(8,128)(2,1)S(1)} %pad_maximum_fusion.refs_0_.refs_8_.refs_16_.refs_24_.refs_32_.refs_40_.refs_48_.refs_56_), channel_id=1, source_target_pairs={{0,192},{1,193},{2,194},{3,195},{4,196},{5,197},{6,198},{7,199},{8... | collective-permute-start | bytes 1572872 | tf_op jit(solution)/shard_map/ppermute | solution.py:46
  14.8 16.8 %collective-permute-start.5 = (bf16[256,1024]{1,0:T(8,128)(2,1)S(1)}, bf16[256,1024]{1,0:T(8,128)(2,1)S(1)}, u32[]{:S(2)}, u32[]{:S(2)}) collective-permute-start(bf16[256,1024]{1,0:T(8,128)(2,1)S(1)} %pad_maximum_fusion.refs_0_.refs_8_.refs_16_.refs_24_.refs_32_.refs_40_.refs_48_.refs_56_), channel_id=1, source_target_pairs={{0,128},{1,129},{2,130},{3,131},{4,132},{5,133},{6,134},{7,135},{8... | collective-permute-start | bytes 1572872 | tf_op jit(solution)/shard_map/ppermute | solution.py:46
  16.0 15.9 %collective-permute-start.6 = (bf16[256,1024]{1,0:T(8,128)(2,1)S(1)}, bf16[256,1024]{1,0:T(8,128)(2,1)S(1)}, u32[]{:S(2)}, u32[]{:S(2)}) collective-permute-start(bf16[256,1024]{1,0:T(8,128)(2,1)S(1)} %pad_maximum_fusion.refs_0_.refs_8_.refs_16_.refs_24_.refs_32_.refs_40_.refs_48_.refs_56_), channel_id=1, source_target_pairs={{0,8},{1,9},{2,10},{3,11},{4,12},{5,13},{6,14},{7,15},{8,0},{9,1},... | collective-permute-start | bytes 1572872 | tf_op jit(solution)/shard_map/ppermute | solution.py:46
  18.7 15.1 %collective-permute-start.10 = (bf16[256,1024]{1,0:T(8,128)(2,1)S(1)}, bf16[256,1024]{1,0:T(8,128)(2,1)S(1)}, u32[]{:S(2)}, u32[]{:S(2)}) collective-permute-start(bf16[256,1024]{1,0:T(8,128)(2,1)S(1)} %pad_maximum_fusion.1.refs_1_.refs_9_.refs_17_.refs_25_.refs_33_.refs_41_.refs_49_.refs_57_), channel_id=1, source_target_pairs={{0,64},{1,65},{2,66},{3,67},{4,68},{5,69},{6,70},{7,71},{8,24},{9,... | collective-permute-start | bytes 1572872 | tf_op jit(solution)/shard_map/ppermute | solution.py:46
  20.0 9.3 %copy-start.3 = (f32[64]{0:T(128)S(1)}, f32[64]{0:T(128)}, u32[]{:S(2)}) copy-start(f32[64]{0:T(128)} %param.14) | copy-start | bytes 772
  20.0 12.1 %copy-start.1 = (f32[8,64]{1,0:T(8,128)S(1)}, f32[8,64]{1,0:T(8,128)}, u32[]{:S(2)}) copy-start(f32[8,64]{1,0:T(8,128)} %param.13) | copy-start | bytes 6148
  20.0 24.7 %copy-start.2 = (s32[8]{0:T(128)S(1)}, s32[8]{0:T(128)}, u32[]{:S(2)}) copy-start(s32[8]{0:T(128)} %constant.119.clone) | copy-start | bytes 100
  29.4 13.4 %collective-permute-start.11 = (bf16[256,1024]{1,0:T(8,128)(2,1)S(1)}, bf16[256,1024]{1,0:T(8,128)(2,1)S(1)}, u32[]{:S(2)}, u32[]{:S(2)}) collective-permute-start(bf16[256,1024]{1,0:T(8,128)(2,1)S(1)} %pad_maximum_fusion.1.refs_1_.refs_9_.refs_17_.refs_25_.refs_33_.refs_41_.refs_49_.refs_57_), channel_id=1, source_target_pairs={{0,192},{1,193},{2,194},{3,195},{4,196},{5,197},{6,198},{7,199},{8... | collective-permute-start | bytes 1572872 | tf_op jit(solution)/shard_map/ppermute | solution.py:46
  31.0 12.9 %collective-permute-start.12 = (bf16[256,1024]{1,0:T(8,128)(2,1)S(1)}, bf16[256,1024]{1,0:T(8,128)(2,1)S(1)}, u32[]{:S(2)}, u32[]{:S(2)}) collective-permute-start(bf16[256,1024]{1,0:T(8,128)(2,1)S(1)} %pad_maximum_fusion.1.refs_1_.refs_9_.refs_17_.refs_25_.refs_33_.refs_41_.refs_49_.refs_57_), channel_id=1, source_target_pairs={{0,128},{1,129},{2,130},{3,131},{4,132},{5,133},{6,134},{7,135},{8... | collective-permute-start | bytes 1572872 | tf_op jit(solution)/shard_map/ppermute | solution.py:46
  31.6 12.3 %collective-permute-start.7 = (bf16[256,1024]{1,0:T(8,128)(2,1)S(1)}, bf16[256,1024]{1,0:T(8,128)(2,1)S(1)}, u32[]{:S(2)}, u32[]{:S(2)}) collective-permute-start(bf16[256,1024]{1,0:T(8,128)(2,1)S(1)} %collective-permute-done.3.refs_1_.refs_9_.refs_17_.refs_25_.refs_33_.refs_41_.refs_49_.refs_57_), channel_id=1, source_target_pairs={{0,8},{1,9},{2,10},{3,11},{4,12},{5,13},{6,14},{7,15},{8,0},{9,1},... | collective-permute-start | bytes 1572872 | tf_op jit(solution)/shard_map/ppermute | solution.py:46
  31.9 12.5 %collective-permute-start.8 = (bf16[256,1024]{1,0:T(8,128)(2,1)S(1)}, bf16[256,1024]{1,0:T(8,128)(2,1)S(1)}, u32[]{:S(2)}, u32[]{:S(2)}) collective-permute-start(bf16[256,1024]{1,0:T(8,128)(2,1)S(1)} %collective-permute-done.4.refs_2_.refs_10_.refs_18_.refs_26_.refs_34_.refs_42_.refs_50_.refs_58_), channel_id=1, source_target_pairs={{0,8},{1,9},{2,10},{3,11},{4,12},{5,13},{6,14},{7,15},{8,0},{9,1},... | collective-permute-start | bytes 1572872 | tf_op jit(solution)/shard_map/ppermute | solution.py:46
  33.9 10.8 %collective-permute-start.9 = (bf16[256,1024]{1,0:T(8,128)(2,1)S(1)}, bf16[256,1024]{1,0:T(8,128)(2,1)S(1)}, u32[]{:S(2)}, u32[]{:S(2)}) collective-permute-start(bf16[256,1024]{1,0:T(8,128)(2,1)S(1)} %collective-permute-done.5.refs_3_.refs_11_.refs_19_.refs_27_.refs_35_.refs_43_.refs_51_.refs_59_), channel_id=1, source_target_pairs={{0,8},{1,9},{2,10},{3,11},{4,12},{5,13},{6,14},{7,15},{8,0},{9,1},... | collective-permute-start | bytes 1572872 | tf_op jit(solution)/shard_map/ppermute | solution.py:46
  42.7 8.5 %collective-permute-start.13 = (bf16[256,1024]{1,0:T(8,128)(2,1)S(1)}, bf16[256,1024]{1,0:T(8,128)(2,1)S(1)}, u32[]{:S(2)}, u32[]{:S(2)}) collective-permute-start(bf16[256,1024]{1,0:T(8,128)(2,1)S(1)} %pad_maximum_fusion.1.refs_1_.refs_9_.refs_17_.refs_25_.refs_33_.refs_41_.refs_49_.refs_57_), channel_id=1, source_target_pairs={{0,8},{1,9},{2,10},{3,11},{4,12},{5,13},{6,14},{7,15},{8,0},{9,1},... | collective-permute-start | bytes 1572872 | tf_op jit(solution)/shard_map/ppermute | solution.py:46
  43.9 7.4 %collective-permute-start.14 = (bf16[256,1024]{1,0:T(8,128)(2,1)S(1)}, bf16[256,1024]{1,0:T(8,128)(2,1)S(1)}, u32[]{:S(2)}, u32[]{:S(2)}) collective-permute-start(bf16[256,1024]{1,0:T(8,128)(2,1)S(1)} %collective-permute-done.10.refs_2_.refs_10_.refs_18_.refs_26_.refs_34_.refs_42_.refs_50_.refs_58_), channel_id=1, source_target_pairs={{0,8},{1,9},{2,10},{3,11},{4,12},{5,13},{6,14},{7,15},{8,0},{9,1},... | collective-permute-start | bytes 1572872 | tf_op jit(solution)/shard_map/ppermute | solution.py:46
  43.9 7.4 %collective-permute-start.15 = (bf16[256,1024]{1,0:T(8,128)(2,1)S(1)}, bf16[256,1024]{1,0:T(8,128)(2,1)S(1)}, u32[]{:S(2)}, u32[]{:S(2)}) collective-permute-start(bf16[256,1024]{1,0:T(8,128)(2,1)S(1)} %collective-permute-done.11.refs_3_.refs_11_.refs_19_.refs_27_.refs_35_.refs_43_.refs_51_.refs_59_), channel_id=1, source_target_pairs={{0,8},{1,9},{2,10},{3,11},{4,12},{5,13},{6,14},{7,15},{8,0},{9,1},... | collective-permute-start | bytes 1572872 | tf_op jit(solution)/shard_map/ppermute | solution.py:46
  44.4 6.9 %collective-permute-start.16 = (bf16[256,1024]{1,0:T(8,128)(2,1)S(1)}, bf16[256,1024]{1,0:T(8,128)(2,1)S(1)}, u32[]{:S(2)}, u32[]{:S(2)}) collective-permute-start(bf16[256,1024]{1,0:T(8,128)(2,1)S(1)} %collective-permute-done.12.refs_4_.refs_12_.refs_20_.refs_28_.refs_36_.refs_44_.refs_52_.refs_60_), channel_id=1, source_target_pairs={{0,8},{1,9},{2,10},{3,11},{4,12},{5,13},{6,14},{7,15},{8,0},{9,1},... | collective-permute-start | bytes 1572872 | tf_op jit(solution)/shard_map/ppermute | solution.py:46
  57.7 46.5 %copy-start = (f32[64,2,128]{2,1,0:T(2,128)S(1)}, f32[64,2,128]{2,1,0:T(2,128)}, u32[]{:S(2)}) copy-start(f32[64,2,128]{2,1,0:T(2,128)} %param.12) | copy-start | bytes 196612
  57.8 4.0 %collective-permute-start.17 = (bf16[3,2,64,128]{3,2,1,0:T(8,128)(2,1)S(1)}, bf16[3,2,64,128]{3,2,1,0:T(8,128)(2,1)S(1)}, u32[]{:S(2)}, u32[]{:S(2)}) collective-permute-start(bf16[3,2,64,128]{3,2,1,0:T(8,128)(2,1)S(1)} %get-tuple-element.21), channel_id=1, source_target_pairs={{0,1},{1,2},{2,3},{3,4},{4,5},{5,6},{6,7},{7,0},{8,15},{9,8},{10,9... | collective-permute-start | bytes 294920 | tf_op jit(solution)/shard_map/ppermute | solution.py:46
  57.8 3.6 %collective-permute-start.18 = (bf16[2,2,64,128]{3,2,1,0:T(8,128)(2,1)S(1)}, bf16[2,2,64,128]{3,2,1,0:T(8,128)(2,1)S(1)}, u32[]{:S(2)}, u32[]{:S(2)}) collective-permute-start(bf16[2,2,64,128]{3,2,1,0:T(8,128)(2,1)S(1)} %get-tuple-element.22), channel_id=1, source_target_pairs={{0,7},{1,0},{2,1},{3,2},{4,3},{5,4},{6,5},{7,6},{8,9},{9,10},{10,1... | collective-permute-start | bytes 196616 | tf_op jit(solution)/shard_map/ppermute | solution.py:46
  59.5 33.7 %collective-permute-start.28 = (bf16[3,8,64,128]{3,2,1,0:T(8,128)(2,1)S(1)}, bf16[3,8,64,128]{3,2,1,0:T(8,128)(2,1)S(1)}, u32[]{:S(2)}, u32[]{:S(2)}) collective-permute-start(bf16[3,8,64,128]{3,2,1,0:T(8,128)(2,1)S(1)} %get-tuple-element.26), channel_id=1, source_target_pairs={{0,1},{1,2},{2,3},{3,4},{4,5},{5,6},{6,7},{7,0},{8,15},{9,8},{10,9... | collective-permute-start | bytes 1179656 | tf_op jit(solution)/shard_map/ppermute | solution.py:46
  61.8 7.7 %collective-permute-start.19 = (bf16[2,64,128]{2,1,0:T(8,128)(2,1)S(1)}, bf16[2,64,128]{2,1,0:T(8,128)(2,1)S(1)}, u32[]{:S(2)}, u32[]{:S(2)}) collective-permute-start(bf16[2,64,128]{2,1,0:T(8,128)(2,1)S(1)} %get-tuple-element.38), channel_id=1, source_target_pairs={{0,5},{1,6},{2,7},{3,0},{4,1},{5,2},{6,3},{7,4},{8,11},{9,12},{10,... | collective-permute-start | bytes 98312 | tf_op jit(solution)/shard_map/ppermute | solution.py:46
  67.4 6.8 %collective-permute-start.20 = (bf16[2,64,128]{2,1,0:T(8,128)(2,1)S(1)}, bf16[2,64,128]{2,1,0:T(8,128)(2,1)S(1)}, u32[]{:S(2)}, u32[]{:S(2)}) collective-permute-start(bf16[2,64,128]{2,1,0:T(8,128)(2,1)S(1)} %get-tuple-element.37), channel_id=1, source_target_pairs={{0,3},{1,4},{2,5},{3,6},{4,7},{5,0},{6,1},{7,2},{8,13},{9,14},{10,... | collective-permute-start | bytes 98312 | tf_op jit(solution)/shard_map/ppermute | solution.py:46
  67.9 21.9 %collective-permute-start.29 = (bf16[2,8,64,128]{3,2,1,0:T(8,128)(2,1)S(1)}, bf16[2,8,64,128]{3,2,1,0:T(8,128)(2,1)S(1)}, u32[]{:S(2)}, u32[]{:S(2)}) collective-permute-start(bf16[2,8,64,128]{3,2,1,0:T(8,128)(2,1)S(1)} %get-tuple-element.27), channel_id=1, source_target_pairs={{0,7},{1,0},{2,1},{3,2},{4,3},{5,4},{6,5},{7,6},{8,9},{9,10},{10,1... | collective-permute-start | bytes 786440 | tf_op jit(solution)/shard_map/ppermute | solution.py:46
  74.7 2.9 %collective-permute-start.21 = (f32[3,64,128]{2,1,0:T(8,128)S(1)}, f32[3,64,128]{2,1,0:T(8,128)S(1)}, u32[]{:S(2)}, u32[]{:S(2)}) collective-permute-start(f32[3,64,128]{2,1,0:T(8,128)S(1)} %shard_map.94.own_ref), channel_id=1, source_target_pairs={{0,8},{1,9},{2,10},{3,11},{4,12},{5,13},{6,14},{7,15},{8,0},{9,1},... | collective-permute-start | bytes 294920 | tf_op jit(solution)/shard_map/ppermute | solution.py:46
  78.2 5.3 %collective-permute-start.22 = (f32[3,64,128]{2,1,0:T(8,128)S(1)}, f32[3,64,128]{2,1,0:T(8,128)S(1)}, u32[]{:S(2)}, u32[]{:S(2)}) collective-permute-start(f32[3,64,128]{2,1,0:T(8,128)S(1)} %shard_map.95.own_ref), channel_id=1, source_target_pairs={{0,16},{1,17},{2,18},{3,19},{4,20},{5,21},{6,22},{7,23},{8,24},{9,... | collective-permute-start | bytes 294920 | tf_op jit(solution)/shard_map/ppermute | solution.py:46
  79.4 18.5 %collective-permute-start.32 = (bf16[3,8,64,128]{3,2,1,0:T(8,128)(2,1)S(1)}, bf16[3,8,64,128]{3,2,1,0:T(8,128)(2,1)S(1)}, u32[]{:S(2)}, u32[]{:S(2)}) collective-permute-start(bf16[3,8,64,128]{3,2,1,0:T(8,128)(2,1)S(1)} %get-tuple-element.30), channel_id=1, source_target_pairs={{0,1},{1,2},{2,3},{3,4},{4,5},{5,6},{6,7},{7,0},{8,15},{9,8},{10,9... | collective-permute-start | bytes 1179656 | tf_op jit(solution)/shard_map/ppermute | solution.py:46
  80.9 6.2 %collective-permute-start.23 = (f32[3,64,128]{2,1,0:T(8,128)S(1)}, f32[3,64,128]{2,1,0:T(8,128)S(1)}, u32[]{:S(2)}, u32[]{:S(2)}) collective-permute-start(f32[3,64,128]{2,1,0:T(8,128)S(1)} %shard_map.95.own_ref), channel_id=1, source_target_pairs={{0,32},{1,33},{2,34},{3,35},{4,36},{5,37},{6,38},{7,39},{8,40},{9,... | collective-permute-start | bytes 294920 | tf_op jit(solution)/shard_map/ppermute | solution.py:46
  83.5 3.9 %collective-permute-start.24 = (f32[3,64,128]{2,1,0:T(8,128)S(1)}, f32[3,64,128]{2,1,0:T(8,128)S(1)}, u32[]{:S(2)}, u32[]{:S(2)}) collective-permute-start(f32[3,64,128]{2,1,0:T(8,128)S(1)} %shard_map.95.own_ref), channel_id=1, source_target_pairs={{0,48},{1,49},{2,50},{3,51},{4,52},{5,53},{6,54},{7,55},{8,56},{9,... | collective-permute-start | bytes 294920 | tf_op jit(solution)/shard_map/ppermute | solution.py:46
  87.1 10.0 %collective-permute-start.33 = (bf16[2,8,64,128]{3,2,1,0:T(8,128)(2,1)S(1)}, bf16[2,8,64,128]{3,2,1,0:T(8,128)(2,1)S(1)}, u32[]{:S(2)}, u32[]{:S(2)}) collective-permute-start(bf16[2,8,64,128]{3,2,1,0:T(8,128)(2,1)S(1)} %get-tuple-element.31), channel_id=1, source_target_pairs={{0,7},{1,0},{2,1},{3,2},{4,3},{5,4},{6,5},{7,6},{8,9},{9,10},{10,1... | collective-permute-start | bytes 786440 | tf_op jit(solution)/shard_map/ppermute | solution.py:46
  88.6 13.2 %collective-permute-start.25 = (f32[3,64,128]{2,1,0:T(8,128)S(1)}, f32[3,64,128]{2,1,0:T(8,128)S(1)}, u32[]{:S(2)}, u32[]{:S(2)}) collective-permute-start(f32[3,64,128]{2,1,0:T(8,128)S(1)} %get-tuple-element.23), channel_id=1, source_target_pairs={{0,64},{1,65},{2,66},{3,67},{4,68},{5,69},{6,70},{7,71},{8,72},{9,... | collective-permute-start | bytes 294920 | tf_op jit(solution)/shard_map/ppermute | solution.py:46
  89.8 12.8 %collective-permute-start.26 = (f32[3,64,128]{2,1,0:T(8,128)S(1)}, f32[3,64,128]{2,1,0:T(8,128)S(1)}, u32[]{:S(2)}, u32[]{:S(2)}) collective-permute-start(f32[3,64,128]{2,1,0:T(8,128)S(1)} %get-tuple-element.23), channel_id=1, source_target_pairs={{0,128},{1,129},{2,130},{3,131},{4,132},{5,133},{6,134},{7,135},{8... | collective-permute-start | bytes 294920 | tf_op jit(solution)/shard_map/ppermute | solution.py:46
  93.3 14.1 %collective-permute-start.30 = (bf16[8,64,128]{2,1,0:T(8,128)(2,1)S(1)}, bf16[8,64,128]{2,1,0:T(8,128)(2,1)S(1)}, u32[]{:S(2)}, u32[]{:S(2)}) collective-permute-start(bf16[8,64,128]{2,1,0:T(8,128)(2,1)S(1)} %get-tuple-element.36), channel_id=1, source_target_pairs={{0,5},{1,6},{2,7},{3,0},{4,1},{5,2},{6,3},{7,4},{8,11},{9,12},{10,... | collective-permute-start | bytes 393224 | tf_op jit(solution)/shard_map/ppermute | solution.py:46
  97.2 14.0 %collective-permute-start.31 = (bf16[8,64,128]{2,1,0:T(8,128)(2,1)S(1)}, bf16[8,64,128]{2,1,0:T(8,128)(2,1)S(1)}, u32[]{:S(2)}, u32[]{:S(2)}) collective-permute-start(bf16[8,64,128]{2,1,0:T(8,128)(2,1)S(1)} %get-tuple-element.35), channel_id=1, source_target_pairs={{0,3},{1,4},{2,5},{3,6},{4,7},{5,0},{6,1},{7,2},{8,13},{9,14},{10,... | collective-permute-start | bytes 393224 | tf_op jit(solution)/shard_map/ppermute | solution.py:46
  98.0 13.2 %collective-permute-start.34 = (bf16[8,64,128]{2,1,0:T(8,128)(2,1)S(1)}, bf16[8,64,128]{2,1,0:T(8,128)(2,1)S(1)}, u32[]{:S(2)}, u32[]{:S(2)}) collective-permute-start(bf16[8,64,128]{2,1,0:T(8,128)(2,1)S(1)} %get-tuple-element.34), channel_id=1, source_target_pairs={{0,5},{1,6},{2,7},{3,0},{4,1},{5,2},{6,3},{7,4},{8,11},{9,12},{10,... | collective-permute-start | bytes 393224 | tf_op jit(solution)/shard_map/ppermute | solution.py:46
  101.8 16.6 %collective-permute-start.35 = (bf16[8,64,128]{2,1,0:T(8,128)(2,1)S(1)}, bf16[8,64,128]{2,1,0:T(8,128)(2,1)S(1)}, u32[]{:S(2)}, u32[]{:S(2)}) collective-permute-start(bf16[8,64,128]{2,1,0:T(8,128)(2,1)S(1)} %get-tuple-element.33), channel_id=1, source_target_pairs={{0,3},{1,4},{2,5},{3,6},{4,7},{5,0},{6,1},{7,2},{8,13},{9,14},{10,... | collective-permute-start | bytes 393224 | tf_op jit(solution)/shard_map/ppermute | solution.py:46
  102.6 3.8 %collective-permute-start.27 = (f32[3,64,128]{2,1,0:T(8,128)S(1)}, f32[3,64,128]{2,1,0:T(8,128)S(1)}, u32[]{:S(2)}, u32[]{:S(2)}) collective-permute-start(f32[3,64,128]{2,1,0:T(8,128)S(1)} %get-tuple-element.23), channel_id=1, source_target_pairs={{0,192},{1,193},{2,194},{3,195},{4,196},{5,197},{6,198},{7,199},{8... | collective-permute-start | bytes 294920 | tf_op jit(solution)/shard_map/ppermute | solution.py:46

commit v3 on v2

--- a/solution.py
+++ b/solution.py
@@ -46,10 +46,10 @@
     return lax.ppermute(array, BOTH, perm)
 
 
-def energy_kernel(slots, times, ret_ref, mir_ref, out_ref):
+def energy_kernel(skip, slots, times, ret_ref, mir_ref, out_ref):
     orbitals = ret_ref.shape[2]
     slot_count = ret_ref.shape[1]
-    now = times[0] + pl.program_id(0)
+    now = times[0] + skip + pl.program_id(0)
     first_source = times[1]
     low = lax.broadcasted_iota(jnp.int32, (orbitals, 2 * orbitals), 1) < orbitals
     low_row = lax.broadcasted_iota(jnp.int32, (1, 2 * orbitals), 1) < orbitals
@@ -78,17 +78,19 @@
     lax.fori_loop(0, slot_count // 2, pair, 0, unroll=4)
 
 
-def energy_call(retarded, mirrored, slots, times):
+def energy_call(retarded, mirrored, slots, times, part, parts):
     steps, sources, orbitals, width = retarded.shape
+    steps = steps // parts
+    skip = part * steps
     return pl.pallas_call(
-        energy_kernel,
+        lambda *refs: energy_kernel(skip, *refs),
         out_shape=jax.ShapeDtypeStruct((steps, 2, orbitals, sources * orbitals), jnp.bfloat16),
         grid_spec=pltpu.PrefetchScalarGridSpec(
             num_scalar_prefetch=2,
             grid=(steps,),
             in_specs=[
-                pl.BlockSpec((1, sources, orbitals, width), lambda t, *_: (t, 0, 0, 0)),
-                pl.BlockSpec((sources, 1, orbitals, width), lambda t, *_: (0, t, 0, 0)),
+                pl.BlockSpec((1, sources, orbitals, width), lambda t, *_: (t + skip, 0, 0, 0)),
+                pl.BlockSpec((sources, 1, orbitals, width), lambda t, *_: (0, t + skip, 0, 0)),
             ],
             out_specs=pl.BlockSpec(
                 (1, 2, orbitals, sources * orbitals), lambda t, *_: (t, 0, 0, 0)
@@ -113,8 +115,10 @@
 
 
 def product_call(norm, cols, energy, factors, panels, kinds, even_ends=None):
-    steps, _, orbitals, depth = energy.shape
+    steps = sum(part.shape[0] for part in energy)
+    _, _, orbitals, depth = energy[0].shape
     width = 2 * orbitals
+    runs = len(energy)
     shape = [jax.ShapeDtypeStruct((count, steps, orbitals, width), kind) for count, kind in kinds]
     places = [(n, at) for n, (count, _) in enumerate(kinds) for at in range(count)]
     pieces, tiles = len(panels), len(places)
@@ -130,10 +134,11 @@
         extra = [even_ends]
     packed = [(0, 0), (0, 1), (0, 2), (1, 0), (1, 1), (2, 0), (2, 1), (2, 2)]
 
-    def body(cols_ref, energy_ref, fre_ref, fim_ref, *refs):
+    def body(cols_ref, *refs):
+        energy_refs, (fre_ref, fim_ref), refs = refs[:runs], refs[runs : runs + 2], refs[runs + 2 :]
         even_refs, refs = refs[: len(extra)], refs[len(extra) :]
         panel_refs, out_refs = refs[: tiles * pieces], refs[tiles * pieces :]
-        left = energy_ref[...].reshape(steps * 2 * orbitals, depth)
+        left = jnp.concatenate([ref[...].reshape(-1, depth) for ref in energy_refs], axis=0)
         right = jnp.concatenate(
             [
                 jnp.concatenate(
@@ -172,7 +177,7 @@
         grid_spec=pltpu.PrefetchScalarGridSpec(
             num_scalar_prefetch=1,
             grid=(1,),
-            in_specs=[pl.BlockSpec(memory_space=pltpu.VMEM)] * (3 + len(extra))
+            in_specs=[pl.BlockSpec(memory_space=pltpu.VMEM)] * (runs + 2 + len(extra))
             + [panel_spec(panel, tile) for tile in range(tiles) for panel in panels],
             out_specs=[pl.BlockSpec(memory_space=pltpu.VMEM)] * len(shape),
         ),
@@ -182,7 +187,7 @@
             bytes_accessed=2 * depth * (steps * 2 * orbitals + tiles * width),
             transcendentals=0,
         ),
-    )(cols, energy, *factors, *extra, *(panels * tiles))
+    )(cols, *energy, *factors, *extra, *(panels * tiles))
 
 
 def sum_kernel(own_ref, ahead_ref, back_ref, from5_ref, from3_ref, sum_ref):
@@ -325,7 +330,9 @@
 
 
 def near_line(local):
-    moved = [local] + [send(local, plane_perm(-off, True)) for off in OFFSETS[1:]]
+    moved = [local]
+    for off in OFFSETS[1:]:
+        moved.append(send(local, plane_perm(-off, True)))
     return [jnp.concatenate([m[chunk] for m in moved], axis=0) for chunk in range(2)]
 
 
@@ -391,7 +398,10 @@
     local = jnp.moveaxis(lesser_panel.reshape(orbitals, panels // 2, 2, width), 2, 0)
     local = local.reshape(2, orbitals, panels // 2 * width)
     times = jnp.stack([row_index * steps, col_index * sources]).astype(jnp.int32)
-    energy = energy_call(retarded, mirrored, slot_table(row_index), times)
+    slots = slot_table(row_index)
+    energy = []
+    for part in range(2):
+        energy.append(energy_call(retarded, mirrored, slots, times, part, 2))
 
     def cols_of(rels):
         return ((col_index + way * jnp.array(rels, jnp.int32)) % Z).astype(jnp.int32)
@@ -408,7 +418,9 @@
     line0, line1 = near_line(local)
     blocks0 = far_blocks(line0)
     blocks1 = far_blocks(line1)
-    panels0 = blocks0 + [send(block, CORE_SWAP) for block in blocks0]
+    panels0 = list(blocks0)
+    for block in blocks0:
+        panels0.append(send(block, CORE_SWAP))
     factors = (fre, fim)
     *terms0, own0, rest0, ends0 = column_product(norm, cols_of, energy, factors, panels0)
     parts0 = column_sum(*terms0, rest0)

time: 120 us -> 121 us (level)
    pallas_call x1 -> x2, Pallas kernels: 9.28 us -> 10.5 us  [energy_call(): pl.pallas_call(lambda *refs: energy_kernel(skip, *refs), out_shape=jax.Sh...]
  transfers between devices with their start and end apart: 36 -> 36, of which waited for: 16 -> 16; matrix products, arithmetic and copies ran while one was open for 2% -> 2% of each run, Pallas kernels for 16% -> 17%
where the time goes in v3:
time: 121 us
  starting transfers between devices  49.8 us (41%)
  waiting for transfers between devices  39.6 us (33%)
  Pallas kernels  28.1 us (23%)
  local copies, waits for them, and re-layouts  1.74 us (1%)
  other arithmetic  1.46 us (1%)
    ppermute x36, starting transfers between devices, send(): return lax.ppermute(array, BOTH, perm)  49.8 us
    ppermute x36, waiting for transfers between devices, send(): return lax.ppermute(array, BOTH, perm)  39.6 us
    pallas_call x2, Pallas kernels, product_call(): pl.pallas_call(body, out_shape=shape, grid_spec=pltpu.PrefetchScalarGridS...  12.8 us
    pallas_call x2, Pallas kernels, energy_call(): pl.pallas_call(lambda *refs: energy_kernel(skip, *refs), out_shape=jax.Sh...  10.5 us
    pallas_call x6, Pallas kernels, small_call(): pl.pallas_call(kernel, out_shape=out_shape, in_specs=specs, out_specs=out...  4.79 us
  transfers between devices with their start and end apart: 36, of which 16 were waited for; matrix products, arithmetic and copies ran while one was open for 2% of the time, Pallas kernels for 17%

profile of v3, /device:TPU:65, one launch (start us, length us, event | category | flops | bytes accessed | tf_op | source)
XLA Modules:
  0.0 121.1 jit_solution(4567967853507308223)
XLA Ops:
  0.0 1.0 copy.18
  1.0 0.1 reshape.62
  1.1 1.4 %collective-permute-start = (bf16[2,64,1024]{2,1,0:T(8,128)(2,1)S(1)}, bf16[2,64,1024]{2,1,0:T(8,128)(2,1)S(1)}, u32[]{:S(2)}, u32[]{:S(2)}) collective-permute-start(bf16[2,64,1024]{2,1,0:T(8,128)(2,1)S(1)} %reshape.62), channel_id=1, source_target_pairs={{0,16},{1,17},{2,18},{3,19},{4,20},{5,21},{6,22},{7,23},{8,72},{9,... | collective-permute-start | bytes 786440 | tf_op jit(solution)/shard_map/ppermute | solution.py:46
  2.5 1.5 %collective-permute-start.1 = (bf16[2,64,1024]{2,1,0:T(8,128)(2,1)S(1)}, bf16[2,64,1024]{2,1,0:T(8,128)(2,1)S(1)}, u32[]{:S(2)}, u32[]{:S(2)}) collective-permute-start(bf16[2,64,1024]{2,1,0:T(8,128)(2,1)S(1)} %reshape.62), channel_id=1, source_target_pairs={{0,48},{1,49},{2,50},{3,51},{4,52},{5,53},{6,54},{7,55},{8,200},{9... | collective-permute-start | bytes 786440 | tf_op jit(solution)/shard_map/ppermute | solution.py:46
  4.0 1.6 %collective-permute-start.2 = (bf16[2,64,1024]{2,1,0:T(8,128)(2,1)S(1)}, bf16[2,64,1024]{2,1,0:T(8,128)(2,1)S(1)}, u32[]{:S(2)}, u32[]{:S(2)}) collective-permute-start(bf16[2,64,1024]{2,1,0:T(8,128)(2,1)S(1)} %reshape.62), channel_id=1, source_target_pairs={{0,32},{1,33},{2,34},{3,35},{4,36},{5,37},{6,38},{7,39},{8,136},{9... | collective-permute-start | bytes 786440 | tf_op jit(solution)/shard_map/ppermute | solution.py:46
  5.6 0.8 select_add_fusion.3
  6.4 0.1 add.142
  6.9 1.1 collective-permute-done
  8.0 2.1 %collective-permute-done.1 = bf16[2,64,1024]{2,1,0:T(8,128)(2,1)S(1)} collective-permute-done((bf16[2,64,1024]{2,1,0:T(8,128)(2,1)S(1)}, bf16[2,64,1024]{2,1,0:T(8,128)(2,1)S(1)}, u32[]{:S(2)}, u32[]{:S(2)}) %collective-permute-start.1) | collective-permute-done | bytes 262176 | tf_op jit(solution)/shard_map/ppermute | solution.py:46
  10.2 1.8 %collective-permute-done.2 = bf16[2,64,1024]{2,1,0:T(8,128)(2,1)S(1)} collective-permute-done((bf16[2,64,1024]{2,1,0:T(8,128)(2,1)S(1)}, bf16[2,64,1024]{2,1,0:T(8,128)(2,1)S(1)}, u32[]{:S(2)}, u32[]{:S(2)}) %collective-permute-start.2) | collective-permute-done | bytes 262176 | tf_op jit(solution)/shard_map/ppermute | solution.py:46
  12.0 1.0 collective-permute-start.3
  13.0 1.8 %collective-permute-start.4 = (bf16[256,1024]{1,0:T(8,128)(2,1)S(1)}, bf16[256,1024]{1,0:T(8,128)(2,1)S(1)}, u32[]{:S(2)}, u32[]{:S(2)}) collective-permute-start(bf16[256,1024]{1,0:T(8,128)(2,1)S(1)} %pad_maximum_fusion.refs_4_.refs_12_.refs_20_.refs_28_.refs_36_.refs_44_.refs_52_.refs_60_), channel_id=1, source_target_pairs={{0,192},{1,193},{2,194},{3,195},{4,196},{5,197},{6,198},{7,199},{8... | collective-permute-start | bytes 1572872 | tf_op jit(solution)/shard_map/ppermute | solution.py:46
  14.8 1.2 %collective-permute-start.5 = (bf16[256,1024]{1,0:T(8,128)(2,1)S(1)}, bf16[256,1024]{1,0:T(8,128)(2,1)S(1)}, u32[]{:S(2)}, u32[]{:S(2)}) collective-permute-start(bf16[256,1024]{1,0:T(8,128)(2,1)S(1)} %pad_maximum_fusion.refs_4_.refs_12_.refs_20_.refs_28_.refs_36_.refs_44_.refs_52_.refs_60_), channel_id=1, source_target_pairs={{0,128},{1,129},{2,130},{3,131},{4,132},{5,133},{6,134},{7,135},{8... | collective-permute-start | bytes 1572872 | tf_op jit(solution)/shard_map/ppermute | solution.py:46
  16.0 2.6 %collective-permute-start.6 = (bf16[256,1024]{1,0:T(8,128)(2,1)S(1)}, bf16[256,1024]{1,0:T(8,128)(2,1)S(1)}, u32[]{:S(2)}, u32[]{:S(2)}) collective-permute-start(bf16[256,1024]{1,0:T(8,128)(2,1)S(1)} %pad_maximum_fusion.refs_4_.refs_12_.refs_20_.refs_28_.refs_36_.refs_44_.refs_52_.refs_60_), channel_id=1, source_target_pairs={{0,8},{1,9},{2,10},{3,11},{4,12},{5,13},{6,14},{7,15},{8,0},{9,1},... | collective-permute-start | bytes 1572872 | tf_op jit(solution)/shard_map/ppermute | solution.py:46
  18.7 1.2 %collective-permute-start.10 = (bf16[256,1024]{1,0:T(8,128)(2,1)S(1)}, bf16[256,1024]{1,0:T(8,128)(2,1)S(1)}, u32[]{:S(2)}, u32[]{:S(2)}) collective-permute-start(bf16[256,1024]{1,0:T(8,128)(2,1)S(1)} %pad_maximum_fusion.1.refs_5_.refs_13_.refs_21_.refs_29_.refs_37_.refs_45_.refs_53_.refs_61_), channel_id=1, source_target_pairs={{0,64},{1,65},{2,66},{3,67},{4,68},{5,69},{6,70},{7,71},{8,24},{9,... | collective-permute-start | bytes 1572872 | tf_op jit(solution)/shard_map/ppermute | solution.py:46
  20.0 5.3 %shard_map.92.refs_1_ = bf16[4,2,64,2048]{3,2,1,0:T(8,128)(2,1)S(1)} custom-call(s32[32]{0:T(128)S(1)} %pad_add_fusion.1.refs_0_, s32[2]{0:T(128)S(1)} %pad_add_fusion.2.refs_1_, bf16[8,32,64,128]{3,2,1,0:T(8,128)(2,1)} %refs_2_.3, bf16[32,8,64,128]{3,2,1,0:T(8,128)(2,1)} %refs_3_.3), custom_call_target="tpu_custom_call" | custom-call | flops 20971520 | bytes 6291456 | tf_op jit(solution)/shard_map/pallas_call | solution.py:85
  25.3 5.3 %shard_map.91.refs_0_ = bf16[4,2,64,2048]{3,2,1,0:T(8,128)(2,1)S(1)} custom-call(s32[32]{0:T(128)S(1)} %pad_add_fusion.1.refs_0_, s32[2]{0:T(128)S(1)} %pad_add_fusion.2.refs_1_, bf16[8,32,64,128]{3,2,1,0:T(8,128)(2,1)} %refs_2_.3, bf16[32,8,64,128]{3,2,1,0:T(8,128)(2,1)} %refs_3_.3), custom_call_target="tpu_custom_call" | custom-call | flops 20971520 | bytes 6291456 | tf_op jit(solution)/shard_map/pallas_call | solution.py:85
  30.7 1.6 %collective-permute-start.11 = (bf16[256,1024]{1,0:T(8,128)(2,1)S(1)}, bf16[256,1024]{1,0:T(8,128)(2,1)S(1)}, u32[]{:S(2)}, u32[]{:S(2)}) collective-permute-start(bf16[256,1024]{1,0:T(8,128)(2,1)S(1)} %pad_maximum_fusion.1.refs_5_.refs_13_.refs_21_.refs_29_.refs_37_.refs_45_.refs_53_.refs_61_), channel_id=1, source_target_pairs={{0,192},{1,193},{2,194},{3,195},{4,196},{5,197},{6,198},{7,199},{8... | collective-permute-start | bytes 1572872 | tf_op jit(solution)/shard_map/ppermute | solution.py:46
  32.3 0.6 collective-permute-start.12
  32.9 0.3 collective-permute-start.7
  33.2 0.2 collective-permute-start.8
  33.4 0.5 collective-permute-done.10.refs_6_.refs_14_.refs_22_.refs_30_.refs_38_.refs_46_.refs_54_.refs_62_
  33.9 1.1 collective-permute-start.9
  35.0 0.1 broadcast_multiply_fusion.refs_3_.fim_ref
  35.2 8.9 %collective-permute-done.11.refs_7_.refs_15_.refs_23_.refs_31_.refs_39_.refs_47_.refs_55_.refs_63_ = bf16[256,1024]{1,0:T(8,128)(2,1)S(1)} collective-permute-done((bf16[256,1024]{1,0:T(8,128)(2,1)S(1)}, bf16[256,1024]{1,0:T(8,128)(2,1)S(1)}, u32[]{:S(2)}, u32[]{:S(2)}) %collective-permute-start.11) | collective-permute-done | bytes 524320 | tf_op jit(solution)/shard_map/ppermute | solution.py:46
  44.0 1.2 collective-permute-start.13
  45.2 0.5 collective-permute-start.15
  45.7 0.3 collective-permute-start.16
  46.0 0.1 broadcast_in_dim.12.refs_2_.fre_ref
  46.1 6.4 %shard_map.93 = (bf16[3,8,64,128]{3,2,1,0:T(8,128)(2,1)S(1)}, bf16[2,8,64,128]{3,2,1,0:T(8,128)(2,1)S(1)}, f32[1,8,64,128]{3,2,1,0:T(8,128)S(1)}, f32[2,8,64,128]{3,2,1,0:T(8,128)S(1)}, f32[8,64,128]{2,1,0:T(8,128)S(1)}) custom-call(s32[8]{0:T(128)S(1)} %and_select_fusion.4.cols_ref, bf16[4,2,64,2048]{3,2,1,0:T(8,128)(2,1)S(1)} %shard_map.91.refs_0_, ...), custom_call_target="tpu_custom_call" | custom-call | flops 4294967296 | bytes 8388608 | tf_op jit(solution)/shard_map/pallas_call | solution.py:174
  52.6 6.4 %shard_map.94 = (bf16[3,8,64,128]{3,2,1,0:T(8,128)(2,1)S(1)}, bf16[2,8,64,128]{3,2,1,0:T(8,128)(2,1)S(1)}, f32[1,8,64,128]{3,2,1,0:T(8,128)S(1)}, f32[2,8,64,128...) custom-call(s32[8]{0:T(128)S(1)} %and_select_fusion.4.cols_ref, ...), custom_call_target="tpu_custom_call" | custom-call | flops 4294967296 | bytes 8388608 | tf_op jit(solution)/shard_map/pallas_call | solution.py:174
  59.1 1.7 %collective-permute-start.18 = (bf16[2,2,64,128]{3,2,1,0:T(8,128)(2,1)S(1)}, bf16[2,2,64,128]{3,2,1,0:T(8,128)(2,1)S(1)}, u32[]{:S(2)}, u32[]{:S(2)}) collective-permute-start(bf16[2,2,64,128]{3,2,1,0:T(8,128)(2,1)S(1)} %get-tuple-element.22), channel_id=1, source_target_pairs={{0,7},{1,0},{2,1},{3,2},{4,3},{5,4},{6,5},{7,6},{8,9},{9,10},{10,1... | collective-permute-start | bytes 196616 | tf_op jit(solution)/shard_map/ppermute | solution.py:46
  60.8 1.9 %collective-permute-done.18.back_ref = bf16[2,2,64,128]{3,2,1,0:T(8,128)(2,1)S(1)} collective-permute-done((bf16[2,2,64,128]{3,2,1,0:T(8,128)(2,1)S(1)}, bf16[2,2,64,128]{3,2,1,0:T(8,128)(2,1)S(1)}, u32[]{:S(2)}, u32[]{:S(2)}) %collective-permute-start.18) | collective-permute-done | bytes 65568 | tf_op jit(solution)/shard_map/ppermute | solution.py:46
  62.7 0.3 collective-permute-done.17.ahead_ref
  63.1 5.6 %collective-permute-start.19 = (bf16[2,64,128]{2,1,0:T(8,128)(2,1)S(1)}, bf16[2,64,128]{2,1,0:T(8,128)(2,1)S(1)}, u32[]{:S(2)}, u32[]{:S(2)}) collective-permute-start(bf16[2,64,128]{2,1,0:T(8,128)(2,1)S(1)} %get-tuple-element.38), channel_id=1, source_target_pairs={{0,5},{1,6},{2,7},{3,0},{4,1},{5,2},{6,3},{7,4},{8,11},{9,12},{10,... | collective-permute-start | bytes 98312 | tf_op jit(solution)/shard_map/ppermute | solution.py:46
  68.7 0.5 collective-permute-start.20
  69.2 0.6 collective-permute-start.29
  69.7 1.0 collective-permute-done.19.from5_ref
  70.8 4.7 %collective-permute-done.20.from3_ref = bf16[2,64,128]{2,1,0:T(8,128)(2,1)S(1)} collective-permute-done((bf16[2,64,128]{2,1,0:T(8,128)(2,1)S(1)}, bf16[2,64,128]{2,1,0:T(8,128)(2,1)S(1)}, u32[]{:S(2)}, u32[]{:S(2)}) %collective-permute-start.20) | collective-permute-done | bytes 32800 | tf_op jit(solution)/shard_map/ppermute | solution.py:46
  75.4 0.6 shard_map.95.own_ref
  76.0 1.9 %collective-permute-start.21 = (f32[3,64,128]{2,1,0:T(8,128)S(1)}, f32[3,64,128]{2,1,0:T(8,128)S(1)}, u32[]{:S(2)}, u32[]{:S(2)}) collective-permute-start(f32[3,64,128]{2,1,0:T(8,128)S(1)} %shard_map.95.own_ref), channel_id=1, source_target_pairs={{0,8},{1,9},{2,10},{3,11},{4,12},{5,13},{6,14},{7,15},{8,0},{9,1},... | collective-permute-start | bytes 294920 | tf_op jit(solution)/shard_map/ppermute | solution.py:46
  78.0 0.9 collective-permute-done.21.other_ref.core_ref
  78.9 0.6 shard_map.96.own_ref
  79.5 1.2 %collective-permute-start.22 = (f32[3,64,128]{2,1,0:T(8,128)S(1)}, f32[3,64,128]{2,1,0:T(8,128)S(1)}, u32[]{:S(2)}, u32[]{:S(2)}) collective-permute-start(f32[3,64,128]{2,1,0:T(8,128)S(1)} %shard_map.96.own_ref), channel_id=1, source_target_pairs={{0,16},{1,17},{2,18},{3,19},{4,20},{5,21},{6,22},{7,23},{8,24},{9,... | collective-permute-start | bytes 294920 | tf_op jit(solution)/shard_map/ppermute | solution.py:46
  80.7 1.4 %collective-permute-start.32 = (bf16[3,8,64,128]{3,2,1,0:T(8,128)(2,1)S(1)}, bf16[3,8,64,128]{3,2,1,0:T(8,128)(2,1)S(1)}, u32[]{:S(2)}, u32[]{:S(2)}) collective-permute-start(bf16[3,8,64,128]{3,2,1,0:T(8,128)(2,1)S(1)} %get-tuple-element.30), channel_id=1, source_target_pairs={{0,1},{1,2},{2,3},{3,4},{4,5},{5,6},{6,7},{7,0},{8,15},{9,8},{10,9... | collective-permute-start | bytes 1179656 | tf_op jit(solution)/shard_map/ppermute | solution.py:46
  82.2 2.3 %collective-permute-start.23 = (f32[3,64,128]{2,1,0:T(8,128)S(1)}, f32[3,64,128]{2,1,0:T(8,128)S(1)}, u32[]{:S(2)}, u32[]{:S(2)}) collective-permute-start(f32[3,64,128]{2,1,0:T(8,128)S(1)} %shard_map.96.own_ref), channel_id=1, source_target_pairs={{0,32},{1,33},{2,34},{3,35},{4,36},{5,37},{6,38},{7,39},{8,40},{9,... | collective-permute-start | bytes 294920 | tf_op jit(solution)/shard_map/ppermute | solution.py:46
  84.4 0.4 collective-permute-done.22.d1_ref
  84.8 0.9 collective-permute-start.24
  85.8 2.5 %collective-permute-done.23.d2_ref = f32[3,64,128]{2,1,0:T(8,128)S(1)} collective-permute-done((f32[3,64,128]{2,1,0:T(8,128)S(1)}, f32[3,64,128]{2,1,0:T(8,128)S(1)}, u32[]{:S(2)}, u32[]{:S(2)}) %collective-permute-start.23) | collective-permute-done | bytes 98336 | tf_op jit(solution)/shard_map/ppermute | solution.py:46
  88.2 0.4 collective-permute-done.24.d3_ref
  88.7 1.1 shard_map.97
  89.8 0.9 collective-permute-start.25
  90.6 3.8 %collective-permute-start.26 = (f32[3,64,128]{2,1,0:T(8,128)S(1)}, f32[3,64,128]{2,1,0:T(8,128)S(1)}, u32[]{:S(2)}, u32[]{:S(2)}) collective-permute-start(f32[3,64,128]{2,1,0:T(8,128)S(1)} %get-tuple-element.23), channel_id=1, source_target_pairs={{0,128},{1,129},{2,130},{3,131},{4,132},{5,133},{6,134},{7,135},{8... | collective-permute-start | bytes 294920 | tf_op jit(solution)/shard_map/ppermute | solution.py:46
  94.4 0.1 fusion.1
  94.5 3.9 %collective-permute-start.30 = (bf16[8,64,128]{2,1,0:T(8,128)(2,1)S(1)}, bf16[8,64,128]{2,1,0:T(8,128)(2,1)S(1)}, u32[]{:S(2)}, u32[]{:S(2)}) collective-permute-start(bf16[8,64,128]{2,1,0:T(8,128)(2,1)S(1)} %get-tuple-element.36), channel_id=1, source_target_pairs={{0,5},{1,6},{2,7},{3,0},{4,1},{5,2},{6,3},{7,4},{8,11},{9,12},{10,... | collective-permute-start | bytes 393224 | tf_op jit(solution)/shard_map/ppermute | solution.py:46
  98.4 0.7 collective-permute-start.31
  99.3 3.8 %collective-permute-start.34 = (bf16[8,64,128]{2,1,0:T(8,128)(2,1)S(1)}, bf16[8,64,128]{2,1,0:T(8,128)(2,1)S(1)}, u32[]{:S(2)}, u32[]{:S(2)}) collective-permute-start(bf16[8,64,128]{2,1,0:T(8,128)(2,1)S(1)} %get-tuple-element.34), channel_id=1, source_target_pairs={{0,5},{1,6},{2,7},{3,0},{4,1},{5,2},{6,3},{7,4},{8,11},{9,12},{10,... | collective-permute-start | bytes 393224 | tf_op jit(solution)/shard_map/ppermute | solution.py:46
  103.1 0.7 collective-permute-start.35
  103.8 1.6 %collective-permute-start.27 = (f32[3,64,128]{2,1,0:T(8,128)S(1)}, f32[3,64,128]{2,1,0:T(8,128)S(1)}, u32[]{:S(2)}, u32[]{:S(2)}) collective-permute-start(f32[3,64,128]{2,1,0:T(8,128)S(1)} %get-tuple-element.23), channel_id=1, source_target_pairs={{0,192},{1,193},{2,194},{3,195},{4,196},{5,197},{6,198},{7,199},{8... | collective-permute-start | bytes 294920 | tf_op jit(solution)/shard_map/ppermute | solution.py:46
  105.5 2.1 %collective-permute-done.27.d3_ref = f32[3,64,128]{2,1,0:T(8,128)S(1)} collective-permute-done((f32[3,64,128]{2,1,0:T(8,128)S(1)}, f32[3,64,128]{2,1,0:T(8,128)S(1)}, u32[]{:S(2)}, u32[]{:S(2)}) %collective-permute-start.27) | collective-permute-done | bytes 98336 | tf_op jit(solution)/shard_map/ppermute | solution.py:46
  107.6 1.0 shard_map.98.enter_ref
  108.6 3.9 %collective-permute-done.31.from3_ref = bf16[8,64,128]{2,1,0:T(8,128)(2,1)S(1)} collective-permute-done((bf16[8,64,128]{2,1,0:T(8,128)(2,1)S(1)}, bf16[8,64,128]{2,1,0:T(8,128)(2,1)S(1)}, u32[]{:S(2)}, u32[]{:S(2)}) %collective-permute-start.31) | collective-permute-done | bytes 131104 | tf_op jit(solution)/shard_map/ppermute | solution.py:46
  112.6 7.2 %collective-permute-done.35.from3_ref = bf16[8,64,128]{2,1,0:T(8,128)(2,1)S(1)} collective-permute-done((bf16[8,64,128]{2,1,0:T(8,128)(2,1)S(1)}, bf16[8,64,128]{2,1,0:T(8,128)(2,1)S(1)}, u32[]{:S(2)}, u32[]{:S(2)}) %collective-permute-start.35) | collective-permute-done | bytes 131104 | tf_op jit(solution)/shard_map/ppermute | solution.py:46
  119.7 1.4 %shard_map.100 = f32[8,64,2,128]{3,2,1,0:T(2,128)} custom-call(f32[8,64,128]{2,1,0:T(8,128)S(1)} %broadcast_in_dim.12.refs_2_.fre_ref, f32[8,64,128]{2,1,0:T(8,128)S(1)} %broadcast_multiply_fusion.refs_3_.fim_ref, f32[2,64,128]{2,1,0:T(8,128)S(1)} %shard_map.98.enter_ref, f32[8,64,128]{2,1,0:T(8,128)S(1)} %shard_map.99.even_ref, ...), custom_call_target="tpu_custom_call" | custom-call | flops 1000000 | bytes 1048576 | tf_op jit(solution)/shard_map/pallas_call | solution.py:322
  (55 shorter events, 1.1 us)
Async XLA Ops:
  1.1 6.9 %collective-permute-start = (bf16[2,64,1024]{2,1,0:T(8,128)(2,1)S(1)}, bf16[2,64,1024]{2,1,0:T(8,128)(2,1)S(1)}, u32[]{:S(2)}, u32[]{:S(2)}) collective-permute-start(bf16[2,64,1024]{2,1,0:T(8,128)(2,1)S(1)} %reshape.62), channel_id=1, source_target_pairs={{0,16},{1,17},{2,18},{3,19},{4,20},{5,21},{6,22},{7,23},{8,72},{9,... | collective-permute-start | bytes 786440 | tf_op jit(solution)/shard_map/ppermute | solution.py:46
  2.5 7.7 %collective-permute-start.1 = (bf16[2,64,1024]{2,1,0:T(8,128)(2,1)S(1)}, bf16[2,64,1024]{2,1,0:T(8,128)(2,1)S(1)}, u32[]{:S(2)}, u32[]{:S(2)}) collective-permute-start(bf16[2,64,1024]{2,1,0:T(8,128)(2,1)S(1)} %reshape.62), channel_id=1, source_target_pairs={{0,48},{1,49},{2,50},{3,51},{4,52},{5,53},{6,54},{7,55},{8,200},{9... | collective-permute-start | bytes 786440 | tf_op jit(solution)/shard_map/ppermute | solution.py:46
  4.0 8.0 %collective-permute-start.2 = (bf16[2,64,1024]{2,1,0:T(8,128)(2,1)S(1)}, bf16[2,64,1024]{2,1,0:T(8,128)(2,1)S(1)}, u32[]{:S(2)}, u32[]{:S(2)}) collective-permute-start(bf16[2,64,1024]{2,1,0:T(8,128)(2,1)S(1)} %reshape.62), channel_id=1, source_target_pairs={{0,32},{1,33},{2,34},{3,35},{4,36},{5,37},{6,38},{7,39},{8,136},{9... | collective-permute-start | bytes 786440 | tf_op jit(solution)/shard_map/ppermute | solution.py:46
  12.0 18.6 %collective-permute-start.3 = (bf16[256,1024]{1,0:T(8,128)(2,1)S(1)}, bf16[256,1024]{1,0:T(8,128)(2,1)S(1)}, u32[]{:S(2)}, u32[]{:S(2)}) collective-permute-start(bf16[256,1024]{1,0:T(8,128)(2,1)S(1)} %pad_maximum_fusion.refs_4_.refs_12_.refs_20_.refs_28_.refs_36_.refs_44_.refs_52_.refs_60_), channel_id=1, source_target_pairs={{0,64},{1,65},{2,66},{3,67},{4,68},{5,69},{6,70},{7,71},{8,24},{9,... | collective-permute-start | bytes 1572872 | tf_op jit(solution)/shard_map/ppermute | solution.py:46
  13.0 19.2 %collective-permute-start.4 = (bf16[256,1024]{1,0:T(8,128)(2,1)S(1)}, bf16[256,1024]{1,0:T(8,128)(2,1)S(1)}, u32[]{:S(2)}, u32[]{:S(2)}) collective-permute-start(bf16[256,1024]{1,0:T(8,128)(2,1)S(1)} %pad_maximum_fusion.refs_4_.refs_12_.refs_20_.refs_28_.refs_36_.refs_44_.refs_52_.refs_60_), channel_id=1, source_target_pairs={{0,192},{1,193},{2,194},{3,195},{4,196},{5,197},{6,198},{7,199},{8... | collective-permute-start | bytes 1572872 | tf_op jit(solution)/shard_map/ppermute | solution.py:46
  14.8 18.1 %collective-permute-start.5 = (bf16[256,1024]{1,0:T(8,128)(2,1)S(1)}, bf16[256,1024]{1,0:T(8,128)(2,1)S(1)}, u32[]{:S(2)}, u32[]{:S(2)}) collective-permute-start(bf16[256,1024]{1,0:T(8,128)(2,1)S(1)} %pad_maximum_fusion.refs_4_.refs_12_.refs_20_.refs_28_.refs_36_.refs_44_.refs_52_.refs_60_), channel_id=1, source_target_pairs={{0,128},{1,129},{2,130},{3,131},{4,132},{5,133},{6,134},{7,135},{8... | collective-permute-start | bytes 1572872 | tf_op jit(solution)/shard_map/ppermute | solution.py:46
  16.0 17.2 %collective-permute-start.6 = (bf16[256,1024]{1,0:T(8,128)(2,1)S(1)}, bf16[256,1024]{1,0:T(8,128)(2,1)S(1)}, u32[]{:S(2)}, u32[]{:S(2)}) collective-permute-start(bf16[256,1024]{1,0:T(8,128)(2,1)S(1)} %pad_maximum_fusion.refs_4_.refs_12_.refs_20_.refs_28_.refs_36_.refs_44_.refs_52_.refs_60_), channel_id=1, source_target_pairs={{0,8},{1,9},{2,10},{3,11},{4,12},{5,13},{6,14},{7,15},{8,0},{9,1},... | collective-permute-start | bytes 1572872 | tf_op jit(solution)/shard_map/ppermute | solution.py:46
  18.7 15.1 %collective-permute-start.10 = (bf16[256,1024]{1,0:T(8,128)(2,1)S(1)}, bf16[256,1024]{1,0:T(8,128)(2,1)S(1)}, u32[]{:S(2)}, u32[]{:S(2)}) collective-permute-start(bf16[256,1024]{1,0:T(8,128)(2,1)S(1)} %pad_maximum_fusion.1.refs_5_.refs_13_.refs_21_.refs_29_.refs_37_.refs_45_.refs_53_.refs_61_), channel_id=1, source_target_pairs={{0,64},{1,65},{2,66},{3,67},{4,68},{5,69},{6,70},{7,71},{8,24},{9,... | collective-permute-start | bytes 1572872 | tf_op jit(solution)/shard_map/ppermute | solution.py:46
  25.3 5.3 %copy-start.3 = (f32[64]{0:T(128)S(1)}, f32[64]{0:T(128)}, u32[]{:S(2)}) copy-start(f32[64]{0:T(128)} %param.14) | copy-start | bytes 772
  25.3 8.1 %copy-start.1 = (f32[8,64]{1,0:T(8,128)S(1)}, f32[8,64]{1,0:T(8,128)}, u32[]{:S(2)}) copy-start(f32[8,64]{1,0:T(8,128)} %param.13) | copy-start | bytes 6148
  25.3 20.7 %copy-start.2 = (s32[8]{0:T(128)S(1)}, s32[8]{0:T(128)}, u32[]{:S(2)}) copy-start(s32[8]{0:T(128)} %constant.119.clone) | copy-start | bytes 100
  30.7 13.4 %collective-permute-start.11 = (bf16[256,1024]{1,0:T(8,128)(2,1)S(1)}, bf16[256,1024]{1,0:T(8,128)(2,1)S(1)}, u32[]{:S(2)}, u32[]{:S(2)}) collective-permute-start(bf16[256,1024]{1,0:T(8,128)(2,1)S(1)} %pad_maximum_fusion.1.refs_5_.refs_13_.refs_21_.refs_29_.refs_37_.refs_45_.refs_53_.refs_61_), channel_id=1, source_target_pairs={{0,192},{1,193},{2,194},{3,195},{4,196},{5,197},{6,198},{7,199},{8... | collective-permute-start | bytes 1572872 | tf_op jit(solution)/shard_map/ppermute | solution.py:46
  32.3 12.9 %collective-permute-start.12 = (bf16[256,1024]{1,0:T(8,128)(2,1)S(1)}, bf16[256,1024]{1,0:T(8,128)(2,1)S(1)}, u32[]{:S(2)}, u32[]{:S(2)}) collective-permute-start(bf16[256,1024]{1,0:T(8,128)(2,1)S(1)} %pad_maximum_fusion.1.refs_5_.refs_13_.refs_21_.refs_29_.refs_37_.refs_45_.refs_53_.refs_61_), channel_id=1, source_target_pairs={{0,128},{1,129},{2,130},{3,131},{4,132},{5,133},{6,134},{7,135},{8... | collective-permute-start | bytes 1572872 | tf_op jit(solution)/shard_map/ppermute | solution.py:46
  32.9 12.3 %collective-permute-start.7 = (bf16[256,1024]{1,0:T(8,128)(2,1)S(1)}, bf16[256,1024]{1,0:T(8,128)(2,1)S(1)}, u32[]{:S(2)}, u32[]{:S(2)}) collective-permute-start(bf16[256,1024]{1,0:T(8,128)(2,1)S(1)} %collective-permute-done.3.refs_5_.refs_13_.refs_21_.refs_29_.refs_37_.refs_45_.refs_53_.refs_61_), channel_id=1, source_target_pairs={{0,8},{1,9},{2,10},{3,11},{4,12},{5,13},{6,14},{7,15},{8,0},{9,1},... | collective-permute-start | bytes 1572872 | tf_op jit(solution)/shard_map/ppermute | solution.py:46
  33.2 12.5 %collective-permute-start.8 = (bf16[256,1024]{1,0:T(8,128)(2,1)S(1)}, bf16[256,1024]{1,0:T(8,128)(2,1)S(1)}, u32[]{:S(2)}, u32[]{:S(2)}) collective-permute-start(bf16[256,1024]{1,0:T(8,128)(2,1)S(1)} %collective-permute-done.4.refs_6_.refs_14_.refs_22_.refs_30_.refs_38_.refs_46_.refs_54_.refs_62_), channel_id=1, source_target_pairs={{0,8},{1,9},{2,10},{3,11},{4,12},{5,13},{6,14},{7,15},{8,0},{9,1},... | collective-permute-start | bytes 1572872 | tf_op jit(solution)/shard_map/ppermute | solution.py:46
  33.9 12.1 %collective-permute-start.9 = (bf16[256,1024]{1,0:T(8,128)(2,1)S(1)}, bf16[256,1024]{1,0:T(8,128)(2,1)S(1)}, u32[]{:S(2)}, u32[]{:S(2)}) collective-permute-start(bf16[256,1024]{1,0:T(8,128)(2,1)S(1)} %collective-permute-done.5.refs_7_.refs_15_.refs_23_.refs_31_.refs_39_.refs_47_.refs_55_.refs_63_), channel_id=1, source_target_pairs={{0,8},{1,9},{2,10},{3,11},{4,12},{5,13},{6,14},{7,15},{8,0},{9,1},... | collective-permute-start | bytes 1572872 | tf_op jit(solution)/shard_map/ppermute | solution.py:46
  44.0 8.5 %collective-permute-start.13 = (bf16[256,1024]{1,0:T(8,128)(2,1)S(1)}, bf16[256,1024]{1,0:T(8,128)(2,1)S(1)}, u32[]{:S(2)}, u32[]{:S(2)}) collective-permute-start(bf16[256,1024]{1,0:T(8,128)(2,1)S(1)} %pad_maximum_fusion.1.refs_5_.refs_13_.refs_21_.refs_29_.refs_37_.refs_45_.refs_53_.refs_61_), channel_id=1, source_target_pairs={{0,8},{1,9},{2,10},{3,11},{4,12},{5,13},{6,14},{7,15},{8,0},{9,1},... | collective-permute-start | bytes 1572872 | tf_op jit(solution)/shard_map/ppermute | solution.py:46
  45.2 7.4 %collective-permute-start.14 = (bf16[256,1024]{1,0:T(8,128)(2,1)S(1)}, bf16[256,1024]{1,0:T(8,128)(2,1)S(1)}, u32[]{:S(2)}, u32[]{:S(2)}) collective-permute-start(bf16[256,1024]{1,0:T(8,128)(2,1)S(1)} %collective-permute-done.10.refs_6_.refs_14_.refs_22_.refs_30_.refs_38_.refs_46_.refs_54_.refs_62_), channel_id=1, source_target_pairs={{0,8},{1,9},{2,10},{3,11},{4,12},{5,13},{6,14},{7,15},{8,0},{9,1},... | collective-permute-start | bytes 1572872 | tf_op jit(solution)/shard_map/ppermute | solution.py:46
  45.2 7.4 %collective-permute-start.15 = (bf16[256,1024]{1,0:T(8,128)(2,1)S(1)}, bf16[256,1024]{1,0:T(8,128)(2,1)S(1)}, u32[]{:S(2)}, u32[]{:S(2)}) collective-permute-start(bf16[256,1024]{1,0:T(8,128)(2,1)S(1)} %collective-permute-done.11.refs_7_.refs_15_.refs_23_.refs_31_.refs_39_.refs_47_.refs_55_.refs_63_), channel_id=1, source_target_pairs={{0,8},{1,9},{2,10},{3,11},{4,12},{5,13},{6,14},{7,15},{8,0},{9,1},... | collective-permute-start | bytes 1572872 | tf_op jit(solution)/shard_map/ppermute | solution.py:46
  45.7 6.9 %collective-permute-start.16 = (bf16[256,1024]{1,0:T(8,128)(2,1)S(1)}, bf16[256,1024]{1,0:T(8,128)(2,1)S(1)}, u32[]{:S(2)}, u32[]{:S(2)}) collective-permute-start(bf16[256,1024]{1,0:T(8,128)(2,1)S(1)} %collective-permute-done.12.refs_8_.refs_16_.refs_24_.refs_32_.refs_40_.refs_48_.refs_56_.refs_64_), channel_id=1, source_target_pairs={{0,8},{1,9},{2,10},{3,11},{4,12},{5,13},{6,14},{7,15},{8,0},{9,1},... | collective-permute-start | bytes 1572872 | tf_op jit(solution)/shard_map/ppermute | solution.py:46
  59.0 46.5 %copy-start = (f32[64,2,128]{2,1,0:T(2,128)S(1)}, f32[64,2,128]{2,1,0:T(2,128)}, u32[]{:S(2)}) copy-start(f32[64,2,128]{2,1,0:T(2,128)} %param.12) | copy-start | bytes 196612
  59.0 4.0 %collective-permute-start.17 = (bf16[3,2,64,128]{3,2,1,0:T(8,128)(2,1)S(1)}, bf16[3,2,64,128]{3,2,1,0:T(8,128)(2,1)S(1)}, u32[]{:S(2)}, u32[]{:S(2)}) collective-permute-start(bf16[3,2,64,128]{3,2,1,0:T(8,128)(2,1)S(1)} %get-tuple-element.21), channel_id=1, source_target_pairs={{0,1},{1,2},{2,3},{3,4},{4,5},{5,6},{6,7},{7,0},{8,15},{9,8},{10,9... | collective-permute-start | bytes 294920 | tf_op jit(solution)/shard_map/ppermute | solution.py:46
  59.1 3.6 %collective-permute-start.18 = (bf16[2,2,64,128]{3,2,1,0:T(8,128)(2,1)S(1)}, bf16[2,2,64,128]{3,2,1,0:T(8,128)(2,1)S(1)}, u32[]{:S(2)}, u32[]{:S(2)}) collective-permute-start(bf16[2,2,64,128]{3,2,1,0:T(8,128)(2,1)S(1)} %get-tuple-element.22), channel_id=1, source_target_pairs={{0,7},{1,0},{2,1},{3,2},{4,3},{5,4},{6,5},{7,6},{8,9},{9,10},{10,1... | collective-permute-start | bytes 196616 | tf_op jit(solution)/shard_map/ppermute | solution.py:46
  60.8 33.6 %collective-permute-start.28 = (bf16[3,8,64,128]{3,2,1,0:T(8,128)(2,1)S(1)}, bf16[3,8,64,128]{3,2,1,0:T(8,128)(2,1)S(1)}, u32[]{:S(2)}, u32[]{:S(2)}) collective-permute-start(bf16[3,8,64,128]{3,2,1,0:T(8,128)(2,1)S(1)} %get-tuple-element.26), channel_id=1, source_target_pairs={{0,1},{1,2},{2,3},{3,4},{4,5},{5,6},{6,7},{7,0},{8,15},{9,8},{10,9... | collective-permute-start | bytes 1179656 | tf_op jit(solution)/shard_map/ppermute | solution.py:46
  63.1 7.7 %collective-permute-start.19 = (bf16[2,64,128]{2,1,0:T(8,128)(2,1)S(1)}, bf16[2,64,128]{2,1,0:T(8,128)(2,1)S(1)}, u32[]{:S(2)}, u32[]{:S(2)}) collective-permute-start(bf16[2,64,128]{2,1,0:T(8,128)(2,1)S(1)} %get-tuple-element.38), channel_id=1, source_target_pairs={{0,5},{1,6},{2,7},{3,0},{4,1},{5,2},{6,3},{7,4},{8,11},{9,12},{10,... | collective-permute-start | bytes 98312 | tf_op jit(solution)/shard_map/ppermute | solution.py:46
  68.7 6.8 %collective-permute-start.20 = (bf16[2,64,128]{2,1,0:T(8,128)(2,1)S(1)}, bf16[2,64,128]{2,1,0:T(8,128)(2,1)S(1)}, u32[]{:S(2)}, u32[]{:S(2)}) collective-permute-start(bf16[2,64,128]{2,1,0:T(8,128)(2,1)S(1)} %get-tuple-element.37), channel_id=1, source_target_pairs={{0,3},{1,4},{2,5},{3,6},{4,7},{5,0},{6,1},{7,2},{8,13},{9,14},{10,... | collective-permute-start | bytes 98312 | tf_op jit(solution)/shard_map/ppermute | solution.py:46
  69.2 21.5 %collective-permute-start.29 = (bf16[2,8,64,128]{3,2,1,0:T(8,128)(2,1)S(1)}, bf16[2,8,64,128]{3,2,1,0:T(8,128)(2,1)S(1)}, u32[]{:S(2)}, u32[]{:S(2)}) collective-permute-start(bf16[2,8,64,128]{3,2,1,0:T(8,128)(2,1)S(1)} %get-tuple-element.27), channel_id=1, source_target_pairs={{0,7},{1,0},{2,1},{3,2},{4,3},{5,4},{6,5},{7,6},{8,9},{9,10},{10,1... | collective-permute-start | bytes 786440 | tf_op jit(solution)/shard_map/ppermute | solution.py:46
  76.0 2.9 %collective-permute-start.21 = (f32[3,64,128]{2,1,0:T(8,128)S(1)}, f32[3,64,128]{2,1,0:T(8,128)S(1)}, u32[]{:S(2)}, u32[]{:S(2)}) collective-permute-start(f32[3,64,128]{2,1,0:T(8,128)S(1)} %shard_map.95.own_ref), channel_id=1, source_target_pairs={{0,8},{1,9},{2,10},{3,11},{4,12},{5,13},{6,14},{7,15},{8,0},{9,1},... | collective-permute-start | bytes 294920 | tf_op jit(solution)/shard_map/ppermute | solution.py:46
  79.5 5.3 %collective-permute-start.22 = (f32[3,64,128]{2,1,0:T(8,128)S(1)}, f32[3,64,128]{2,1,0:T(8,128)S(1)}, u32[]{:S(2)}, u32[]{:S(2)}) collective-permute-start(f32[3,64,128]{2,1,0:T(8,128)S(1)} %shard_map.96.own_ref), channel_id=1, source_target_pairs={{0,16},{1,17},{2,18},{3,19},{4,20},{5,21},{6,22},{7,23},{8,24},{9,... | collective-permute-start | bytes 294920 | tf_op jit(solution)/shard_map/ppermute | solution.py:46
  80.7 18.4 %collective-permute-start.32 = (bf16[3,8,64,128]{3,2,1,0:T(8,128)(2,1)S(1)}, bf16[3,8,64,128]{3,2,1,0:T(8,128)(2,1)S(1)}, u32[]{:S(2)}, u32[]{:S(2)}) collective-permute-start(bf16[3,8,64,128]{3,2,1,0:T(8,128)(2,1)S(1)} %get-tuple-element.30), channel_id=1, source_target_pairs={{0,1},{1,2},{2,3},{3,4},{4,5},{5,6},{6,7},{7,0},{8,15},{9,8},{10,9... | collective-permute-start | bytes 1179656 | tf_op jit(solution)/shard_map/ppermute | solution.py:46
  82.2 6.1 %collective-permute-start.23 = (f32[3,64,128]{2,1,0:T(8,128)S(1)}, f32[3,64,128]{2,1,0:T(8,128)S(1)}, u32[]{:S(2)}, u32[]{:S(2)}) collective-permute-start(f32[3,64,128]{2,1,0:T(8,128)S(1)} %shard_map.96.own_ref), channel_id=1, source_target_pairs={{0,32},{1,33},{2,34},{3,35},{4,36},{5,37},{6,38},{7,39},{8,40},{9,... | collective-permute-start | bytes 294920 | tf_op jit(solution)/shard_map/ppermute | solution.py:46
  84.8 3.9 %collective-permute-start.24 = (f32[3,64,128]{2,1,0:T(8,128)S(1)}, f32[3,64,128]{2,1,0:T(8,128)S(1)}, u32[]{:S(2)}, u32[]{:S(2)}) collective-permute-start(f32[3,64,128]{2,1,0:T(8,128)S(1)} %shard_map.96.own_ref), channel_id=1, source_target_pairs={{0,48},{1,49},{2,50},{3,51},{4,52},{5,53},{6,54},{7,55},{8,56},{9,... | collective-permute-start | bytes 294920 | tf_op jit(solution)/shard_map/ppermute | solution.py:46
  88.2 10.2 %collective-permute-start.33 = (bf16[2,8,64,128]{3,2,1,0:T(8,128)(2,1)S(1)}, bf16[2,8,64,128]{3,2,1,0:T(8,128)(2,1)S(1)}, u32[]{:S(2)}, u32[]{:S(2)}) collective-permute-start(bf16[2,8,64,128]{3,2,1,0:T(8,128)(2,1)S(1)} %get-tuple-element.31), channel_id=1, source_target_pairs={{0,7},{1,0},{2,1},{3,2},{4,3},{5,4},{6,5},{7,6},{8,9},{9,10},{10,1... | collective-permute-start | bytes 786440 | tf_op jit(solution)/shard_map/ppermute | solution.py:46
  89.8 13.3 %collective-permute-start.25 = (f32[3,64,128]{2,1,0:T(8,128)S(1)}, f32[3,64,128]{2,1,0:T(8,128)S(1)}, u32[]{:S(2)}, u32[]{:S(2)}) collective-permute-start(f32[3,64,128]{2,1,0:T(8,128)S(1)} %get-tuple-element.23), channel_id=1, source_target_pairs={{0,64},{1,65},{2,66},{3,67},{4,68},{5,69},{6,70},{7,71},{8,72},{9,... | collective-permute-start | bytes 294920 | tf_op jit(solution)/shard_map/ppermute | solution.py:46
  90.6 13.2 %collective-permute-start.26 = (f32[3,64,128]{2,1,0:T(8,128)S(1)}, f32[3,64,128]{2,1,0:T(8,128)S(1)}, u32[]{:S(2)}, u32[]{:S(2)}) collective-permute-start(f32[3,64,128]{2,1,0:T(8,128)S(1)} %get-tuple-element.23), channel_id=1, source_target_pairs={{0,128},{1,129},{2,130},{3,131},{4,132},{5,133},{6,134},{7,135},{8... | collective-permute-start | bytes 294920 | tf_op jit(solution)/shard_map/ppermute | solution.py:46
  94.5 14.1 %collective-permute-start.30 = (bf16[8,64,128]{2,1,0:T(8,128)(2,1)S(1)}, bf16[8,64,128]{2,1,0:T(8,128)(2,1)S(1)}, u32[]{:S(2)}, u32[]{:S(2)}) collective-permute-start(bf16[8,64,128]{2,1,0:T(8,128)(2,1)S(1)} %get-tuple-element.36), channel_id=1, source_target_pairs={{0,5},{1,6},{2,7},{3,0},{4,1},{5,2},{6,3},{7,4},{8,11},{9,12},{10,... | collective-permute-start | bytes 393224 | tf_op jit(solution)/shard_map/ppermute | solution.py:46
  98.4 14.1 %collective-permute-start.31 = (bf16[8,64,128]{2,1,0:T(8,128)(2,1)S(1)}, bf16[8,64,128]{2,1,0:T(8,128)(2,1)S(1)}, u32[]{:S(2)}, u32[]{:S(2)}) collective-permute-start(bf16[8,64,128]{2,1,0:T(8,128)(2,1)S(1)} %get-tuple-element.35), channel_id=1, source_target_pairs={{0,3},{1,4},{2,5},{3,6},{4,7},{5,0},{6,1},{7,2},{8,13},{9,14},{10,... | collective-permute-start | bytes 393224 | tf_op jit(solution)/shard_map/ppermute | solution.py:46
  99.3 13.3 %collective-permute-start.34 = (bf16[8,64,128]{2,1,0:T(8,128)(2,1)S(1)}, bf16[8,64,128]{2,1,0:T(8,128)(2,1)S(1)}, u32[]{:S(2)}, u32[]{:S(2)}) collective-permute-start(bf16[8,64,128]{2,1,0:T(8,128)(2,1)S(1)} %get-tuple-element.34), channel_id=1, source_target_pairs={{0,5},{1,6},{2,7},{3,0},{4,1},{5,2},{6,3},{7,4},{8,11},{9,12},{10,... | collective-permute-start | bytes 393224 | tf_op jit(solution)/shard_map/ppermute | solution.py:46
  103.1 16.6 %collective-permute-start.35 = (bf16[8,64,128]{2,1,0:T(8,128)(2,1)S(1)}, bf16[8,64,128]{2,1,0:T(8,128)(2,1)S(1)}, u32[]{:S(2)}, u32[]{:S(2)}) collective-permute-start(bf16[8,64,128]{2,1,0:T(8,128)(2,1)S(1)} %get-tuple-element.33), channel_id=1, source_target_pairs={{0,3},{1,4},{2,5},{3,6},{4,7},{5,0},{6,1},{7,2},{8,13},{9,14},{10,... | collective-permute-start | bytes 393224 | tf_op jit(solution)/shard_map/ppermute | solution.py:46
  103.8 3.8 %collective-permute-start.27 = (f32[3,64,128]{2,1,0:T(8,128)S(1)}, f32[3,64,128]{2,1,0:T(8,128)S(1)}, u32[]{:S(2)}, u32[]{:S(2)}) collective-permute-start(f32[3,64,128]{2,1,0:T(8,128)S(1)} %get-tuple-element.23), channel_id=1, source_target_pairs={{0,192},{1,193},{2,194},{3,195},{4,196},{5,197},{6,198},{7,199},{8... | collective-permute-start | bytes 294920 | tf_op jit(solution)/shard_map/ppermute | solution.py:46

commit v4 on v3

--- a/solution.py
+++ b/solution.py
@@ -137,13 +137,12 @@
     def body(cols_ref, *refs):
         energy_refs, (fre_ref, fim_ref), refs = refs[:runs], refs[runs : runs + 2], refs[runs + 2 :]
         even_refs, refs = refs[: len(extra)], refs[len(extra) :]
-        panel_refs, out_refs = refs[: tiles * pieces], refs[tiles * pieces :]
+        panel_refs, out_refs = refs[:pieces], refs[pieces:]
+        starts = [pl.multiple_of(cols_ref[tile] * width, width) for tile in range(tiles)]
         left = jnp.concatenate([ref[...].reshape(-1, depth) for ref in energy_refs], axis=0)
         right = jnp.concatenate(
             [
-                jnp.concatenate(
-                    [ref[...] for ref in panel_refs[tile * pieces : (tile + 1) * pieces]], axis=0
-                )
+                jnp.concatenate([ref[:, pl.ds(starts[tile], width)] for ref in panel_refs], axis=0)
                 for tile in range(tiles)
             ],
             axis=1,
@@ -168,26 +167,19 @@
                 target[place, 0] = even_refs[0][tile].astype(target.dtype)
                 target[place, 1] = end.astype(target.dtype)
 
-    def panel_spec(panel, tile):
-        return pl.BlockSpec((panel.shape[0], width), lambda n, cols: (0, cols[tile]))
-
+    vmem = pl.BlockSpec(memory_space=pltpu.VMEM)
     return pl.pallas_call(
         body,
         out_shape=shape,
-        grid_spec=pltpu.PrefetchScalarGridSpec(
-            num_scalar_prefetch=1,
-            grid=(1,),
-            in_specs=[pl.BlockSpec(memory_space=pltpu.VMEM)] * (runs + 2 + len(extra))
-            + [panel_spec(panel, tile) for tile in range(tiles) for panel in panels],
-            out_specs=[pl.BlockSpec(memory_space=pltpu.VMEM)] * len(shape),
-        ),
+        in_specs=[pl.BlockSpec(memory_space=pltpu.SMEM)] + [vmem] * (runs + 2 + len(extra) + pieces),
+        out_specs=[vmem] * len(shape),
         compiler_params=pltpu.CompilerParams(vmem_limit_bytes=34 << 20),
         cost_estimate=pl.CostEstimate(
             flops=2 * tiles * steps * 2 * orbitals * depth * width,
             bytes_accessed=2 * depth * (steps * 2 * orbitals + tiles * width),
             transcendentals=0,
         ),
-    )(cols, *energy, *factors, *extra, *(panels * tiles))
+    )(cols, *energy, *factors, *extra, *panels)
 
 
 def sum_kernel(own_ref, ahead_ref, back_ref, from5_ref, from3_ref, sum_ref):
@@ -289,21 +281,31 @@
         total_ref[n] = plane
 
 
-def enter_kernel(where_ref, init_ref, d1_ref, d2_ref, d3_ref, x_ref, core_ref, out_ref):
+def last_kernel(
+    where_ref,
+    fre_ref,
+    fim_ref,
+    init_ref,
+    d1_ref,
+    d2_ref,
+    d3_ref,
+    x_ref,
+    core_ref,
+    even_ref,
+    own_ref,
+    ahead_ref,
+    back_ref,
+    from5_ref,
+    from3_ref,
+    out_ref,
+):
+    steps = fre_ref.shape[0]
     one = unit(init_ref.shape[1:])
     column = before_of(where_ref[2], [read(d1_ref), read(d2_ref), read(d3_ref)], one)
     start = after(column, [init_ref[0], init_ref[1], one[2]])
     start = after(read(x_ref), start)
     start = after(chosen(where_ref[0] == 1, read(core_ref), one), start)
-    for half in range(2):
-        out_ref[half] = start[half]
-
-
-def last_kernel(
-    fre_ref, fim_ref, enter_ref, even_ref, own_ref, ahead_ref, back_ref, from5_ref, from3_ref, out_ref
-):
-    steps = fre_ref.shape[0]
-    even, odd = enter_ref[0], enter_ref[1]
+    even, odd = start[0], start[1]
     for t in range(steps):
         value = own_ref[0, t]
         for arrived in (ahead_ref[2, t], back_ref[1, t], from5_ref[t], from3_ref[t]):
@@ -445,22 +447,16 @@
 
     before_x, line = small_call(line_kernel, (message, message), where, chip, *behind)
     behind = [send(line, column_perm(back)) for back in (1, 2, 3)]
-    entering = small_call(
-        enter_kernel,
-        jax.ShapeDtypeStruct((2, orbitals, width), jnp.float32),
+    return small_call(
+        last_kernel,
+        jax.ShapeDtypeStruct((steps, orbitals, 2, width), jnp.float32),
         where,
+        fre,
+        fim,
         start,
         *behind,
         before_x,
         other,
-    )
-    return small_call(
-        last_kernel,
-        jax.ShapeDtypeStruct((steps, orbitals, 2, width), jnp.float32),
-        None,
-        fre,
-        fim,
-        entering,
         sum0,
         own1,
         *parts1,

time: 121 us -> 119 us (0.983)
  the two profiles are of different devices: /device:TPU:65 before, /device:TPU:1 now
where the time goes in v4:
time: 119 us
  starting transfers between devices  58 us (49%)
  waiting for transfers between devices  31 us (26%)
  Pallas kernels  26.7 us (22%)
  local copies, waits for them, and re-layouts  1.74 us (1%)
  other arithmetic  1.46 us (1%)
    ppermute x36, starting transfers between devices, send(): return lax.ppermute(array, BOTH, perm)  58 us
    ppermute x36, waiting for transfers between devices, send(): return lax.ppermute(array, BOTH, perm)  31 us
    pallas_call x2, Pallas kernels, product_call(): pl.pallas_call(body, out_shape=shape, in_specs=[pl.BlockSpec(memory_space...  11.4 us
    pallas_call x2, Pallas kernels, energy_call(): pl.pallas_call(lambda *refs: energy_kernel(skip, *refs), out_shape=jax.Sh...  10.5 us
    pallas_call x5, Pallas kernels, small_call(): pl.pallas_call(kernel, out_shape=out_shape, in_specs=specs, out_specs=out...  4.79 us
  transfers between devices with their start and end apart: 36, of which 11 were waited for; matrix products, arithmetic and copies ran while one was open for 2% of the time, Pallas kernels for 16%

profile of v4, /device:TPU:1, one launch (start us, length us, event | category | flops | bytes accessed | tf_op | source)
XLA Modules:
  0.0 119.3 jit_solution(7724682430241942483)
XLA Ops:
  0.0 1.0 copy.18
  1.0 0.1 reshape.62
  1.1 2.2 %collective-permute-start = (bf16[2,64,1024]{2,1,0:T(8,128)(2,1)S(1)}, bf16[2,64,1024]{2,1,0:T(8,128)(2,1)S(1)}, u32[]{:S(2)}, u32[]{:S(2)}) collective-permute-start(bf16[2,64,1024]{2,1,0:T(8,128)(2,1)S(1)} %reshape.62), channel_id=1, source_target_pairs={{0,16},{1,17},{2,18},{3,19},{4,20},{5,21},{6,22},{7,23},{8,72},{9,... | collective-permute-start | bytes 786440 | tf_op jit(solution)/shard_map/ppermute | solution.py:46
  3.3 1.5 %collective-permute-start.1 = (bf16[2,64,1024]{2,1,0:T(8,128)(2,1)S(1)}, bf16[2,64,1024]{2,1,0:T(8,128)(2,1)S(1)}, u32[]{:S(2)}, u32[]{:S(2)}) collective-permute-start(bf16[2,64,1024]{2,1,0:T(8,128)(2,1)S(1)} %reshape.62), channel_id=1, source_target_pairs={{0,48},{1,49},{2,50},{3,51},{4,52},{5,53},{6,54},{7,55},{8,200},{9... | collective-permute-start | bytes 786440 | tf_op jit(solution)/shard_map/ppermute | solution.py:46
  4.8 1.6 %collective-permute-start.2 = (bf16[2,64,1024]{2,1,0:T(8,128)(2,1)S(1)}, bf16[2,64,1024]{2,1,0:T(8,128)(2,1)S(1)}, u32[]{:S(2)}, u32[]{:S(2)}) collective-permute-start(bf16[2,64,1024]{2,1,0:T(8,128)(2,1)S(1)} %reshape.62), channel_id=1, source_target_pairs={{0,32},{1,33},{2,34},{3,35},{4,36},{5,37},{6,38},{7,39},{8,136},{9... | collective-permute-start | bytes 786440 | tf_op jit(solution)/shard_map/ppermute | solution.py:46
  6.4 0.8 select_add_fusion.3
  7.2 0.1 add.142
  7.3 0.1 add.146
  7.4 0.1 add.152
  7.5 0.1 add.155
  7.7 1.1 collective-permute-done
  8.8 2.1 %collective-permute-done.1 = bf16[2,64,1024]{2,1,0:T(8,128)(2,1)S(1)} collective-permute-done((bf16[2,64,1024]{2,1,0:T(8,128)(2,1)S(1)}, bf16[2,64,1024]{2,1,0:T(8,128)(2,1)S(1)}, u32[]{:S(2)}, u32[]{:S(2)}) %collective-permute-start.1) | collective-permute-done | bytes 262176 | tf_op jit(solution)/shard_map/ppermute | solution.py:46
  11.0 1.8 %collective-permute-done.2 = bf16[2,64,1024]{2,1,0:T(8,128)(2,1)S(1)} collective-permute-done((bf16[2,64,1024]{2,1,0:T(8,128)(2,1)S(1)}, bf16[2,64,1024]{2,1,0:T(8,128)(2,1)S(1)}, u32[]{:S(2)}, u32[]{:S(2)}) %collective-permute-start.2) | collective-permute-done | bytes 262176 | tf_op jit(solution)/shard_map/ppermute | solution.py:46
  12.9 1.0 collective-permute-start.3
  13.8 1.8 %collective-permute-start.4 = (bf16[256,1024]{1,0:T(8,128)(2,1)S(1)}, bf16[256,1024]{1,0:T(8,128)(2,1)S(1)}, u32[]{:S(2)}, u32[]{:S(2)}) collective-permute-start(bf16[256,1024]{1,0:T(8,128)(2,1)S(1)} %pad_maximum_fusion.refs_4_), channel_id=1, source_target_pairs={{0,192},{1,193},{2,194},{3,195},{4,196},{5,197},{6,198},{7,199},{8... | collective-permute-start | bytes 1572872 | tf_op jit(solution)/shard_map/ppermute | solution.py:46
  15.6 1.2 %collective-permute-start.5 = (bf16[256,1024]{1,0:T(8,128)(2,1)S(1)}, bf16[256,1024]{1,0:T(8,128)(2,1)S(1)}, u32[]{:S(2)}, u32[]{:S(2)}) collective-permute-start(bf16[256,1024]{1,0:T(8,128)(2,1)S(1)} %pad_maximum_fusion.refs_4_), channel_id=1, source_target_pairs={{0,128},{1,129},{2,130},{3,131},{4,132},{5,133},{6,134},{7,135},{8... | collective-permute-start | bytes 1572872 | tf_op jit(solution)/shard_map/ppermute | solution.py:46
  16.8 2.6 %collective-permute-start.6 = (bf16[256,1024]{1,0:T(8,128)(2,1)S(1)}, bf16[256,1024]{1,0:T(8,128)(2,1)S(1)}, u32[]{:S(2)}, u32[]{:S(2)}) collective-permute-start(bf16[256,1024]{1,0:T(8,128)(2,1)S(1)} %pad_maximum_fusion.refs_4_), channel_id=1, source_target_pairs={{0,8},{1,9},{2,10},{3,11},{4,12},{5,13},{6,14},{7,15},{8,0},{9,1},... | collective-permute-start | bytes 1572872 | tf_op jit(solution)/shard_map/ppermute | solution.py:46
  19.5 1.2 %collective-permute-start.10 = (bf16[256,1024]{1,0:T(8,128)(2,1)S(1)}, bf16[256,1024]{1,0:T(8,128)(2,1)S(1)}, u32[]{:S(2)}, u32[]{:S(2)}) collective-permute-start(bf16[256,1024]{1,0:T(8,128)(2,1)S(1)} %pad_maximum_fusion.1.refs_5_), channel_id=1, source_target_pairs={{0,64},{1,65},{2,66},{3,67},{4,68},{5,69},{6,70},{7,71},{8,24},{9,... | collective-permute-start | bytes 1572872 | tf_op jit(solution)/shard_map/ppermute | solution.py:46
  20.8 5.3 %shard_map.92.refs_1_ = bf16[4,2,64,2048]{3,2,1,0:T(8,128)(2,1)S(1)} custom-call(s32[32]{0:T(128)S(1)} %pad_add_fusion.1.refs_0_, s32[2]{0:T(128)S(1)} %pad_add_fusion.2.refs_1_, bf16[8,32,64,128]{3,2,1,0:T(8,128)(2,1)} %refs_2_.3, bf16[32,8,64,128]{3,2,1,0:T(8,128)(2,1)} %refs_3_.3), custom_call_target="tpu_custom_call" | custom-call | flops 20971520 | bytes 6291456 | tf_op jit(solution)/shard_map/pallas_call | solution.py:85
  26.1 5.3 %shard_map.91.refs_0_ = bf16[4,2,64,2048]{3,2,1,0:T(8,128)(2,1)S(1)} custom-call(s32[32]{0:T(128)S(1)} %pad_add_fusion.1.refs_0_, s32[2]{0:T(128)S(1)} %pad_add_fusion.2.refs_1_, bf16[8,32,64,128]{3,2,1,0:T(8,128)(2,1)} %refs_2_.3, bf16[32,8,64,128]{3,2,1,0:T(8,128)(2,1)} %refs_3_.3), custom_call_target="tpu_custom_call" | custom-call | flops 20971520 | bytes 6291456 | tf_op jit(solution)/shard_map/pallas_call | solution.py:85
  31.5 1.6 %collective-permute-start.11 = (bf16[256,1024]{1,0:T(8,128)(2,1)S(1)}, bf16[256,1024]{1,0:T(8,128)(2,1)S(1)}, u32[]{:S(2)}, u32[]{:S(2)}) collective-permute-start(bf16[256,1024]{1,0:T(8,128)(2,1)S(1)} %pad_maximum_fusion.1.refs_5_), channel_id=1, source_target_pairs={{0,192},{1,193},{2,194},{3,195},{4,196},{5,197},{6,198},{7,199},{8... | collective-permute-start | bytes 1572872 | tf_op jit(solution)/shard_map/ppermute | solution.py:46
  33.1 0.6 collective-permute-start.12
  33.7 1.7 %collective-permute-start.7 = (bf16[256,1024]{1,0:T(8,128)(2,1)S(1)}, bf16[256,1024]{1,0:T(8,128)(2,1)S(1)}, u32[]{:S(2)}, u32[]{:S(2)}) collective-permute-start(bf16[256,1024]{1,0:T(8,128)(2,1)S(1)} %collective-permute-done.3.refs_5_), channel_id=1, source_target_pairs={{0,8},{1,9},{2,10},{3,11},{4,12},{5,13},{6,14},{7,15},{8,0},{9,1},... | collective-permute-start | bytes 1572872 | tf_op jit(solution)/shard_map/ppermute | solution.py:46
  35.4 0.1 collective-permute-start.8
  35.6 1.7 %collective-permute-start.9 = (bf16[256,1024]{1,0:T(8,128)(2,1)S(1)}, bf16[256,1024]{1,0:T(8,128)(2,1)S(1)}, u32[]{:S(2)}, u32[]{:S(2)}) collective-permute-start(bf16[256,1024]{1,0:T(8,128)(2,1)S(1)} %collective-permute-done.5.refs_7_), channel_id=1, source_target_pairs={{0,8},{1,9},{2,10},{3,11},{4,12},{5,13},{6,14},{7,15},{8,0},{9,1},... | collective-permute-start | bytes 1572872 | tf_op jit(solution)/shard_map/ppermute | solution.py:46
  37.3 0.1 broadcast_multiply_fusion.refs_3_.fim_ref
  37.4 7.4 %collective-permute-done.11.refs_7_ = bf16[256,1024]{1,0:T(8,128)(2,1)S(1)} collective-permute-done((bf16[256,1024]{1,0:T(8,128)(2,1)S(1)}, bf16[256,1024]{1,0:T(8,128)(2,1)S(1)}, u32[]{:S(2)}, u32[]{:S(2)}) %collective-permute-start.11) | collective-permute-done | bytes 524320 | tf_op jit(solution)/shard_map/ppermute | solution.py:46
  44.8 1.2 collective-permute-start.13
  46.0 0.5 collective-permute-start.15
  46.5 0.3 collective-permute-start.16
  46.8 0.1 broadcast_in_dim.12.refs_2_.fre_ref
  47.0 5.7 %shard_map.93 = (bf16[3,8,64,128]{3,2,1,0:T(8,128)(2,1)S(1)}, bf16[2,8,64,128]{3,2,1,0:T(8,128)(2,1)S(1)}, f32[1,8,64,128]{3,2,1,0:T(8,128)S(1)}, f32[2,8,64,128]{3,2,1,0:T(8,128)S(1)}, f32[8,64,128]{2,1,0:T(8,128)S(1)}) custom-call(s32[8]{0:T(128)S(1)} %and_select_fusion.4.cols_ref, bf16[4,2,64,2048]{3,2,1,0:T(8,128)(2,1)S(1)} %shard_map.91.refs_0_, ...), custom_call_target="tpu_custom_call" | custom-call | flops 4294967296 | bytes 8388608 | tf_op jit(solution)/shard_map/pallas_call | solution.py:171
  52.7 5.7 %shard_map.94 = (bf16[3,8,64,128]{3,2,1,0:T(8,128)(2,1)S(1)}, bf16[2,8,64,128]{3,2,1,0:T(8,128)(2,1)S(1)}, f32[1,8,64,128]{3,2,1,0:T(8,128)S(1)}, f32[2,8,64,128...) custom-call(s32[8]{0:T(128)S(1)} %and_select_fusion.4.cols_ref, ...), custom_call_target="tpu_custom_call" | custom-call | flops 4294967296 | bytes 8388608 | tf_op jit(solution)/shard_map/pallas_call | solution.py:171
  58.4 5.7 %collective-permute-start.17 = (bf16[3,2,64,128]{3,2,1,0:T(8,128)(2,1)S(1)}, bf16[3,2,64,128]{3,2,1,0:T(8,128)(2,1)S(1)}, u32[]{:S(2)}, u32[]{:S(2)}) collective-permute-start(bf16[3,2,64,128]{3,2,1,0:T(8,128)(2,1)S(1)} %get-tuple-element.21), channel_id=1, source_target_pairs={{0,1},{1,2},{2,3},{3,4},{4,5},{5,6},{6,7},{7,0},{8,15},{9,8},{10,9... | collective-permute-start | bytes 294920 | tf_op jit(solution)/shard_map/ppermute | solution.py:46
  64.1 2.7 %collective-permute-start.28 = (bf16[3,8,64,128]{3,2,1,0:T(8,128)(2,1)S(1)}, bf16[3,8,64,128]{3,2,1,0:T(8,128)(2,1)S(1)}, u32[]{:S(2)}, u32[]{:S(2)}) collective-permute-start(bf16[3,8,64,128]{3,2,1,0:T(8,128)(2,1)S(1)} %get-tuple-element.26), channel_id=1, source_target_pairs={{0,1},{1,2},{2,3},{3,4},{4,5},{5,6},{6,7},{7,0},{8,15},{9,8},{10,9... | collective-permute-start | bytes 1179656 | tf_op jit(solution)/shard_map/ppermute | solution.py:46
  66.8 1.4 %collective-permute-start.29 = (bf16[2,8,64,128]{3,2,1,0:T(8,128)(2,1)S(1)}, bf16[2,8,64,128]{3,2,1,0:T(8,128)(2,1)S(1)}, u32[]{:S(2)}, u32[]{:S(2)}) collective-permute-start(bf16[2,8,64,128]{3,2,1,0:T(8,128)(2,1)S(1)} %get-tuple-element.27), channel_id=1, source_target_pairs={{0,7},{1,0},{2,1},{3,2},{4,3},{5,4},{6,5},{7,6},{8,9},{9,10},{10,1... | collective-permute-start | bytes 786440 | tf_op jit(solution)/shard_map/ppermute | solution.py:46
  68.2 0.2 collective-permute-done.18.back_ref
  68.4 0.2 collective-permute-start.19
  68.6 4.4 %collective-permute-start.20 = (bf16[2,64,128]{2,1,0:T(8,128)(2,1)S(1)}, bf16[2,64,128]{2,1,0:T(8,128)(2,1)S(1)}, u32[]{:S(2)}, u32[]{:S(2)}) collective-permute-start(bf16[2,64,128]{2,1,0:T(8,128)(2,1)S(1)} %get-tuple-element.37), channel_id=1, source_target_pairs={{0,3},{1,4},{2,5},{3,6},{4,7},{5,0},{6,1},{7,2},{8,13},{9,14},{10,... | collective-permute-start | bytes 98312 | tf_op jit(solution)/shard_map/ppermute | solution.py:46
  73.0 2.9 %collective-permute-done.19.from5_ref = bf16[2,64,128]{2,1,0:T(8,128)(2,1)S(1)} collective-permute-done((bf16[2,64,128]{2,1,0:T(8,128)(2,1)S(1)}, bf16[2,64,128]{2,1,0:T(8,128)(2,1)S(1)}, u32[]{:S(2)}, u32[]{:S(2)}) %collective-permute-start.19) | collective-permute-done | bytes 32800 | tf_op jit(solution)/shard_map/ppermute | solution.py:46
  75.9 1.0 collective-permute-start.33
  76.9 3.7 %collective-permute-done.20.from3_ref = bf16[2,64,128]{2,1,0:T(8,128)(2,1)S(1)} collective-permute-done((bf16[2,64,128]{2,1,0:T(8,128)(2,1)S(1)}, bf16[2,64,128]{2,1,0:T(8,128)(2,1)S(1)}, u32[]{:S(2)}, u32[]{:S(2)}) %collective-permute-start.20) | collective-permute-done | bytes 32800 | tf_op jit(solution)/shard_map/ppermute | solution.py:46
  80.6 0.6 shard_map.95.own_ref
  81.2 4.8 %collective-permute-start.21 = (f32[3,64,128]{2,1,0:T(8,128)S(1)}, f32[3,64,128]{2,1,0:T(8,128)S(1)}, u32[]{:S(2)}, u32[]{:S(2)}) collective-permute-start(f32[3,64,128]{2,1,0:T(8,128)S(1)} %shard_map.95.own_ref), channel_id=1, source_target_pairs={{0,8},{1,9},{2,10},{3,11},{4,12},{5,13},{6,14},{7,15},{8,0},{9,1},... | collective-permute-start | bytes 294920 | tf_op jit(solution)/shard_map/ppermute | solution.py:46
  86.1 0.9 collective-permute-done.21.other_ref.core_ref
  86.9 0.6 shard_map.96.own_ref
  87.6 1.2 %collective-permute-start.22 = (f32[3,64,128]{2,1,0:T(8,128)S(1)}, f32[3,64,128]{2,1,0:T(8,128)S(1)}, u32[]{:S(2)}, u32[]{:S(2)}) collective-permute-start(f32[3,64,128]{2,1,0:T(8,128)S(1)} %shard_map.96.own_ref), channel_id=1, source_target_pairs={{0,16},{1,17},{2,18},{3,19},{4,20},{5,21},{6,22},{7,23},{8,24},{9,... | collective-permute-start | bytes 294920 | tf_op jit(solution)/shard_map/ppermute | solution.py:46
  88.8 2.3 %collective-permute-start.23 = (f32[3,64,128]{2,1,0:T(8,128)S(1)}, f32[3,64,128]{2,1,0:T(8,128)S(1)}, u32[]{:S(2)}, u32[]{:S(2)}) collective-permute-start(f32[3,64,128]{2,1,0:T(8,128)S(1)} %shard_map.96.own_ref), channel_id=1, source_target_pairs={{0,32},{1,33},{2,34},{3,35},{4,36},{5,37},{6,38},{7,39},{8,40},{9,... | collective-permute-start | bytes 294920 | tf_op jit(solution)/shard_map/ppermute | solution.py:46
  91.1 0.2 collective-permute-start.24
  91.3 0.1 fusion.1
  91.4 0.1 collective-permute-start.30
  91.5 4.5 %collective-permute-start.31 = (bf16[8,64,128]{2,1,0:T(8,128)(2,1)S(1)}, bf16[8,64,128]{2,1,0:T(8,128)(2,1)S(1)}, u32[]{:S(2)}, u32[]{:S(2)}) collective-permute-start(bf16[8,64,128]{2,1,0:T(8,128)(2,1)S(1)} %get-tuple-element.35), channel_id=1, source_target_pairs={{0,3},{1,4},{2,5},{3,6},{4,7},{5,0},{6,1},{7,2},{8,13},{9,14},{10,... | collective-permute-start | bytes 393224 | tf_op jit(solution)/shard_map/ppermute | solution.py:46
  96.0 0.1 fusion.3
  96.1 0.1 collective-permute-start.34
  96.2 4.5 %collective-permute-start.35 = (bf16[8,64,128]{2,1,0:T(8,128)(2,1)S(1)}, bf16[8,64,128]{2,1,0:T(8,128)(2,1)S(1)}, u32[]{:S(2)}, u32[]{:S(2)}) collective-permute-start(bf16[8,64,128]{2,1,0:T(8,128)(2,1)S(1)} %get-tuple-element.33), channel_id=1, source_target_pairs={{0,3},{1,4},{2,5},{3,6},{4,7},{5,0},{6,1},{7,2},{8,13},{9,14},{10,... | collective-permute-start | bytes 393224 | tf_op jit(solution)/shard_map/ppermute | solution.py:46
  100.6 1.1 shard_map.97
  101.7 0.9 collective-permute-start.25
  102.6 7.2 %collective-permute-done.30.from5_ref = bf16[8,64,128]{2,1,0:T(8,128)(2,1)S(1)} collective-permute-done((bf16[8,64,128]{2,1,0:T(8,128)(2,1)S(1)}, bf16[8,64,128]{2,1,0:T(8,128)(2,1)S(1)}, u32[]{:S(2)}, u32[]{:S(2)}) %collective-permute-start.30) | collective-permute-done | bytes 131104 | tf_op jit(solution)/shard_map/ppermute | solution.py:46
  109.8 0.9 collective-permute-start.26
  110.7 2.5 %collective-permute-start.27 = (f32[3,64,128]{2,1,0:T(8,128)S(1)}, f32[3,64,128]{2,1,0:T(8,128)S(1)}, u32[]{:S(2)}, u32[]{:S(2)}) collective-permute-start(f32[3,64,128]{2,1,0:T(8,128)S(1)} %get-tuple-element.23), channel_id=1, source_target_pairs={{0,192},{1,193},{2,194},{3,195},{4,196},{5,197},{6,198},{7,199},{8... | collective-permute-start | bytes 294920 | tf_op jit(solution)/shard_map/ppermute | solution.py:46
  113.2 0.1 shard_map.98.even_ref
  113.3 1.5 %collective-permute-done.26.d2_ref = f32[3,64,128]{2,1,0:T(8,128)S(1)} collective-permute-done((f32[3,64,128]{2,1,0:T(8,128)S(1)}, f32[3,64,128]{2,1,0:T(8,128)S(1)}, u32[]{:S(2)}, u32[]{:S(2)}) %collective-permute-start.26) | collective-permute-done | bytes 98336 | tf_op jit(solution)/shard_map/ppermute | solution.py:46
  114.8 2.1 %collective-permute-done.27.d3_ref = f32[3,64,128]{2,1,0:T(8,128)S(1)} collective-permute-done((f32[3,64,128]{2,1,0:T(8,128)S(1)}, f32[3,64,128]{2,1,0:T(8,128)S(1)}, u32[]{:S(2)}, u32[]{:S(2)}) %collective-permute-start.27) | collective-permute-done | bytes 98336 | tf_op jit(solution)/shard_map/ppermute | solution.py:46
  116.9 2.4 %shard_map.99 = f32[8,64,2,128]{3,2,1,0:T(2,128)} custom-call(s32[3]{0:T(128)S(1)} %pad_add_fusion.where_ref, f32[8,64,128]{2,1,0:T(8,128)S(1)} %broadcast_in_dim.12.refs_2_.fre_ref, f32[8,64,128]{2,1,0:T(8,128)S(1)} %broadcast_multiply_fusion.refs_3_.fim_ref, f32[2,64,128]{2,1,0:T(8,128)S(1)} %bitcast.48, f32[3,64,128]{2,1,0:T(8,128)S(1)} %collective-permute-done.25.d1_ref, ...), custom_call_target="tpu_custom_call" | custom-call | flops 1000000 | bytes 1048576 | tf_op jit(solution)/shard_map/pallas_call | solution.py:324
  (54 shorter events, 0.6 us)
Async XLA Ops:
  1.1 7.7 %collective-permute-start = (bf16[2,64,1024]{2,1,0:T(8,128)(2,1)S(1)}, bf16[2,64,1024]{2,1,0:T(8,128)(2,1)S(1)}, u32[]{:S(2)}, u32[]{:S(2)}) collective-permute-start(bf16[2,64,1024]{2,1,0:T(8,128)(2,1)S(1)} %reshape.62), channel_id=1, source_target_pairs={{0,16},{1,17},{2,18},{3,19},{4,20},{5,21},{6,22},{7,23},{8,72},{9,... | collective-permute-start | bytes 786440 | tf_op jit(solution)/shard_map/ppermute | solution.py:46
  3.3 7.7 %collective-permute-start.1 = (bf16[2,64,1024]{2,1,0:T(8,128)(2,1)S(1)}, bf16[2,64,1024]{2,1,0:T(8,128)(2,1)S(1)}, u32[]{:S(2)}, u32[]{:S(2)}) collective-permute-start(bf16[2,64,1024]{2,1,0:T(8,128)(2,1)S(1)} %reshape.62), channel_id=1, source_target_pairs={{0,48},{1,49},{2,50},{3,51},{4,52},{5,53},{6,54},{7,55},{8,200},{9... | collective-permute-start | bytes 786440 | tf_op jit(solution)/shard_map/ppermute | solution.py:46
  4.8 8.0 %collective-permute-start.2 = (bf16[2,64,1024]{2,1,0:T(8,128)(2,1)S(1)}, bf16[2,64,1024]{2,1,0:T(8,128)(2,1)S(1)}, u32[]{:S(2)}, u32[]{:S(2)}) collective-permute-start(bf16[2,64,1024]{2,1,0:T(8,128)(2,1)S(1)} %reshape.62), channel_id=1, source_target_pairs={{0,32},{1,33},{2,34},{3,35},{4,36},{5,37},{6,38},{7,39},{8,136},{9... | collective-permute-start | bytes 786440 | tf_op jit(solution)/shard_map/ppermute | solution.py:46
  12.9 18.6 %collective-permute-start.3 = (bf16[256,1024]{1,0:T(8,128)(2,1)S(1)}, bf16[256,1024]{1,0:T(8,128)(2,1)S(1)}, u32[]{:S(2)}, u32[]{:S(2)}) collective-permute-start(bf16[256,1024]{1,0:T(8,128)(2,1)S(1)} %pad_maximum_fusion.refs_4_), channel_id=1, source_target_pairs={{0,64},{1,65},{2,66},{3,67},{4,68},{5,69},{6,70},{7,71},{8,24},{9,... | collective-permute-start | bytes 1572872 | tf_op jit(solution)/shard_map/ppermute | solution.py:46
  13.8 19.2 %collective-permute-start.4 = (bf16[256,1024]{1,0:T(8,128)(2,1)S(1)}, bf16[256,1024]{1,0:T(8,128)(2,1)S(1)}, u32[]{:S(2)}, u32[]{:S(2)}) collective-permute-start(bf16[256,1024]{1,0:T(8,128)(2,1)S(1)} %pad_maximum_fusion.refs_4_), channel_id=1, source_target_pairs={{0,192},{1,193},{2,194},{3,195},{4,196},{5,197},{6,198},{7,199},{8... | collective-permute-start | bytes 1572872 | tf_op jit(solution)/shard_map/ppermute | solution.py:46
  15.6 18.1 %collective-permute-start.5 = (bf16[256,1024]{1,0:T(8,128)(2,1)S(1)}, bf16[256,1024]{1,0:T(8,128)(2,1)S(1)}, u32[]{:S(2)}, u32[]{:S(2)}) collective-permute-start(bf16[256,1024]{1,0:T(8,128)(2,1)S(1)} %pad_maximum_fusion.refs_4_), channel_id=1, source_target_pairs={{0,128},{1,129},{2,130},{3,131},{4,132},{5,133},{6,134},{7,135},{8... | collective-permute-start | bytes 1572872 | tf_op jit(solution)/shard_map/ppermute | solution.py:46
  16.8 18.6 %collective-permute-start.6 = (bf16[256,1024]{1,0:T(8,128)(2,1)S(1)}, bf16[256,1024]{1,0:T(8,128)(2,1)S(1)}, u32[]{:S(2)}, u32[]{:S(2)}) collective-permute-start(bf16[256,1024]{1,0:T(8,128)(2,1)S(1)} %pad_maximum_fusion.refs_4_), channel_id=1, source_target_pairs={{0,8},{1,9},{2,10},{3,11},{4,12},{5,13},{6,14},{7,15},{8,0},{9,1},... | collective-permute-start | bytes 1572872 | tf_op jit(solution)/shard_map/ppermute | solution.py:46
  19.5 16.0 %collective-permute-start.10 = (bf16[256,1024]{1,0:T(8,128)(2,1)S(1)}, bf16[256,1024]{1,0:T(8,128)(2,1)S(1)}, u32[]{:S(2)}, u32[]{:S(2)}) collective-permute-start(bf16[256,1024]{1,0:T(8,128)(2,1)S(1)} %pad_maximum_fusion.1.refs_5_), channel_id=1, source_target_pairs={{0,64},{1,65},{2,66},{3,67},{4,68},{5,69},{6,70},{7,71},{8,24},{9,... | collective-permute-start | bytes 1572872 | tf_op jit(solution)/shard_map/ppermute | solution.py:46
  26.1 5.3 %copy-start.3 = (f32[64]{0:T(128)S(1)}, f32[64]{0:T(128)}, u32[]{:S(2)}) copy-start(f32[64]{0:T(128)} %param.14) | copy-start | bytes 772
  26.1 9.4 %copy-start.1 = (f32[8,64]{1,0:T(8,128)S(1)}, f32[8,64]{1,0:T(8,128)}, u32[]{:S(2)}) copy-start(f32[8,64]{1,0:T(8,128)} %param.13) | copy-start | bytes 6148
  26.1 20.7 %copy-start.2 = (s32[8]{0:T(128)S(1)}, s32[8]{0:T(128)}, u32[]{:S(2)}) copy-start(s32[8]{0:T(128)} %constant.119.clone) | copy-start | bytes 100
  31.5 13.4 %collective-permute-start.11 = (bf16[256,1024]{1,0:T(8,128)(2,1)S(1)}, bf16[256,1024]{1,0:T(8,128)(2,1)S(1)}, u32[]{:S(2)}, u32[]{:S(2)}) collective-permute-start(bf16[256,1024]{1,0:T(8,128)(2,1)S(1)} %pad_maximum_fusion.1.refs_5_), channel_id=1, source_target_pairs={{0,192},{1,193},{2,194},{3,195},{4,196},{5,197},{6,198},{7,199},{8... | collective-permute-start | bytes 1572872 | tf_op jit(solution)/shard_map/ppermute | solution.py:46
  33.1 12.9 %collective-permute-start.12 = (bf16[256,1024]{1,0:T(8,128)(2,1)S(1)}, bf16[256,1024]{1,0:T(8,128)(2,1)S(1)}, u32[]{:S(2)}, u32[]{:S(2)}) collective-permute-start(bf16[256,1024]{1,0:T(8,128)(2,1)S(1)} %pad_maximum_fusion.1.refs_5_), channel_id=1, source_target_pairs={{0,128},{1,129},{2,130},{3,131},{4,132},{5,133},{6,134},{7,135},{8... | collective-permute-start | bytes 1572872 | tf_op jit(solution)/shard_map/ppermute | solution.py:46
  33.7 12.3 %collective-permute-start.7 = (bf16[256,1024]{1,0:T(8,128)(2,1)S(1)}, bf16[256,1024]{1,0:T(8,128)(2,1)S(1)}, u32[]{:S(2)}, u32[]{:S(2)}) collective-permute-start(bf16[256,1024]{1,0:T(8,128)(2,1)S(1)} %collective-permute-done.3.refs_5_), channel_id=1, source_target_pairs={{0,8},{1,9},{2,10},{3,11},{4,12},{5,13},{6,14},{7,15},{8,0},{9,1},... | collective-permute-start | bytes 1572872 | tf_op jit(solution)/shard_map/ppermute | solution.py:46
  35.4 11.1 %collective-permute-start.8 = (bf16[256,1024]{1,0:T(8,128)(2,1)S(1)}, bf16[256,1024]{1,0:T(8,128)(2,1)S(1)}, u32[]{:S(2)}, u32[]{:S(2)}) collective-permute-start(bf16[256,1024]{1,0:T(8,128)(2,1)S(1)} %collective-permute-done.4.refs_6_), channel_id=1, source_target_pairs={{0,8},{1,9},{2,10},{3,11},{4,12},{5,13},{6,14},{7,15},{8,0},{9,1},... | collective-permute-start | bytes 1572872 | tf_op jit(solution)/shard_map/ppermute | solution.py:46
  35.6 11.3 %collective-permute-start.9 = (bf16[256,1024]{1,0:T(8,128)(2,1)S(1)}, bf16[256,1024]{1,0:T(8,128)(2,1)S(1)}, u32[]{:S(2)}, u32[]{:S(2)}) collective-permute-start(bf16[256,1024]{1,0:T(8,128)(2,1)S(1)} %collective-permute-done.5.refs_7_), channel_id=1, source_target_pairs={{0,8},{1,9},{2,10},{3,11},{4,12},{5,13},{6,14},{7,15},{8,0},{9,1},... | collective-permute-start | bytes 1572872 | tf_op jit(solution)/shard_map/ppermute | solution.py:46
  44.8 7.8 %collective-permute-start.13 = (bf16[256,1024]{1,0:T(8,128)(2,1)S(1)}, bf16[256,1024]{1,0:T(8,128)(2,1)S(1)}, u32[]{:S(2)}, u32[]{:S(2)}) collective-permute-start(bf16[256,1024]{1,0:T(8,128)(2,1)S(1)} %pad_maximum_fusion.1.refs_5_), channel_id=1, source_target_pairs={{0,8},{1,9},{2,10},{3,11},{4,12},{5,13},{6,14},{7,15},{8,0},{9,1},... | collective-permute-start | bytes 1572872 | tf_op jit(solution)/shard_map/ppermute | solution.py:46
  46.0 6.7 %collective-permute-start.14 = (bf16[256,1024]{1,0:T(8,128)(2,1)S(1)}, bf16[256,1024]{1,0:T(8,128)(2,1)S(1)}, u32[]{:S(2)}, u32[]{:S(2)}) collective-permute-start(bf16[256,1024]{1,0:T(8,128)(2,1)S(1)} %collective-permute-done.10.refs_6_), channel_id=1, source_target_pairs={{0,8},{1,9},{2,10},{3,11},{4,12},{5,13},{6,14},{7,15},{8,0},{9,1},... | collective-permute-start | bytes 1572872 | tf_op jit(solution)/shard_map/ppermute | solution.py:46
  46.0 6.7 %collective-permute-start.15 = (bf16[256,1024]{1,0:T(8,128)(2,1)S(1)}, bf16[256,1024]{1,0:T(8,128)(2,1)S(1)}, u32[]{:S(2)}, u32[]{:S(2)}) collective-permute-start(bf16[256,1024]{1,0:T(8,128)(2,1)S(1)} %collective-permute-done.11.refs_7_), channel_id=1, source_target_pairs={{0,8},{1,9},{2,10},{3,11},{4,12},{5,13},{6,14},{7,15},{8,0},{9,1},... | collective-permute-start | bytes 1572872 | tf_op jit(solution)/shard_map/ppermute | solution.py:46
  46.5 6.2 %collective-permute-start.16 = (bf16[256,1024]{1,0:T(8,128)(2,1)S(1)}, bf16[256,1024]{1,0:T(8,128)(2,1)S(1)}, u32[]{:S(2)}, u32[]{:S(2)}) collective-permute-start(bf16[256,1024]{1,0:T(8,128)(2,1)S(1)} %collective-permute-done.12.refs_8_), channel_id=1, source_target_pairs={{0,8},{1,9},{2,10},{3,11},{4,12},{5,13},{6,14},{7,15},{8,0},{9,1},... | collective-permute-start | bytes 1572872 | tf_op jit(solution)/shard_map/ppermute | solution.py:46
  58.4 54.8 %copy-start = (f32[64,2,128]{2,1,0:T(2,128)S(1)}, f32[64,2,128]{2,1,0:T(2,128)}, u32[]{:S(2)}) copy-start(f32[64,2,128]{2,1,0:T(2,128)} %param.12) | copy-start | bytes 196612
  58.4 10.0 %collective-permute-start.17 = (bf16[3,2,64,128]{3,2,1,0:T(8,128)(2,1)S(1)}, bf16[3,2,64,128]{3,2,1,0:T(8,128)(2,1)S(1)}, u32[]{:S(2)}, u32[]{:S(2)}) collective-permute-start(bf16[3,2,64,128]{3,2,1,0:T(8,128)(2,1)S(1)} %get-tuple-element.21), channel_id=1, source_target_pairs={{0,1},{1,2},{2,3},{3,4},{4,5},{5,6},{6,7},{7,0},{8,15},{9,8},{10,9... | collective-permute-start | bytes 294920 | tf_op jit(solution)/shard_map/ppermute | solution.py:46
  64.1 4.3 %collective-permute-start.18 = (bf16[2,2,64,128]{3,2,1,0:T(8,128)(2,1)S(1)}, bf16[2,2,64,128]{3,2,1,0:T(8,128)(2,1)S(1)}, u32[]{:S(2)}, u32[]{:S(2)}) collective-permute-start(bf16[2,2,64,128]{3,2,1,0:T(8,128)(2,1)S(1)} %get-tuple-element.22), channel_id=1, source_target_pairs={{0,7},{1,0},{2,1},{3,2},{4,3},{5,4},{6,5},{7,6},{8,9},{9,10},{10,1... | collective-permute-start | bytes 196616 | tf_op jit(solution)/shard_map/ppermute | solution.py:46
  64.1 27.0 %collective-permute-start.28 = (bf16[3,8,64,128]{3,2,1,0:T(8,128)(2,1)S(1)}, bf16[3,8,64,128]{3,2,1,0:T(8,128)(2,1)S(1)}, u32[]{:S(2)}, u32[]{:S(2)}) collective-permute-start(bf16[3,8,64,128]{3,2,1,0:T(8,128)(2,1)S(1)} %get-tuple-element.26), channel_id=1, source_target_pairs={{0,1},{1,2},{2,3},{3,4},{4,5},{5,6},{6,7},{7,0},{8,15},{9,8},{10,9... | collective-permute-start | bytes 1179656 | tf_op jit(solution)/shard_map/ppermute | solution.py:46
  66.8 24.7 %collective-permute-start.32 = (bf16[3,8,64,128]{3,2,1,0:T(8,128)(2,1)S(1)}, bf16[3,8,64,128]{3,2,1,0:T(8,128)(2,1)S(1)}, u32[]{:S(2)}, u32[]{:S(2)}) collective-permute-start(bf16[3,8,64,128]{3,2,1,0:T(8,128)(2,1)S(1)} %get-tuple-element.30), channel_id=1, source_target_pairs={{0,1},{1,2},{2,3},{3,4},{4,5},{5,6},{6,7},{7,0},{8,15},{9,8},{10,9... | collective-permute-start | bytes 1179656 | tf_op jit(solution)/shard_map/ppermute | solution.py:46
  66.8 22.0 %collective-permute-start.29 = (bf16[2,8,64,128]{3,2,1,0:T(8,128)(2,1)S(1)}, bf16[2,8,64,128]{3,2,1,0:T(8,128)(2,1)S(1)}, u32[]{:S(2)}, u32[]{:S(2)}) collective-permute-start(bf16[2,8,64,128]{3,2,1,0:T(8,128)(2,1)S(1)} %get-tuple-element.27), channel_id=1, source_target_pairs={{0,7},{1,0},{2,1},{3,2},{4,3},{5,4},{6,5},{7,6},{8,9},{9,10},{10,1... | collective-permute-start | bytes 786440 | tf_op jit(solution)/shard_map/ppermute | solution.py:46
  68.4 7.5 %collective-permute-start.19 = (bf16[2,64,128]{2,1,0:T(8,128)(2,1)S(1)}, bf16[2,64,128]{2,1,0:T(8,128)(2,1)S(1)}, u32[]{:S(2)}, u32[]{:S(2)}) collective-permute-start(bf16[2,64,128]{2,1,0:T(8,128)(2,1)S(1)} %get-tuple-element.38), channel_id=1, source_target_pairs={{0,5},{1,6},{2,7},{3,0},{4,1},{5,2},{6,3},{7,4},{8,11},{9,12},{10,... | collective-permute-start | bytes 98312 | tf_op jit(solution)/shard_map/ppermute | solution.py:46
  68.6 12.0 %collective-permute-start.20 = (bf16[2,64,128]{2,1,0:T(8,128)(2,1)S(1)}, bf16[2,64,128]{2,1,0:T(8,128)(2,1)S(1)}, u32[]{:S(2)}, u32[]{:S(2)}) collective-permute-start(bf16[2,64,128]{2,1,0:T(8,128)(2,1)S(1)} %get-tuple-element.37), channel_id=1, source_target_pairs={{0,3},{1,4},{2,5},{3,6},{4,7},{5,0},{6,1},{7,2},{8,13},{9,14},{10,... | collective-permute-start | bytes 98312 | tf_op jit(solution)/shard_map/ppermute | solution.py:46
  75.9 15.5 %collective-permute-start.33 = (bf16[2,8,64,128]{3,2,1,0:T(8,128)(2,1)S(1)}, bf16[2,8,64,128]{3,2,1,0:T(8,128)(2,1)S(1)}, u32[]{:S(2)}, u32[]{:S(2)}) collective-permute-start(bf16[2,8,64,128]{3,2,1,0:T(8,128)(2,1)S(1)} %get-tuple-element.31), channel_id=1, source_target_pairs={{0,7},{1,0},{2,1},{3,2},{4,3},{5,4},{6,5},{7,6},{8,9},{9,10},{10,1... | collective-permute-start | bytes 786440 | tf_op jit(solution)/shard_map/ppermute | solution.py:46
  81.2 5.7 %collective-permute-start.21 = (f32[3,64,128]{2,1,0:T(8,128)S(1)}, f32[3,64,128]{2,1,0:T(8,128)S(1)}, u32[]{:S(2)}, u32[]{:S(2)}) collective-permute-start(f32[3,64,128]{2,1,0:T(8,128)S(1)} %shard_map.95.own_ref), channel_id=1, source_target_pairs={{0,8},{1,9},{2,10},{3,11},{4,12},{5,13},{6,14},{7,15},{8,0},{9,1},... | collective-permute-start | bytes 294920 | tf_op jit(solution)/shard_map/ppermute | solution.py:46
  87.6 8.5 %collective-permute-start.22 = (f32[3,64,128]{2,1,0:T(8,128)S(1)}, f32[3,64,128]{2,1,0:T(8,128)S(1)}, u32[]{:S(2)}, u32[]{:S(2)}) collective-permute-start(f32[3,64,128]{2,1,0:T(8,128)S(1)} %shard_map.96.own_ref), channel_id=1, source_target_pairs={{0,16},{1,17},{2,18},{3,19},{4,20},{5,21},{6,22},{7,23},{8,24},{9,... | collective-permute-start | bytes 294920 | tf_op jit(solution)/shard_map/ppermute | solution.py:46
  88.8 7.4 %collective-permute-start.23 = (f32[3,64,128]{2,1,0:T(8,128)S(1)}, f32[3,64,128]{2,1,0:T(8,128)S(1)}, u32[]{:S(2)}, u32[]{:S(2)}) collective-permute-start(f32[3,64,128]{2,1,0:T(8,128)S(1)} %shard_map.96.own_ref), channel_id=1, source_target_pairs={{0,32},{1,33},{2,34},{3,35},{4,36},{5,37},{6,38},{7,39},{8,40},{9,... | collective-permute-start | bytes 294920 | tf_op jit(solution)/shard_map/ppermute | solution.py:46
  91.1 9.5 %collective-permute-start.24 = (f32[3,64,128]{2,1,0:T(8,128)S(1)}, f32[3,64,128]{2,1,0:T(8,128)S(1)}, u32[]{:S(2)}, u32[]{:S(2)}) collective-permute-start(f32[3,64,128]{2,1,0:T(8,128)S(1)} %shard_map.96.own_ref), channel_id=1, source_target_pairs={{0,48},{1,49},{2,50},{3,51},{4,52},{5,53},{6,54},{7,55},{8,56},{9,... | collective-permute-start | bytes 294920 | tf_op jit(solution)/shard_map/ppermute | solution.py:46
  91.4 18.4 %collective-permute-start.30 = (bf16[8,64,128]{2,1,0:T(8,128)(2,1)S(1)}, bf16[8,64,128]{2,1,0:T(8,128)(2,1)S(1)}, u32[]{:S(2)}, u32[]{:S(2)}) collective-permute-start(bf16[8,64,128]{2,1,0:T(8,128)(2,1)S(1)} %get-tuple-element.36), channel_id=1, source_target_pairs={{0,5},{1,6},{2,7},{3,0},{4,1},{5,2},{6,3},{7,4},{8,11},{9,12},{10,... | collective-permute-start | bytes 393224 | tf_op jit(solution)/shard_map/ppermute | solution.py:46
  91.5 19.2 %collective-permute-start.31 = (bf16[8,64,128]{2,1,0:T(8,128)(2,1)S(1)}, bf16[8,64,128]{2,1,0:T(8,128)(2,1)S(1)}, u32[]{:S(2)}, u32[]{:S(2)}) collective-permute-start(bf16[8,64,128]{2,1,0:T(8,128)(2,1)S(1)} %get-tuple-element.35), channel_id=1, source_target_pairs={{0,3},{1,4},{2,5},{3,6},{4,7},{5,0},{6,1},{7,2},{8,13},{9,14},{10,... | collective-permute-start | bytes 393224 | tf_op jit(solution)/shard_map/ppermute | solution.py:46
  96.1 20.8 %collective-permute-start.34 = (bf16[8,64,128]{2,1,0:T(8,128)(2,1)S(1)}, bf16[8,64,128]{2,1,0:T(8,128)(2,1)S(1)}, u32[]{:S(2)}, u32[]{:S(2)}) collective-permute-start(bf16[8,64,128]{2,1,0:T(8,128)(2,1)S(1)} %get-tuple-element.34), channel_id=1, source_target_pairs={{0,5},{1,6},{2,7},{3,0},{4,1},{5,2},{6,3},{7,4},{8,11},{9,12},{10,... | collective-permute-start | bytes 393224 | tf_op jit(solution)/shard_map/ppermute | solution.py:46
  96.2 20.7 %collective-permute-start.35 = (bf16[8,64,128]{2,1,0:T(8,128)(2,1)S(1)}, bf16[8,64,128]{2,1,0:T(8,128)(2,1)S(1)}, u32[]{:S(2)}, u32[]{:S(2)}) collective-permute-start(bf16[8,64,128]{2,1,0:T(8,128)(2,1)S(1)} %get-tuple-element.33), channel_id=1, source_target_pairs={{0,3},{1,4},{2,5},{3,6},{4,7},{5,0},{6,1},{7,2},{8,13},{9,14},{10,... | collective-permute-start | bytes 393224 | tf_op jit(solution)/shard_map/ppermute | solution.py:46
  101.7 11.5 %collective-permute-start.25 = (f32[3,64,128]{2,1,0:T(8,128)S(1)}, f32[3,64,128]{2,1,0:T(8,128)S(1)}, u32[]{:S(2)}, u32[]{:S(2)}) collective-permute-start(f32[3,64,128]{2,1,0:T(8,128)S(1)} %get-tuple-element.23), channel_id=1, source_target_pairs={{0,64},{1,65},{2,66},{3,67},{4,68},{5,69},{6,70},{7,71},{8,72},{9,... | collective-permute-start | bytes 294920 | tf_op jit(solution)/shard_map/ppermute | solution.py:46
  109.8 5.0 %collective-permute-start.26 = (f32[3,64,128]{2,1,0:T(8,128)S(1)}, f32[3,64,128]{2,1,0:T(8,128)S(1)}, u32[]{:S(2)}, u32[]{:S(2)}) collective-permute-start(f32[3,64,128]{2,1,0:T(8,128)S(1)} %get-tuple-element.23), channel_id=1, source_target_pairs={{0,128},{1,129},{2,130},{3,131},{4,132},{5,133},{6,134},{7,135},{8... | collective-permute-start | bytes 294920 | tf_op jit(solution)/shard_map/ppermute | solution.py:46
  110.7 6.1 %collective-permute-start.27 = (f32[3,64,128]{2,1,0:T(8,128)S(1)}, f32[3,64,128]{2,1,0:T(8,128)S(1)}, u32[]{:S(2)}, u32[]{:S(2)}) collective-permute-start(f32[3,64,128]{2,1,0:T(8,128)S(1)} %get-tuple-element.23), channel_id=1, source_target_pairs={{0,192},{1,193},{2,194},{3,195},{4,196},{5,197},{6,198},{7,199},{8... | collective-permute-start | bytes 294920 | tf_op jit(solution)/shard_map/ppermute | solution.py:46
